TPU v7x, 32 devices: a whole 2x2x4 slice. The times are simulated.
32 devices in a mesh: groups: 2 (over y), row: 4 (over z), col: 4 (over x, core).
Axes of the slice: x: 2, y: 2, z: 4, core: 2. Of those that a mesh axis runs over, the one named last changes fastest.
Arguments:
- prev_solution: float32 [16384, 1024], P(None, ('groups', 'row', 'col')), parts along dimension 1, may hold values from -6 to 6
- factor_panel: float32 [1024, 16384], P(None, ('row', 'col')), may hold values from -0.0625 to 0.0625
- right_side: float32 [1024, 1024], P('row', ('groups', 'col')), parts along dimension 1, may hold values from -6 to 6
- window_factor: float32 [1024, 1024], P('row'), may hold values from -2 to 2, as said below
Outputs:
- window_solution: float32 [1024, 1024], P('row', ('groups', 'col')), parts along dimension 1
There are 2 independent parts, one for each index of `groups`. A program takes and returns all parts, laid end to end along the dimension named above; an argument that names none is the same for every part. Nothing has to cross between parts.
Inputs may be any that keep to these rules, and one draw needn't show every extreme that they name: `window_factor`: lower triangular, with diagonal entries between 1 and 2.
All inputs are finite; a program needn't handle non-finite values.
Results may differ from a plain program's by a relative error of at most 0.0003.
Values sent between devices are 32-bit elements; how exact they have to be, the bound alone decides.
No kernel may reach another device: no remote copies, remote signals or barrier semaphores. Data moves between devices by JAX's collectives and lax.ppermute only.
A program may use at most 64 MiB of HBM per device.

v0:
```python
import jax
import jax.numpy as jnp
from jax import lax
from jax.sharding import PartitionSpec as P


def broadcast(value, axis, root):
    mine = lax.axis_index(axis) == root
    return lax.psum(jnp.where(mine, value, jnp.zeros_like(value)), axis)


def shards(prev_solution, factor_panel, right_side, window_factor):
    highest = lax.Precision.HIGHEST
    row_count = lax.axis_size("row")
    row_index = lax.axis_index("row")
    strip_rows = right_side.shape[0]
    by_rows = lax.all_to_all(prev_solution, ("row", "col"), split_axis=0, concat_axis=1, tiled=True)
    row_summed = lax.psum_scatter(
        jnp.dot(factor_panel, by_rows, precision=highest, preferred_element_type=jnp.float32),
        "row",
        scatter_dimension=0,
        tiled=True,
    )
    coupling = lax.psum_scatter(row_summed, "col", scatter_dimension=1, tiled=True)
    residual = right_side - coupling
    own_block = lax.dynamic_slice_in_dim(window_factor, row_index * strip_rows, strip_rows, 1)

    def sweep_step(strip_index, state_pair):
        pending, solved = state_pair
        candidate = jax.scipy.linalg.solve_triangular(own_block, pending, lower=True)
        arrived = broadcast(candidate, "row", strip_index)
        column_block = lax.dynamic_slice_in_dim(
            window_factor, strip_index * strip_rows, strip_rows, 1
        )
        update = jnp.dot(
            column_block, arrived, precision=highest, preferred_element_type=jnp.float32
        )
        pending = jnp.where(row_index > strip_index, pending - update, pending)
        solved = jnp.where(row_index == strip_index, arrived, solved)
        return (pending, solved)

    pending, solved = lax.fori_loop(0, row_count, sweep_step, (residual, jnp.zeros_like(residual)))
    return solved


def solution(mesh):
    in_specs = (
        P(None, ("groups", "row", "col")),
        P(None, ("row", "col")),
        P("row", ("groups", "col")),
        P("row", None),
    )
    out_specs = P("row", ("groups", "col"))
    return jax.shard_map(shards, mesh=mesh, in_specs=in_specs, out_specs=out_specs, check_vma=False)
```

profile of v0, /device:TPU:0, one launch (start us, length us, event | category | flops | bytes accessed | tf_op | source)
XLA Modules:
  0.0 303.0 jit_solution(4795972882912780716)
XLA Ops:
  6.5 1.7 copy.13
  8.3 54.7 %all_to_all.19 = f32[16,1024,32]{1,2,0:T(8,128)S(1)} all-to-all(f32[16,1024,32]{1,2,0:T(8,128)S(1)} %bitcast.42), channel_id=1, replica_groups=mesh['groups'=2,'row'=4,'col'=4] {'row','col'}, dimensions={0} | all-to-all | bytes 4194304 | tf_op jit(solution)/shard_map/all_to_all | solution.py:17
  63.0 8.1 %fusion.17 = f32[1024,512]{1,0:T(8,128)} fusion(f32[1024,1024]{1,0:T(8,128)S(1)} %copy-done, f32[1024,512]{0,1:T(8,128)S(1)} %bitcast.43), kind=kOutput, calls=%fused_computation.30 | convolution fusion | flops 6442450944 | bytes 8388608 | tf_op jit(solution)/shard_map/dot_general | solution.py:19
  71.2 44.4 %reduce-scatter.3.cloned.1.call-done = f32[256,512]{1,0:T(8,128)} async-done(((f32[1024,512]{1,0:T(8,128)}), f32[256,512]{1,0:T(8,128)}) %reduce-scatter.3.cloned.1.call-update) | async-done | bytes 524304 | tf_op jit(solution)/shard_map/reduce_scatter | solution.py:18
  115.8 4.3 %while.20 = (s32[]{:T(128)}, f32[256,256]{1,0:T(8,128)S(1)}, s32[2,2]{1,0:T(2,128)S(1)}, f32[2,128,128]{2,1,0:T(8,128)S(1)}, s32[]{:T(128)}) while((s32[]{:T(128)}, f32[256,256]{1,0:T(8,128)S(1)}, s32[2,2]{1,0:T(2,128)S(1)}, f32[2,128,128]{2,1,0:T(8,128)S(1)}, s32[]{:T(128)}) %tuple.62), condition=%wide.while_cond, body=%wide.while_body.sunk | while | flops 2 | bytes 131189 | solution.py:30
  115.8 0.7 fusion.33
  116.5 1.5 bitcast_dynamic-update-slice_fusion.2
  118.6 1.5 bitcast_dynamic-update-slice_fusion.2
  120.1 19.7 %custom-call.11 = f32[2,128,128]{1,2,0:T(8,128)S(1)} custom-call(f32[2,128,128]{2,1,0:T(8,128)S(1)} %get-tuple-element.195), custom_call_target="InvertDiagBlocksLowerTriangular" | custom-call | tf_op jit(solution)/shard_map/while/body/eval_jaxpr/jit(_solve_triangular)/triangular_solve | solution.py:30
  139.9 0.9 sub.13
  140.8 154.7 %while.21 = (s32[]{:T(128)}, f32[256,128]{1,0:T(8,128)S(1)}, f32[256,128]{1,0:T(8,128)S(1)}, s32[]{:T(128)}, f32[256,1024]{1,0:T(8,128)S(1)}, /*index=5*/f32[2,1...) while((s32[]{:T(128)}, f32[256,128]{1,0:T(8,128)S(1)}, ...), condition=%wide.region_4.5_spmd.clone, body=%wide.region_2.4_spmd.clone.sunk | while | flops 176472064 | bytes 2752807 | solution.py:42
  141.6 0.7 maximum_select_fusion.2
  142.3 35.6 %all-reduce.2.cloned.1.call-done = f32[256,128]{1,0:T(8,128)} async-done(((f32[256,128]{1,0:T(8,128)}), f32[256,128]{1,0:T(8,128)}) %all-reduce.2.cloned.1.call-update) | async-done | bytes 131088 | tf_op jit(solution)/shard_map/while/body/eval_jaxpr/psum | solution.py:9
  177.9 1.3 fusion.42
  179.2 0.9 select_select_fusion.2
  180.9 0.7 maximum_select_fusion.2
  181.6 34.7 %all-reduce.2.cloned.1.call-done = f32[256,128]{1,0:T(8,128)} async-done(((f32[256,128]{1,0:T(8,128)}), f32[256,128]{1,0:T(8,128)}) %all-reduce.2.cloned.1.call-update) | async-done | bytes 131088 | tf_op jit(solution)/shard_map/while/body/eval_jaxpr/psum | solution.py:9
  216.3 1.3 fusion.42
  218.4 0.7 maximum_select_fusion.2
  219.1 35.8 %all-reduce.2.cloned.1.call-done = f32[256,128]{1,0:T(8,128)} async-done(((f32[256,128]{1,0:T(8,128)}), f32[256,128]{1,0:T(8,128)}) %all-reduce.2.cloned.1.call-update) | async-done | bytes 131088 | tf_op jit(solution)/shard_map/while/body/eval_jaxpr/psum | solution.py:9
  254.9 1.3 fusion.42
  257.0 0.7 maximum_select_fusion.2
  257.7 36.4 %all-reduce.2.cloned.1.call-done = f32[256,128]{1,0:T(8,128)} async-done(((f32[256,128]{1,0:T(8,128)}), f32[256,128]{1,0:T(8,128)}) %all-reduce.2.cloned.1.call-update) | async-done | bytes 131088 | tf_op jit(solution)/shard_map/while/body/eval_jaxpr/psum | solution.py:9
  294.1 1.3 fusion.42
  (45 shorter events, 4.5 us)
Async XLA Ops:
  6.5 109.1 %reduce-scatter.3.cloned.1.call-start = ((), (), s32[]{:S(2)}) async-start(), calls=%async_computation.3 | async-start | bytes 2621440 | tf_op jit(solution)/shard_map/reduce_scatter | solution.py:18
  8.3 54.8 %copy-start = (f32[1024,1024]{1,0:T(8,128)S(1)}, f32[1024,1024]{1,0:T(8,128)}, u32[]{:S(2)}) copy-start(f32[1024,1024]{1,0:T(8,128)} %param.7) | copy-start | bytes 12582916
  71.1 44.6 %copy-start.2 = (f32[256,1024]{1,0:T(8,128)S(1)}, f32[256,1024]{1,0:T(8,128)}, u32[]{:S(2)}) copy-start(f32[256,1024]{1,0:T(8,128)} %param.9) | copy-start | bytes 3145732
  71.1 68.8 %copy-start.3 = (f32[256,128]{1,0:T(8,128)S(1)}, f32[256,128]{1,0:T(8,128)}, u32[]{:S(2)}) copy-start(f32[256,128]{1,0:T(8,128)} %param.8) | copy-start | bytes 393220
  71.1 68.8 %reduce-scatter.5.cloned.1.call-start = ((), (), s32[]{:S(2)}) async-start(), calls=%async_computation.4 | async-start | bytes 655360 | tf_op jit(solution)/shard_map/reduce_scatter | solution.py:24
  140.9 37.0 %all-reduce.2.cloned.1.call-start = ((), (), s32[]{:S(2)}) async-start(), calls=%async_computation.5 | async-start | bytes 262144 | tf_op jit(solution)/shard_map/while/body/eval_jaxpr/psum | solution.py:9
  180.2 36.1 %all-reduce.2.cloned.1.call-start = ((), (), s32[]{:S(2)}) async-start(), calls=%async_computation.5 | async-start | bytes 262144 | tf_op jit(solution)/shard_map/while/body/eval_jaxpr/psum | solution.py:9
  217.7 37.2 %all-reduce.2.cloned.1.call-start = ((), (), s32[]{:S(2)}) async-start(), calls=%async_computation.5 | async-start | bytes 262144 | tf_op jit(solution)/shard_map/while/body/eval_jaxpr/psum | solution.py:9
  256.3 37.9 %all-reduce.2.cloned.1.call-start = ((), (), s32[]{:S(2)}) async-start(), calls=%async_computation.5 | async-start | bytes 262144 | tf_op jit(solution)/shard_map/while/body/eval_jaxpr/psum | solution.py:9
  295.5 0.7 copy-start.1
Sparse Core Ops, SparseCore 0:
  71.2 44.3 reduce-scatter.2
  118.2 21.0 reduce-scatter.4
  144.0 33.8 all-reduce.1
  183.0 33.1 all-reduce.1
  220.5 34.3 all-reduce.1
  259.1 34.9 all-reduce.1
where the time goes:
time: 303 us
  waiting for transfers between devices  187 us (62%)
  blocking collectives  54.7 us (18%)
  other arithmetic  24.4 us (8%)
  matrix products  15.8 us (5%)
  between operations  13.5 us (4%)
  local copies, waits for them, and re-layouts  6.83 us (2%)
    psum x4, waiting for transfers between devices, broadcast(): return lax.psum(jnp.where(mine, value, jnp.zeros_like(value)), axis)  143 us
    all_to_all x1, blocking collectives, shards(): lax.all_to_all(prev_solution, ('row', 'col'), split_axis=0, concat_axis=1...  54.7 us
    reduce_scatter x1, waiting for transfers between devices, shards(): lax.psum_scatter(jnp.dot(factor_panel, by_rows, precision=highest, prefer...  44.4 us
    another operation x3, other arithmetic, sweep_step(): jax.scipy.linalg.solve_triangular(own_block, pending, lower=True)  19.7 us
    dot_general x1, matrix products, shards(): jnp.dot(factor_panel, by_rows, precision=highest, preferred_element_type=...  8.05 us
  transfers between devices with their start and end apart: 6, of which 5 were waited for; matrix products, arithmetic and copies ran while one was open for 8% of the time, Pallas kernels for 0%

commit v1 on v0

v1 whole, which is shorter than its diff:
```python
import functools

import jax
import jax.numpy as jnp
from jax import lax
from jax.experimental import pallas as pl
from jax.experimental.pallas import tpu as pltpu
from jax.sharding import PartitionSpec as P

HIGHEST = lax.Precision.HIGHEST


def dot_exact(a, b):
    return jnp.dot(a, b, precision=HIGHEST, preferred_element_type=jnp.float32)


def invert_kernel(block_ref, inverse_ref):
    count, size, _ = block_ref.shape
    rows = lax.broadcasted_iota(jnp.int32, (size, size), 0)
    cols = lax.broadcasted_iota(jnp.int32, (size, size), 1)
    blocks = [block_ref[t] for t in range(count)]
    inverses = []
    for block in blocks:
        diagonal = jnp.sum(jnp.where(rows == cols, block, 0.0), axis=1, keepdims=True)
        inverses.append(jnp.where(rows == cols, 1.0 / diagonal, 0.0))
    step = 1
    while step < size:
        below = ((rows // step) % 2 == 1) & (cols // step == rows // step - 1)
        for t in range(count):
            coupled = dot_exact(jnp.where(below, blocks[t], 0.0), inverses[t])
            inverses[t] = inverses[t] - dot_exact(inverses[t], coupled)
        step *= 2
    for t in range(count):
        inverse_ref[t] = inverses[t]


def invert_blocks(blocks):
    return pl.pallas_call(
        invert_kernel,
        out_shape=jax.ShapeDtypeStruct(blocks.shape, jnp.float32),
        in_specs=[pl.BlockSpec(memory_space=pltpu.VMEM)],
        out_specs=pl.BlockSpec(memory_space=pltpu.VMEM),
        cost_estimate=pl.CostEstimate(flops=6 * 10**8, bytes_accessed=10**6, transcendentals=0),
    )(blocks)


def solve_kernel(size, factor_ref, right_ref, kept_ref, arrived_ref, solved_ref):
    rows = right_ref.shape[0]
    for start in range(0, rows, size):
        here = pl.ds(start, size)
        residual = right_ref[here, :] - (kept_ref[here, :] + arrived_ref[here, :])
        if start:
            residual = residual - dot_exact(factor_ref[here, pl.ds(0, start)], solved_ref[pl.ds(0, start), :])
        solved_ref[here, :] = dot_exact(factor_ref[here, here], residual)


def solve_window(size, factor, right, kept, arrived):
    return pl.pallas_call(
        functools.partial(solve_kernel, size),
        out_shape=jax.ShapeDtypeStruct(right.shape, jnp.float32),
        in_specs=[pl.BlockSpec(memory_space=pltpu.VMEM)] * 4,
        out_specs=pl.BlockSpec(memory_space=pltpu.VMEM),
        cost_estimate=pl.CostEstimate(flops=2 * 10**9, bytes_accessed=6 * 10**6, transcendentals=0),
    )(factor, right, kept, arrived)


def swap(value, axis, step):
    return lax.ppermute(value, axis, [(i, i ^ step) for i in range(lax.axis_size(axis))])


def place(mine, theirs, bit, dim):
    first = jnp.where(bit == 0, mine, theirs)
    second = jnp.where(bit == 0, theirs, mine)
    return jnp.stack([first, second], axis=dim)


def gather_window(strip, row_index, group_index, col_index):
    row_count, col_count, group_count = (lax.axis_size(a) for a in ("row", "col", "groups"))
    strip_rows, window = strip.shape
    if row_count != 4 or col_count != 4 or group_count != 2:
        return lax.all_gather(strip, "row", axis=0, tiled=True)
    share_rows = strip_rows // (group_count * col_count)
    share = lax.dynamic_slice_in_dim(strip, (group_index * col_count + col_index) * share_rows, share_rows, 0)
    shares = jnp.zeros((row_count, share_rows, window), jnp.float32)
    shares = lax.dynamic_update_slice_in_dim(shares, share[None], row_index, 0)
    for step in (3, 2, 1):
        shares = lax.dynamic_update_slice_in_dim(shares, swap(share, "row", step)[None], row_index ^ step, 0)
    shares = place(shares, swap(shares, "col", 2), col_index >> 1, 1)
    shares = place(shares, swap(shares, "groups", 1), group_index, 1)
    shares = place(shares, swap(shares, "col", 1), col_index & 1, 3)
    return shares.reshape(row_count * strip_rows, window)


def shards(prev_solution, factor_panel, right_side, window_factor):
    row_count, col_count = lax.axis_size("row"), lax.axis_size("col")
    row_index, col_index, group_index = (lax.axis_index(a) for a in ("row", "col", "groups"))
    strip_rows, strip_cols = right_side.shape
    window = window_factor.shape[1]
    size = min(128, strip_rows)

    by_rows = lax.all_to_all(prev_solution, ("row", "col"), split_axis=0, concat_axis=1, tiled=True)

    own = lax.dynamic_slice_in_dim(window_factor, row_index * strip_rows, strip_rows, 1)
    blocks = jnp.stack([own[t : t + size, t : t + size] for t in range(0, strip_rows, size)])
    inverses = invert_blocks(blocks)
    strip = window_factor
    for t in range(strip_rows // size):
        strip = lax.dynamic_update_slice(strip, inverses[t], (t * size, row_index * strip_rows + t * size))
    factor = gather_window(strip, row_index, group_index, col_index)
    right = lax.dynamic_update_slice_in_dim(
        jnp.zeros((window, strip_cols), jnp.float32), right_side, row_index * strip_rows, 0
    )

    partial = jnp.dot(factor_panel, by_rows, precision=lax.Precision.HIGH, preferred_element_type=jnp.float32)

    def block(index):
        return lax.dynamic_slice_in_dim(partial, index * strip_cols, strip_cols, 1)

    if col_count == 4:
        sent = jnp.concatenate([block(col_index ^ 3), block(col_index ^ 1)], axis=0)
        landed = swap(sent, "col", 1)
        far = block(col_index ^ 2) + landed[:window]
        kept = block(col_index) + landed[window:]
        arrived = swap(far, "col", 2)
    else:
        kept = lax.psum_scatter(partial, "col", scatter_dimension=1, tiled=True)
        arrived = jnp.zeros_like(kept)

    solved = solve_window(size, factor, right, kept, arrived)

    if row_count == 4:
        total = lax.dynamic_slice_in_dim(solved, row_index * strip_rows, strip_rows, 0)
        for step in (3, 2, 1):
            part = lax.dynamic_slice_in_dim(solved, (row_index ^ step) * strip_rows, strip_rows, 0)
            total = total + swap(part, "row", step)
        return total
    return lax.psum_scatter(solved, "row", scatter_dimension=0, tiled=True)


def solution(mesh):
    in_specs = (
        P(None, ("groups", "row", "col")),
        P(None, ("row", "col")),
        P("row", ("groups", "col")),
        P("row", None),
    )
    out_specs = P("row", ("groups", "col"))
    return jax.shard_map(shards, mesh=mesh, in_specs=in_specs, out_specs=out_specs, check_vma=False)
```

time: 303 us -> 164 us (0.54)
  waiting for transfers between devices: 187 us -> 103 us
  blocking collectives: 54.7 us -> 0 us
  starting transfers between devices: 0.21 us -> 20.6 us
  between operations: 13.5 us -> 0.16 us
  Pallas kernels: 0 us -> 11.8 us
  other arithmetic: 24.4 us -> 13.3 us
  matrix products: 15.8 us -> 5.93 us
    psum x4 -> x0, waiting for transfers between devices: 143 us -> none  [broadcast(): return lax.psum(jnp.where(mine, value, jnp.zeros_like(value)), axis)]
    ppermute x0 -> x11, waiting for transfers between devices: none -> 103 us  [swap(): lax.ppermute(value, axis, [(i, i ^ step) for i in range(lax.axis_size(axi...]
    all_to_all x1 -> x0, blocking collectives: 54.7 us -> none  [shards(): lax.all_to_all(prev_solution, ('row', 'col'), split_axis=0, concat_axis=1...]
    reduce_scatter x2 -> x0, waiting for transfers between devices: 44.5 us -> none  [the longest x1 44.4 us: shards(): lax.psum_scatter(jnp.dot(factor_panel, by_rows, precision=highest, prefer...]
    ppermute x0 -> x11, starting transfers between devices: none -> 13.2 us  [swap(): lax.ppermute(value, axis, [(i, i ^ step) for i in range(lax.axis_size(axi...]
    pallas_call x0 -> x2, Pallas kernels: none -> 11.8 us  [the longest x1 7.04 us: solve_window(): pl.pallas_call(functools.partial(solve_kernel, size), out_shape=jax.Shape...]
    another operation x3 -> x7, other arithmetic: 19.7 us -> 8.35 us  [the longest x6 7.68 us: place(): return jnp.stack([first, second], axis=dim)]
    all_to_all x0 -> x1, starting transfers between devices: none -> 7.41 us  [shards(): lax.all_to_all(prev_solution, ('row', 'col'), split_axis=0, concat_axis=1...]
  transfers between devices with their start and end apart: 6 -> 12, of which waited for: 5 -> 9; matrix products, arithmetic and copies ran while one was open for 8% -> 13% of each run, Pallas kernels for 0% -> 3%
where the time goes in v1:
time: 164 us
  waiting for transfers between devices  103 us (63%)
  starting transfers between devices  20.6 us (13%)
  other arithmetic  13.3 us (8%)
  Pallas kernels  11.8 us (7%)
  local copies, waits for them, and re-layouts  9 us (5%)
  matrix products  5.93 us (4%)
    ppermute x11, waiting for transfers between devices, swap(): lax.ppermute(value, axis, [(i, i ^ step) for i in range(lax.axis_size(axi...  103 us
    ppermute x11, starting transfers between devices, swap(): lax.ppermute(value, axis, [(i, i ^ step) for i in range(lax.axis_size(axi...  13.2 us
    another operation x6, other arithmetic, place(): return jnp.stack([first, second], axis=dim)  7.68 us
    all_to_all x1, starting transfers between devices, shards(): lax.all_to_all(prev_solution, ('row', 'col'), split_axis=0, concat_axis=1...  7.41 us
    pallas_call x1, Pallas kernels, solve_window(): pl.pallas_call(functools.partial(solve_kernel, size), out_shape=jax.Shape...  7.04 us
    dot_general x1, matrix products, shards(): jnp.dot(factor_panel, by_rows, precision=lax.Precision.HIGH, preferred_el...  5.93 us
    pallas_call x1, Pallas kernels, invert_blocks(): pl.pallas_call(invert_kernel, out_shape=jax.ShapeDtypeStruct(blocks.shape...  4.8 us
  transfers between devices with their start and end apart: 12, of which 9 were waited for; matrix products, arithmetic and copies ran while one was open for 13% of the time, Pallas kernels for 3%

profile of v1, /device:TPU:0, one launch (start us, length us, event | category | flops | bytes accessed | tf_op | source)
XLA Modules:
  0.0 163.9 jit_solution(14761287797140929534)
XLA Ops:
  1.9 1.5 copy.21
  3.4 7.4 %all-to-all-start = ((f32[16,1024,32]{1,2,0:T(8,128)}), f32[16,1024,32]{1,2,0:T(8,128)}, u32[]{:S(2)}, u32[]{:S(2)}) async-start(f32[16,1024,32]{1,2,0:T(8,128)} %bitcast.47), calls=%async_computation | async-start | bytes 4194304 | tf_op jit(solution)/shard_map/all_to_all | solution.py:101
  11.5 4.8 %shard_map.46 = f32[2,128,128]{2,1,0:T(8,128)} custom-call(f32[2,128,128]{2,1,0:T(8,128)} %pad_maximum_fusion.4.block_ref), custom_call_target="tpu_custom_call" | custom-call | flops 600000000 | bytes 1000000 | tf_op jit(solution)/shard_map/pallas_call | solution.py:38
  18.1 3.7 %collective-permute-start = (f32[32,1024]{1,0:T(8,128)S(1)}, f32[32,1024]{1,0:T(8,128)S(1)}, u32[]{:S(2)}, u32[]{:S(2)}) collective-permute-start(f32[32,1024]{1,0:T(8,128)S(1)} %get-tuple-element.6), channel_id=1, source_target_pairs={{0,12},{4,8},{8,4},{12,0},{1,13},{5,9},{9,5},{13,1},{2,14},{6,10},... | collective-permute-start | bytes 393224 | tf_op jit(solution)/shard_map/ppermute | solution.py:68
  22.6 30.4 %collective-permute-done = f32[32,1024]{1,0:T(8,128)S(1)} collective-permute-done((f32[32,1024]{1,0:T(8,128)S(1)}, f32[32,1024]{1,0:T(8,128)S(1)}, u32[]{:S(2)}, u32[]{:S(2)}) %collective-permute-start) | collective-permute-done | bytes 131104 | tf_op jit(solution)/shard_map/ppermute | solution.py:68
  53.0 18.1 %collective-permute-done.1 = f32[32,1024]{1,0:T(8,128)S(1)} collective-permute-done((f32[32,1024]{1,0:T(8,128)S(1)}, f32[32,1024]{1,0:T(8,128)S(1)}, u32[]{:S(2)}, u32[]{:S(2)}) %collective-permute-start.1) | collective-permute-done | bytes 131104 | tf_op jit(solution)/shard_map/ppermute | solution.py:68
  71.1 1.6 collective-permute-start.3
  72.7 12.0 %collective-permute-done.3 = f32[4,32,1024]{2,1,0:T(8,128)S(1)} collective-permute-done((f32[4,32,1024]{2,1,0:T(8,128)S(1)}, f32[4,32,1024]{2,1,0:T(8,128)S(1)}, u32[]{:S(2)}, u32[]{:S(2)}) %collective-permute-start.3) | collective-permute-done | bytes 524320 | tf_op jit(solution)/shard_map/ppermute | solution.py:68
  84.9 1.6 collective-permute-start.4
  86.5 22.4 %collective-permute-done.4 = f32[4,2,32,1024]{3,2,1,0:T(8,128)} collective-permute-done((f32[4,2,32,1024]{3,2,1,0:T(8,128)S(1)}, f32[4,2,32,1024]{3,2,1,0:T(8,128)}, u32[]{:S(2)}, u32[]{:S(2)}) %collective-permute-start.4) | collective-permute-done | bytes 1048608 | tf_op jit(solution)/shard_map/ppermute | solution.py:68
  108.9 1.5 select_bitcast_fusion.3
  110.4 1.5 pad_maximum_fusion.1
  111.8 5.9 %fusion.2 = f32[1024,512]{1,0:T(8,128)S(1)} fusion(f32[1024,1024]{1,0:T(8,128)} %param.5, f32[1024,512]{0,1:T(8,128)} %bitcast.19), kind=kOutput, calls=%fused_computation.32 | convolution fusion | flops 3221225472 | bytes 8388608 | tf_op jit(solution)/shard_map/dot_general | solution.py:114
  122.5 2.1 %slice_add_fusion = (f32[1024,128]{1,0:T(8,128)S(1)}, f32[1024,128]{1,0:T(8,128)}) fusion(f32[2048,128]{1,0:T(8,128)S(1)} %collective-permute-done.6, f32[1024,512]{1,0:T(8,128)} %copy-done, s32[]{:T(128)S(6)} %select_n.100, s32[]{:T(128)S(6)} %select_n.97), kind=kLoop, calls=%fused_computation.9 | loop fusion | flops 262144 | bytes 3145736 | tf_op jit(solution)/shard_map/add | solution.py:122
  124.6 1.5 collective-permute-start.7
  126.1 2.3 %select_bitcast_fusion.1 = (f32[4,2,2,1,32,1024]{5,4,3,2,1,0:T(8,128)S(1)}, f32[4,2,2,1,32,1024]{5,4,3,2,1,0:T(8,128)S(1)}) fusion(f32[4,2,2,32,1024]{4,3,2,1,0:T(8,128)} %collective-permute-done.5, pred[]{:T(512)S(6)} %eq.12, f32[4,1,2,32,1024]{4,3,2,1,0:T(8,128)S(1)} %get-tuple-element.14, f32[4,1,2,32,1024]{4,3,2,1,0:T(8,128)S(1)} %get-tuple-element.13), kind=kLoop, calls=%fused_computation.4 | loop fusion | flops 1572864 | bytes 8388609 | tf_op jit(solution)/shard_map/stack | solution.py:74
  128.4 2.3 %pad_maximum_fusion = f32[4,2,2,2,32,1024]{5,4,3,2,1,0:T(8,128)} fusion(f32[4,2,2,1,32,1024]{5,4,3,2,1,0:T(8,128)S(1)} %get-tuple-element.8, f32[4,2,2,1,32,1024]{5,4,3,2,1,0:T(8,128)S(1)} %get-tuple-element.7), kind=kLoop, calls=%fused_computation | loop fusion | flops 1048576 | bytes 8388608 | tf_op jit(solution)/shard_map/stack | solution.py:74
  130.6 8.2 %collective-permute-done.7.arrived_ref = f32[1024,128]{1,0:T(8,128)S(1)} collective-permute-done((f32[1024,128]{1,0:T(8,128)S(1)}, f32[1024,128]{1,0:T(8,128)S(1)}, u32[]{:S(2)}, u32[]{:S(2)}) %collective-permute-start.7) | collective-permute-done | bytes 524320 | tf_op jit(solution)/shard_map/ppermute | solution.py:68
  139.6 7.0 %shard_map.47 = f32[1024,128]{1,0:T(8,128)} custom-call(f32[1024,1024]{1,0:T(8,128)} %bitcast.48, f32[1024,128]{1,0:T(8,128)} %constant_dynamic-update-slice_fusion.right_ref, f32[1024,128]{1,0:T(8,128)} %get-tuple-element.10.kept_ref, f32[1024,128]{1,0:T(8,128)} %copy-done.3), custom_call_target="tpu_custom_call" | custom-call | flops 2000000000 | bytes 6000000 | tf_op jit(solution)/shard_map/pallas_call | solution.py:58
  147.8 1.5 collective-permute-start.8
  149.3 2.0 %collective-permute-start.9 = (f32[256,128]{1,0:T(8,128)S(1)}, f32[256,128]{1,0:T(8,128)S(1)}, u32[]{:S(2)}, u32[]{:S(2)}) collective-permute-start(f32[256,128]{1,0:T(8,128)S(1)} %get-tuple-element.21), channel_id=1, source_target_pairs={{0,8},{4,12},{8,0},{12,4},{1,9},{5,13},{9,1},{13,5},{2,10},{6,14},... | collective-permute-start | bytes 393224 | tf_op jit(solution)/shard_map/ppermute | solution.py:68
  151.2 3.7 %collective-permute-done.10 = f32[256,128]{1,0:T(8,128)S(1)} collective-permute-done((f32[256,128]{1,0:T(8,128)S(1)}, f32[256,128]{1,0:T(8,128)S(1)}, u32[]{:S(2)}, u32[]{:S(2)}) %collective-permute-start.10) | collective-permute-done | bytes 131104 | tf_op jit(solution)/shard_map/ppermute | solution.py:68
  156.1 6.2 %collective-permute-done.9 = f32[256,128]{1,0:T(8,128)S(1)} collective-permute-done((f32[256,128]{1,0:T(8,128)S(1)}, f32[256,128]{1,0:T(8,128)S(1)}, u32[]{:S(2)}, u32[]{:S(2)}) %collective-permute-start.9) | collective-permute-done | bytes 131104 | tf_op jit(solution)/shard_map/ppermute | solution.py:68
  162.3 1.6 add_add_fusion
  (35 shorter events, 13.2 us)
Async XLA Ops:
  0.0 1.9 %copy-start.1 = (f32[16384,32]{0,1:T(8,128)S(1)}, f32[16384,32]{0,1:T(8,128)}, u32[]{:S(2)}) copy-start(f32[16384,32]{0,1:T(8,128)} %param.4) | copy-start | bytes 6291460
  3.4 108.4 %all-to-all-start = ((f32[16,1024,32]{1,2,0:T(8,128)}), f32[16,1024,32]{1,2,0:T(8,128)}, u32[]{:S(2)}, u32[]{:S(2)}) async-start(f32[16,1024,32]{1,2,0:T(8,128)} %bitcast.47), calls=%async_computation | async-start | bytes 4194304 | tf_op jit(solution)/shard_map/all_to_all | solution.py:101
  18.1 34.8 %collective-permute-start = (f32[32,1024]{1,0:T(8,128)S(1)}, f32[32,1024]{1,0:T(8,128)S(1)}, u32[]{:S(2)}, u32[]{:S(2)}) collective-permute-start(f32[32,1024]{1,0:T(8,128)S(1)} %get-tuple-element.6), channel_id=1, source_target_pairs={{0,12},{4,8},{8,4},{12,0},{1,13},{5,9},{9,5},{13,1},{2,14},{6,10},... | collective-permute-start | bytes 393224 | tf_op jit(solution)/shard_map/ppermute | solution.py:68
  21.8 49.2 %collective-permute-start.1 = (f32[32,1024]{1,0:T(8,128)S(1)}, f32[32,1024]{1,0:T(8,128)S(1)}, u32[]{:S(2)}, u32[]{:S(2)}) collective-permute-start(f32[32,1024]{1,0:T(8,128)S(1)} %get-tuple-element.6), channel_id=1, source_target_pairs={{0,8},{4,12},{8,0},{12,4},{1,9},{5,13},{9,1},{13,5},{2,10},{6,14},... | collective-permute-start | bytes 393224 | tf_op jit(solution)/shard_map/ppermute | solution.py:68
  21.8 49.3 %collective-permute-start.2 = (f32[32,1024]{1,0:T(8,128)S(1)}, f32[32,1024]{1,0:T(8,128)S(1)}, u32[]{:S(2)}, u32[]{:S(2)}) collective-permute-start(f32[32,1024]{1,0:T(8,128)S(1)} %get-tuple-element.6), channel_id=1, source_target_pairs={{0,4},{4,0},{8,12},{12,8},{1,5},{5,1},{9,13},{13,9},{2,6},{6,2},{1... | collective-permute-start | bytes 393224 | tf_op jit(solution)/shard_map/ppermute | solution.py:68
  71.1 13.5 %collective-permute-start.3 = (f32[4,32,1024]{2,1,0:T(8,128)S(1)}, f32[4,32,1024]{2,1,0:T(8,128)S(1)}, u32[]{:S(2)}, u32[]{:S(2)}) collective-permute-start(f32[4,32,1024]{2,1,0:T(8,128)S(1)} %bitcast_dynamic-update-slice_fusion), channel_id=1, source_target_pairs={{0,2},{1,3},{2,0},{3,1},{4,6},{5,7},{6,4},{7,5},{8,10},{9,11},{10,... | collective-permute-start | bytes 1572872 | tf_op jit(solution)/shard_map/ppermute | solution.py:68
  84.9 24.0 %collective-permute-start.4 = (f32[4,2,32,1024]{3,2,1,0:T(8,128)S(1)}, f32[4,2,32,1024]{3,2,1,0:T(8,128)}, u32[]{:S(2)}, u32[]{:S(2)}) collective-permute-start(f32[4,2,32,1024]{3,2,1,0:T(8,128)S(1)} %pad_maximum_fusion.2), channel_id=1, source_target_pairs={{0,16},{16,0},{1,17},{17,1},{2,18},{18,2},{3,19},{19,3},{4,20},{20... | collective-permute-start | bytes 3145736 | tf_op jit(solution)/shard_map/ppermute | solution.py:68
  111.8 14.3 %collective-permute-start.5 = (f32[4,2,2,32,1024]{4,3,2,1,0:T(8,128)}, f32[4,2,2,32,1024]{4,3,2,1,0:T(8,128)}, u32[]{:S(2)}, u32[]{:S(2)}) collective-permute-start(f32[4,2,2,32,1024]{4,3,2,1,0:T(8,128)} %pad_maximum_fusion.1), channel_id=1, source_target_pairs={{0,1},{1,0},{2,3},{3,2},{4,5},{5,4},{6,7},{7,6},{8,9},{9,8},{10,11... | collective-permute-start | bytes 6291464 | tf_op jit(solution)/shard_map/ppermute | solution.py:68
  117.8 1.7 %copy-start = (f32[1024,512]{1,0:T(8,128)}, f32[1024,512]{1,0:T(8,128)S(1)}, u32[]{:S(2)}) copy-start(f32[1024,512]{1,0:T(8,128)S(1)} %fusion.2) | copy-start | bytes 6291460
  117.8 3.0 %copy-start.2 = (f32[256,128]{1,0:T(8,128)S(1)}, f32[256,128]{1,0:T(8,128)}, u32[]{:S(2)}) copy-start(f32[256,128]{1,0:T(8,128)} %param.6) | copy-start | bytes 393220
  119.5 3.0 %collective-permute-start.6 = (f32[2048,128]{1,0:T(8,128)}, f32[2048,128]{1,0:T(8,128)S(1)}, u32[]{:S(2)}, u32[]{:S(2)}) collective-permute-start(f32[2048,128]{1,0:T(8,128)} %pad_maximum_fusion.3), channel_id=1, source_target_pairs={{0,1},{1,0},{2,3},{3,2},{4,5},{5,4},{6,7},{7,6},{8,9},{9,8},{10,11... | collective-permute-start | bytes 3145736 | tf_op jit(solution)/shard_map/ppermute | solution.py:68
  124.6 14.2 %collective-permute-start.7 = (f32[1024,128]{1,0:T(8,128)S(1)}, f32[1024,128]{1,0:T(8,128)S(1)}, u32[]{:S(2)}, u32[]{:S(2)}) collective-permute-start(f32[1024,128]{1,0:T(8,128)S(1)} %get-tuple-element.9), channel_id=1, source_target_pairs={{0,2},{1,3},{2,0},{3,1},{4,6},{5,7},{6,4},{7,5},{8,10},{9,11},{10,... | collective-permute-start | bytes 1572872 | tf_op jit(solution)/shard_map/ppermute | solution.py:68
  138.8 0.8 copy-start.3
  147.7 7.2 %collective-permute-start.10 = (f32[256,128]{1,0:T(8,128)S(1)}, f32[256,128]{1,0:T(8,128)S(1)}, u32[]{:S(2)}, u32[]{:S(2)}) collective-permute-start(f32[256,128]{1,0:T(8,128)S(1)} %get-tuple-element.20), channel_id=1, source_target_pairs={{0,4},{4,0},{8,12},{12,8},{1,5},{5,1},{9,13},{13,9},{2,6},{6,2},{1... | collective-permute-start | bytes 393224 | tf_op jit(solution)/shard_map/ppermute | solution.py:68
  147.8 8.4 %collective-permute-start.8 = (f32[256,128]{1,0:T(8,128)S(1)}, f32[256,128]{1,0:T(8,128)S(1)}, u32[]{:S(2)}, u32[]{:S(2)}) collective-permute-start(f32[256,128]{1,0:T(8,128)S(1)} %get-tuple-element.19), channel_id=1, source_target_pairs={{0,12},{4,8},{8,4},{12,0},{1,13},{5,9},{9,5},{13,1},{2,14},{6,10},... | collective-permute-start | bytes 393224 | tf_op jit(solution)/shard_map/ppermute | solution.py:68
  149.3 13.0 %collective-permute-start.9 = (f32[256,128]{1,0:T(8,128)S(1)}, f32[256,128]{1,0:T(8,128)S(1)}, u32[]{:S(2)}, u32[]{:S(2)}) collective-permute-start(f32[256,128]{1,0:T(8,128)S(1)} %get-tuple-element.21), channel_id=1, source_target_pairs={{0,8},{4,12},{8,0},{12,4},{1,9},{5,13},{9,1},{13,5},{2,10},{6,14},... | collective-permute-start | bytes 393224 | tf_op jit(solution)/shard_map/ppermute | solution.py:68

commit v2 on v0

v2 whole, which is shorter than its diff:
```python
import functools
import math

import jax
import jax.numpy as jnp
from jax import lax
from jax.experimental import pallas as pl
from jax.experimental.pallas import tpu as pltpu
from jax.sharding import Mesh
from jax.sharding import PartitionSpec as P

HIGHEST = lax.Precision.HIGHEST
SIZE = 128
VMEM = pl.BlockSpec(memory_space=pltpu.VMEM)
SMEM = pl.BlockSpec(memory_space=pltpu.SMEM)
QUERY_CUTS = (32,)


def exact(a, b):
    return jnp.dot(a, b, precision=HIGHEST, preferred_element_type=jnp.float32)


def exact_t(a, b):
    return lax.dot_general(a, b, (((1,), (1,)), ((), ())), precision=HIGHEST, preferred_element_type=jnp.float32)


def call(kernel, outs, scratch=(), flops=10**6, scalars=0, spare=4):
    def run(*args):
        moved = sum(a.size * a.dtype.itemsize for a in args)
        held = sum(math.prod(a.shape) * a.dtype.itemsize for a in (*jax.tree.leaves(outs), *scratch))
        return pl.pallas_call(
            kernel,
            out_shape=outs,
            in_specs=[SMEM] * scalars + [VMEM] * (len(args) - scalars),
            out_specs=jax.tree.map(lambda _: VMEM, outs),
            scratch_shapes=list(scratch),
            cost_estimate=pl.CostEstimate(flops=flops, bytes_accessed=moved, transcendentals=0),
            compiler_params=pltpu.CompilerParams(vmem_limit_bytes=moved + held + spare * 2**20),
        )(*args)

    return run


def shape(*dims, dtype=jnp.float32):
    return jax.ShapeDtypeStruct(dims, dtype)


def prepare_kernel(factor_ref, ready_ref):
    rows = lax.broadcasted_iota(jnp.int32, (SIZE, SIZE), 0)
    cols = lax.broadcasted_iota(jnp.int32, (SIZE, SIZE), 1)
    starts = range(0, factor_ref.shape[0], SIZE)
    blocks = [factor_ref[pl.ds(s, SIZE), pl.ds(s, SIZE)] for s in starts]
    inverses = []
    for block in blocks:
        diagonal = jnp.sum(jnp.where(rows == cols, block, 0.0), axis=1, keepdims=True)
        inverses.append(jnp.where(rows == cols, 1.0 / diagonal, 0.0))
    step = 1
    while step < SIZE:
        below = ((rows // step) % 2 == 1) & (cols // step == rows // step - 1)
        coupled = [exact(jnp.where(below, b, 0.0), i) for b, i in zip(blocks, inverses)]
        inverses = [i - exact(i, c) for i, c in zip(inverses, coupled)]
        step *= 2
    for start, inverse in zip(starts, inverses):
        if start:
            ready_ref[pl.ds(start, SIZE), pl.ds(0, start)] = exact(
                inverse, factor_ref[pl.ds(start, SIZE), pl.ds(0, start)]
            )
        ready_ref[pl.ds(start, SIZE), pl.ds(start, SIZE)] = inverse


def halves(value):
    high = value.astype(jnp.bfloat16)
    return high, (value - high.astype(jnp.float32)).astype(jnp.bfloat16)


def split_kernel(ref, high_ref, low_ref):
    for start in range(0, ref.shape[0], 128):
        here = pl.ds(start, 128)
        high_ref[here, :], low_ref[here, :] = halves(ref[here, :])


def split(value, flops):
    return call(split_kernel, [shape(*value.shape, dtype=jnp.bfloat16)] * 2, flops=flops)(value)


def couple_kernel(side_ref, core_ref, queries_ref, *refs):
    *factor_refs, kept_ref, far_ref, q_high, q_low = refs
    count = kept_ref.shape[0]
    columns = factor_refs[0].shape[1]
    for part in range(2):
        rows = pl.ds(pl.multiple_of(((side_ref[0] + part) % 2) * count, 8), count)
        for half in range(2):
            cols = pl.ds(pl.multiple_of(((core_ref[0] + half) % 2) * columns, 128), columns)
            here = (pl.ds(part * count, count), pl.ds(half * columns, columns))
            q_high[here], q_low[here] = halves(queries_ref[rows, cols])

    def product(a, b):
        return lax.dot_general(a, b, (((1,), (1,)), ((), ())), preferred_element_type=jnp.float32)

    for start in range(0, kept_ref.shape[1], 256):
        here = pl.ds(start, 256)
        total = 0.0
        for half in range(2):
            cols = pl.ds(half * columns, columns)
            high, low = (ref[here, :] for ref in factor_refs[2 * half : 2 * half + 2])
            total = total + product(q_high[:, cols], high)
            total = total + product(q_low[:, cols], high) + product(q_high[:, cols], low)
        kept_ref[:, here] = total[:count]
        far_ref[:, here] = total[count:]


def solve_kernel(row_ref, ready_ref, right_ref, kept_ref, arrived_ref, *out_refs):
    *piece_refs, left = out_refs
    strip = right_ref.shape[1]
    window = kept_ref.shape[1]
    row = row_ref[0]
    left[...] = -(kept_ref[...] + arrived_ref[...])
    own = pl.ds(pl.multiple_of(row * strip, strip), strip)
    left[:, own] = left[:, own] + right_ref[...]
    blocks = []
    for start in range(0, window, SIZE):
        here = pl.ds(start, SIZE)
        blocks.append(exact_t(left[:, here], ready_ref[here, here]))
    for i, start in enumerate(range(0, window, SIZE)):
        left[:, pl.ds(start, SIZE)] = blocks[i]
        for k in range(i + 1, len(blocks)):
            blocks[k] = blocks[k] - exact_t(blocks[i], ready_ref[pl.ds(k * SIZE, SIZE), pl.ds(start, SIZE)])
    for step, piece_ref in enumerate(piece_refs):
        piece_ref[...] = left[:, pl.ds(pl.multiple_of((row ^ step) * strip, strip), strip)]


def sum_kernel(core_ref, *refs):
    *piece_refs, own_ref, other_ref, total = refs
    value = piece_refs[0][...]
    for ref in piece_refs[1:]:
        value = value + ref[...]
    total[...] = value
    count = own_ref.shape[0]
    own_ref[...] = total[pl.ds(pl.multiple_of(core_ref[0] * count, 8), count), :]
    other_ref[...] = total[pl.ds(pl.multiple_of((1 - core_ref[0]) * count, 8), count), :]


def finish_kernel(cuts, core_ref, *refs):
    *part_refs, out_ref, total = refs
    offset = 0
    width = sum(cuts)
    for cut, own_ref, other_ref in zip(cuts, part_refs[::2], part_refs[1::2]):
        for ref, core in ((own_ref, core_ref[0]), (other_ref, 1 - core_ref[0])):
            for side in range(2):
                place = pl.multiple_of(side * 2 * width + core * width + offset, 8)
                total[pl.ds(place, cut), :] = ref[pl.ds(side * cut, cut), :]
        offset += cut
    out_ref[...] = total[...].T


def swap(value, axis, step):
    return lax.ppermute(value, axis, [(i, i ^ step) for i in range(lax.axis_size(axis))])


def place(mine, theirs, bit, dim):
    first = jnp.where(bit == 0, mine, theirs)
    second = jnp.where(bit == 0, theirs, mine)
    return jnp.stack([first, second], axis=dim)


def gather_window(strip, row, group, side, core, first, second):
    strip_rows, window = strip.shape
    share_rows = strip_rows // 8
    share = lax.dynamic_slice_in_dim(strip, (group * 4 + side * 2 + core) * share_rows, share_rows, 0)
    landed = [swap(share, "row", step) for step in (3, 2, 1)]
    landed, first = lax.optimization_barrier((landed, first()))
    shares = jnp.zeros((4, share_rows, window), jnp.float32)
    shares = lax.dynamic_update_slice_in_dim(shares, share[None], row, 0)
    for step, value in zip((3, 2, 1), landed):
        shares = lax.dynamic_update_slice_in_dim(shares, value[None], row ^ step, 0)
    near, far = shares[:, :, : window // 2], shares[:, :, window // 2 :]
    near_other, far_other = swap(near, "side", 1), swap(far, "groups", 1)
    near, far = place(near, near_other, side, 1), place(far, far_other, group, 1)
    near_other, far_other = swap(near, "groups", 1), swap(far, "side", 1)
    (near_other, far_other), second = lax.optimization_barrier(((near_other, far_other), second()))
    near, far = place(near, near_other, group, 1), place(far, far_other, side, 2)
    return jnp.concatenate([near, far], axis=-1), first, second


def shards(prev_solution, factor_panel, right_side, window_factor):
    row, group, side, core = (lax.axis_index(a) for a in ("row", "groups", "side", "core"))
    row_1, side_1, core_1 = (jnp.full((1,), v, jnp.int32) for v in (row, side, core))
    strip_rows, strip_cols = right_side.shape
    window = window_factor.shape[1]

    shares, own, other = gather_window(
        window_factor,
        row,
        group,
        side,
        core,
        lambda: split(factor_panel, 5 * 10**10),
        lambda: split(swap(factor_panel, "core", 1), 10**6),
    )
    width = prev_solution.shape[1]
    right = right_side.T.reshape(2, 2, width, strip_rows)
    right_own = lax.dynamic_index_in_dim(right, core, 1, keepdims=False)
    right_other = swap(lax.dynamic_index_in_dim(right, 1 - core, 1, keepdims=False), "core", 1)
    right = place(right_own, right_other, core, 0)

    offset = 0
    parts = []
    for cut in QUERY_CUTS:
        stream = prev_solution[:, offset : offset + cut]
        queries = lax.all_to_all(stream, ("row", "side"), split_axis=0, concat_axis=1, tiled=True).T
        half = queries.shape[0] // 2
        if not offset:
            queries, shares = lax.optimization_barrier((queries, shares))
            factor = place(shares, swap(shares, "core", 1), core, 3).reshape(window, window)
            ready = call(prepare_kernel, shape(window, window))(factor)
        kept, far = call(
            couple_kernel,
            [shape(half, window)] * 2,
            [pltpu.VMEM(queries.shape, jnp.bfloat16)] * 2,
            scalars=2,
        )(side_1, core_1, queries, *own, *other)
        pieces = call(
            solve_kernel, [shape(half, strip_rows)] * 4, [pltpu.VMEM((half, window), jnp.float32)], scalars=1
        )(row_1, ready, right[:, :, offset : offset + cut].reshape(half, strip_rows), kept, swap(far, "side", 1))
        landed = [swap(pieces[step], "row", step) for step in (3, 2, 1)]
        own, other = call(
            sum_kernel, [shape(half // 2, strip_rows)] * 2, [pltpu.VMEM((half, strip_rows), jnp.float32)], scalars=1
        )(core_1, pieces[0], *landed)
        parts += [own, swap(other, "core", 1)]
        offset += cut
    return call(
        functools.partial(finish_kernel, QUERY_CUTS),
        shape(strip_rows, strip_cols),
        [pltpu.VMEM((strip_cols, strip_rows), jnp.float32)],
        scalars=1,
    )(core_1, *parts)


def shards_any(prev_solution, factor_panel, right_side, window_factor):
    row = lax.axis_index("row")
    strip_rows, strip_cols = right_side.shape
    by_rows = lax.all_to_all(prev_solution, ("row", "col"), split_axis=0, concat_axis=1, tiled=True)
    factor = lax.all_gather(window_factor, "row", axis=0, tiled=True)
    right = jnp.zeros((factor.shape[0], strip_cols), jnp.float32)
    right = lax.dynamic_update_slice_in_dim(right, right_side, row * strip_rows, 0)
    partial = exact(factor_panel, by_rows)
    coupling = lax.psum_scatter(partial, "col", scatter_dimension=1, tiled=True)
    solved = jax.scipy.linalg.solve_triangular(factor, right - coupling, lower=True)
    return lax.psum_scatter(solved, "row", scatter_dimension=0, tiled=True)


def solution(mesh):
    staged = mesh.shape["groups"] == 2 and mesh.shape["row"] == 4 and mesh.shape["col"] == 4
    if staged:
        mesh = Mesh(mesh.devices.reshape(2, 4, 2, 2), ("groups", "row", "side", "core"))
    col = ("side", "core") if staged else ("col",)
    in_specs = (P(None, ("groups", "row", *col)), P(None, ("row", *col)), P("row", ("groups", *col)), P("row", None))
    out_specs = P("row", ("groups", *col))
    body = shards if staged else shards_any
    return jax.shard_map(body, mesh=mesh, in_specs=in_specs, out_specs=out_specs, check_vma=False)
```

time: 303 us -> 116 us (0.38)
  waiting for transfers between devices: 187 us -> 46 us
  blocking collectives: 54.7 us -> 0 us
  starting transfers between devices: 0.21 us -> 26.1 us
  Pallas kernels: 0 us -> 21.6 us
  other arithmetic: 24.4 us -> 5.74 us
  matrix products: 15.8 us -> 0 us
  between operations: 13.5 us -> 0.25 us
  local copies, waits for them, and re-layouts: 6.83 us -> 15.6 us
    psum x4 -> x0, waiting for transfers between devices: 143 us -> none  [broadcast(): return lax.psum(jnp.where(mine, value, jnp.zeros_like(value)), axis)]
    all_to_all x1 -> x0, blocking collectives: 54.7 us -> none  [shards(): lax.all_to_all(prev_solution, ('row', 'col'), split_axis=0, concat_axis=1...]
    reduce_scatter x2 -> x0, waiting for transfers between devices: 44.5 us -> none  [the longest x1 44.4 us: shards(): lax.psum_scatter(jnp.dot(factor_panel, by_rows, precision=highest, prefer...]
    ppermute x0 -> x15, waiting for transfers between devices: none -> 43.8 us  [swap(): lax.ppermute(value, axis, [(i, i ^ step) for i in range(lax.axis_size(axi...]
    pallas_call x0 -> x7, Pallas kernels: none -> 21.6 us  [run(): pl.pallas_call(kernel, out_shape=outs, in_specs=[SMEM] * scalars + [VMEM]...]
    ppermute x0 -> x15, starting transfers between devices: none -> 20.1 us  [swap(): lax.ppermute(value, axis, [(i, i ^ step) for i in range(lax.axis_size(axi...]
    another operation x3 -> x9, other arithmetic: 19.7 us -> 4.17 us  [place(): return jnp.stack([first, second], axis=dim)]
    dot_general x5 -> x0, matrix products: 13.3 us -> none  [the longest x1 8.05 us: shards(): jnp.dot(factor_panel, by_rows, precision=highest, preferred_element_type=...]
  transfers between devices with their start and end apart: 6 -> 16, of which waited for: 5 -> 8; matrix products, arithmetic and copies ran while one was open for 8% -> 8% of each run, Pallas kernels for 0% -> 14%
where the time goes in v2:
time: 116 us; the launch traced here: 115 us
  waiting for transfers between devices  46 us (40%)
  starting transfers between devices  26.1 us (22%)
  Pallas kernels  21.6 us (19%)
  local copies, waits for them, and re-layouts  15.6 us (13%)
  other arithmetic  5.74 us (5%)
    ppermute x15, waiting for transfers between devices, swap(): lax.ppermute(value, axis, [(i, i ^ step) for i in range(lax.axis_size(axi...  43.8 us
    pallas_call x7, Pallas kernels, run(): pl.pallas_call(kernel, out_shape=outs, in_specs=[SMEM] * scalars + [VMEM]...  21.6 us
    ppermute x15, starting transfers between devices, swap(): lax.ppermute(value, axis, [(i, i ^ step) for i in range(lax.axis_size(axi...  20.1 us
    unnamed x23, local copies, waits for them, and re-layouts  11.3 us
    all_to_all x1, starting transfers between devices, shards(): lax.all_to_all(stream, ('row', 'side'), split_axis=0, concat_axis=1, tile...  5.95 us
    another operation x9, other arithmetic, place(): return jnp.stack([first, second], axis=dim)  4.17 us
    all_to_all x1, local copies, waits for them, and re-layouts, shards(): lax.all_to_all(stream, ('row', 'side'), split_axis=0, concat_axis=1, tile...  3.19 us
  transfers between devices with their start and end apart: 16, of which 8 were waited for; matrix products, arithmetic and copies ran while one was open for 8% of the time, Pallas kernels for 14%

profile of v2, /device:TPU:0, one launch (start us, length us, event | category | flops | bytes accessed | tf_op | source)
XLA Modules:
  0.0 115.3 jit_solution(1787267405378488965)
XLA Ops:
  1.0 5.1 %collective-permute-start = (f32[32,1024]{1,0:T(8,128)S(1)}, f32[32,1024]{1,0:T(8,128)S(1)}, u32[]{:S(2)}, u32[]{:S(2)}) collective-permute-start(f32[32,1024]{1,0:T(8,128)S(1)} %get-tuple-element.52), channel_id=1, source_target_pairs={{0,12},{4,8},{8,4},{12,0},{1,13},{5,9},{9,5},{13,1},{2,14},{6,10},... | collective-permute-start | bytes 393224 | tf_op jit(solution)/shard_map/ppermute | solution.py:157
  6.7 3.2 %copy.22 = f32[4,8,8,2048]{3,2,0,1:T(8,128)} copy(f32[4,8,8,2048]{3,2,1,0:T(8,128)} %bitcast.68) | data formatting | bytes 4194304 | tf_op jit(solution)/shard_map/all_to_all | solution.py:210
  9.9 5.9 %all-to-all-start = ((f32[8,2048,32]{1,2,0:T(8,128)}), f32[8,2048,32]{1,2,0:T(8,128)S(1)}, u32[]{:S(2)}, u32[]{:S(2)}) async-start(f32[8,2048,32]{1,2,0:T(8,128)} %bitcast.67), calls=%async_computation | async-start | bytes 4194304 | tf_op jit(solution)/shard_map/all_to_all | solution.py:210
  15.9 2.2 %copy-done.8 = f32[1024,1024]{1,0:T(8,128)S(1)} copy-done((f32[1024,1024]{1,0:T(8,128)S(1)}, f32[1024,1024]{1,0:T(8,128)}, u32[]{:S(2)}) %copy-start.8) | copy-done | bytes 4194328
  21.7 2.1 %collective-permute-start.3 = (f32[4,32,512]{2,1,0:T(8,128)S(1)}, f32[4,32,512]{2,1,0:T(8,128)S(1)}, u32[]{:S(2)}, u32[]{:S(2)}) collective-permute-start(f32[4,32,512]{2,1,0:T(8,128)S(1)} %get-tuple-element.66), channel_id=1, source_target_pairs={{0,2},{2,0},{1,3},{3,1},{4,6},{6,4},{5,7},{7,5},{8,10},{10,8},{9,1... | collective-permute-start | bytes 786440 | tf_op jit(solution)/shard_map/ppermute | solution.py:157
  25.3 15.0 %collective-permute-done.3 = f32[4,32,512]{2,1,0:T(8,128)S(1)} collective-permute-done((f32[4,32,512]{2,1,0:T(8,128)S(1)}, f32[4,32,512]{2,1,0:T(8,128)S(1)}, u32[]{:S(2)}, u32[]{:S(2)}) %collective-permute-start.3) | collective-permute-done | bytes 262176 | tf_op jit(solution)/shard_map/ppermute | solution.py:157
  41.4 2.5 %collective-permute-start.6 = (f32[4,2,32,512]{3,2,1,0:T(8,128)S(1)}, f32[4,2,32,512]{3,2,1,0:T(8,128)S(1)}, u32[]{:S(2)}, u32[]{:S(2)}) collective-permute-start(f32[4,2,32,512]{3,2,1,0:T(8,128)S(1)} %pad_maximum_fusion.3), channel_id=1, source_target_pairs={{0,2},{2,0},{1,3},{3,1},{4,6},{6,4},{5,7},{7,5},{8,10},{10,8},{9,1... | collective-permute-start | bytes 1572872 | tf_op jit(solution)/shard_map/ppermute | solution.py:157
  44.0 1.6 %collective-permute-start.4 = (f32[4,2,32,512]{3,2,0,1:T(8,128)S(1)}, f32[4,2,32,512]{3,2,0,1:T(8,128)S(1)}, u32[]{:S(2)}, u32[]{:S(2)}) collective-permute-start(f32[4,2,32,512]{3,2,0,1:T(8,128)S(1)} %pad_maximum_fusion.2), channel_id=1, source_target_pairs={{0,16},{16,0},{1,17},{17,1},{2,18},{18,2},{3,19},{19,3},{4,20},{20... | collective-permute-start | bytes 1572872 | tf_op jit(solution)/shard_map/ppermute | solution.py:157
  45.6 2.9 %shard_map.47 = (bf16[1024,1024]{1,0:T(8,128)(2,1)S(1)}, bf16[1024,1024]{1,0:T(8,128)(2,1)S(1)}) custom-call(f32[1024,1024]{1,0:T(8,128)} %collective-permute-done.7.ref), custom_call_target="tpu_custom_call" | custom-call | flops 1000000 | bytes 4194304 | tf_op jit(solution)/shard_map/pallas_call | solution.py:31
  48.5 12.3 %collective-permute-done.6 = f32[4,2,32,512]{3,2,1,0:T(8,128)S(1)} collective-permute-done((f32[4,2,32,512]{3,2,1,0:T(8,128)S(1)}, f32[4,2,32,512]{3,2,1,0:T(8,128)S(1)}, u32[]{:S(2)}, u32[]{:S(2)}) %collective-permute-start.6) | collective-permute-done | bytes 524320 | tf_op jit(solution)/shard_map/ppermute | solution.py:157
  61.1 1.6 %maximum_maximum_fusion = f32[4,2,2,32,1024]{4,3,2,1,0:T(8,128)} fusion(f32[4,2,1,32,512]{4,3,2,1,0:T(8,128)S(1)} %get-tuple-element.58, f32[4,2,1,32,512]{4,3,2,1,0:T(8,128)S(1)} %get-tuple-element.57, f32[4,1,2,32,512]{4,3,0,2,1:T(8,128)S(1)} %get-tuple-element.56, f32[4,1,2,32,512]{4,3,0,2,1:T(8,128)S(1)} %get-tuple-element.55), kind=kLoop, calls=%fused_computation.2 | loop fusion | flops 1310720 | bytes 4194304 | tf_op jit(solution)/shard_map/concatenate | solution.py:182
  62.7 2.2 %all-to-all-done = f32[8,2048,32]{1,2,0:T(8,128)S(1)} async-done(((f32[8,2048,32]{1,2,0:T(8,128)}), f32[8,2048,32]{1,2,0:T(8,128)S(1)}, u32[]{:S(2)}, u32[]{:S(2)}) %all-to-all-start) | async-done | bytes 2097184 | tf_op jit(solution)/shard_map/all_to_all | solution.py:210
  65.5 3.2 %collective-permute-done.9 = f32[2,32,256]{2,1,0:T(8,128)S(1)} collective-permute-done((f32[2,32,256]{2,1,0:T(8,128)S(1)}, f32[2,32,256]{2,1,0:T(8,128)S(1)}, u32[]{:S(2)}, u32[]{:S(2)}) %collective-permute-start.9) | collective-permute-done | bytes 65568 | tf_op jit(solution)/shard_map/ppermute | solution.py:157
  68.8 1.6 %copy-done.1 = bf16[1024,1024]{1,0:T(8,128)(2,1)S(1)} copy-done((bf16[1024,1024]{1,0:T(8,128)(2,1)S(1)}, bf16[1024,1024]{1,0:T(8,128)(2,1)}, u32[]{:S(2)}) %copy-start.1) | copy-done | bytes 2097176
  70.4 1.6 %copy-done.3 = bf16[1024,1024]{1,0:T(8,128)(2,1)S(1)} copy-done((bf16[1024,1024]{1,0:T(8,128)(2,1)S(1)}, bf16[1024,1024]{1,0:T(8,128)(2,1)}, u32[]{:S(2)}) %copy-start.3) | copy-done | bytes 2097176
  72.0 1.6 %copy-done.5 = bf16[1024,1024]{1,0:T(8,128)(2,1)S(1)} copy-done((bf16[1024,1024]{1,0:T(8,128)(2,1)S(1)}, bf16[1024,1024]{1,0:T(8,128)(2,1)}, u32[]{:S(2)}) %copy-start.5) | copy-done | bytes 2097176
  73.5 1.6 %copy-done.7 = bf16[1024,1024]{1,0:T(8,128)(2,1)S(1)} copy-done((bf16[1024,1024]{1,0:T(8,128)(2,1)S(1)}, bf16[1024,1024]{1,0:T(8,128)(2,1)}, u32[]{:S(2)}) %copy-start.7) | copy-done | bytes 2097176
  75.1 3.5 %shard_map.49 = (f32[128,1024]{1,0:T(8,128)S(1)}, f32[128,1024]{1,0:T(8,128)S(1)}) custom-call(s32[1]{0:T(128)} %bitcast.31.side_ref, s32[1]{0:T(128)} %bitcast.core_ref, f32[256,2048]{1,0:T(8,128)S(1)} %bitcast.65, bf16[1024,1024]{1,0:T(8,128)(2,1)S(1)} %copy-done.1, bf16[1024,1024]{1,0:T(8,128)(2,1)S(1)} %copy-done.3, bf16[1024,1024]{1,0:T(8,128)(2,1)S(1)} %copy-done.5, ...), custom_call_target="tpu_custom_call" | custom-call | flops 1000000 | bytes 10485768 | tf_op jit(solution)/shard_map/pallas_call | solution.py:31
  80.2 2.2 %select_bitcast_fusion.1 = (f32[4,2,2,1,32,1024]{5,4,3,2,1,0:T(8,128)S(1)}, f32[4,2,2,1,32,1024]{5,4,3,2,1,0:T(8,128)S(1)}) fusion(f32[4,2,2,32,1024]{4,3,2,1,0:T(8,128)S(1)} %copy-done.9, f32[4,2,2,32,1024]{4,3,2,1,0:T(8,128)} %collective-permute-done.8, pred[]{:T(512)S(6)} %eq.6), kind=kLoop, calls=%fused_computation.4 | loop fusion | flops 1048576 | bytes 8388609 | tf_op jit(solution)/shard_map/stack | solution.py:163
  83.0 8.4 %shard_map.48.ready_ref = f32[1024,1024]{1,0:T(8,128)S(1)} custom-call(f32[1024,1024]{1,0:T(8,128)S(1)} %bitcast.64), custom_call_target="tpu_custom_call" | custom-call | flops 1000000 | bytes 4194304 | tf_op jit(solution)/shard_map/pallas_call | solution.py:31
  92.9 5.2 %shard_map.50 = (f32[128,256]{1,0:T(8,128)S(1)}, f32[128,256]{1,0:T(8,128)S(1)}, f32[128,256]{1,0:T(8,128)S(1)}, f32[128,256]{1,0:T(8,128)S(1)}) custom-call(s32[1]{0:T(128)} %bitcast.1.row_ref, f32[1024,1024]{1,0:T(8,128)S(1)} %shard_map.48.ready_ref, f32[128,256]{1,0:T(8,128)S(1)} %bitcast.66, f32[128,1024]{1,0:T(8,128)S(1)} %get-tuple-element.43.kept_ref, ...), custom_call_target="tpu_custom_call" | custom-call | flops 1000000 | bytes 5373956 | tf_op jit(solution)/shard_map/pallas_call | solution.py:31
  98.1 2.3 %collective-permute-start.11 = (f32[128,256]{1,0:T(8,128)S(1)}, f32[128,256]{1,0:T(8,128)S(1)}, u32[]{:S(2)}, u32[]{:S(2)}) collective-permute-start(f32[128,256]{1,0:T(8,128)S(1)} %get-tuple-element.46), channel_id=1, source_target_pairs={{0,12},{4,8},{8,4},{12,0},{1,13},{5,9},{9,5},{13,1},{2,14},{6,10},... | collective-permute-start | bytes 393224 | tf_op jit(solution)/shard_map/ppermute | solution.py:157
  102.6 3.9 %collective-permute-done.11.refs_1_ = f32[128,256]{1,0:T(8,128)S(1)} collective-permute-done((f32[128,256]{1,0:T(8,128)S(1)}, f32[128,256]{1,0:T(8,128)S(1)}, u32[]{:S(2)}, u32[]{:S(2)}) %collective-permute-start.11) | collective-permute-done | bytes 131104 | tf_op jit(solution)/shard_map/ppermute | solution.py:157
  106.4 6.7 %collective-permute-done.12.refs_2_ = f32[128,256]{1,0:T(8,128)S(1)} collective-permute-done((f32[128,256]{1,0:T(8,128)S(1)}, f32[128,256]{1,0:T(8,128)S(1)}, u32[]{:S(2)}, u32[]{:S(2)}) %collective-permute-start.12) | collective-permute-done | bytes 131104 | tf_op jit(solution)/shard_map/ppermute | solution.py:157
  (56 shorter events, 16.6 us)
Async XLA Ops:
  1.0 20.5 %collective-permute-start = (f32[32,1024]{1,0:T(8,128)S(1)}, f32[32,1024]{1,0:T(8,128)S(1)}, u32[]{:S(2)}, u32[]{:S(2)}) collective-permute-start(f32[32,1024]{1,0:T(8,128)S(1)} %get-tuple-element.52), channel_id=1, source_target_pairs={{0,12},{4,8},{8,4},{12,0},{1,13},{5,9},{9,5},{13,1},{2,14},{6,10},... | collective-permute-start | bytes 393224 | tf_op jit(solution)/shard_map/ppermute | solution.py:157
  6.1 15.4 %collective-permute-start.1 = (f32[32,1024]{1,0:T(8,128)S(1)}, f32[32,1024]{1,0:T(8,128)S(1)}, u32[]{:S(2)}, u32[]{:S(2)}) collective-permute-start(f32[32,1024]{1,0:T(8,128)S(1)} %get-tuple-element.52), channel_id=1, source_target_pairs={{0,8},{4,12},{8,0},{12,4},{1,9},{5,13},{9,1},{13,5},{2,10},{6,14},... | collective-permute-start | bytes 393224 | tf_op jit(solution)/shard_map/ppermute | solution.py:157
  6.1 15.4 %collective-permute-start.2 = (f32[32,1024]{1,0:T(8,128)S(1)}, f32[32,1024]{1,0:T(8,128)S(1)}, u32[]{:S(2)}, u32[]{:S(2)}) collective-permute-start(f32[32,1024]{1,0:T(8,128)S(1)} %get-tuple-element.52), channel_id=1, source_target_pairs={{0,4},{4,0},{8,12},{12,8},{1,5},{5,1},{9,13},{13,9},{2,6},{6,2},{1... | collective-permute-start | bytes 393224 | tf_op jit(solution)/shard_map/ppermute | solution.py:157
  6.7 38.8 %collective-permute-start.7 = (f32[1024,1024]{1,0:T(8,128)}, f32[1024,1024]{1,0:T(8,128)}, u32[]{:S(2)}, u32[]{:S(2)}) collective-permute-start(f32[1024,1024]{1,0:T(8,128)} %ref.1), channel_id=1, source_target_pairs={{0,1},{1,0},{2,3},{3,2},{4,5},{5,4},{6,7},{7,6},{8,9},{9,8},{10,11... | collective-permute-start | bytes 12582920 | tf_op jit(solution)/shard_map/ppermute | solution.py:157
  9.9 54.9 %all-to-all-start = ((f32[8,2048,32]{1,2,0:T(8,128)}), f32[8,2048,32]{1,2,0:T(8,128)S(1)}, u32[]{:S(2)}, u32[]{:S(2)}) async-start(f32[8,2048,32]{1,2,0:T(8,128)} %bitcast.67), calls=%async_computation | async-start | bytes 4194304 | tf_op jit(solution)/shard_map/all_to_all | solution.py:210
  15.9 2.2 %copy-start.8 = (f32[1024,1024]{1,0:T(8,128)S(1)}, f32[1024,1024]{1,0:T(8,128)}, u32[]{:S(2)}) copy-start(f32[1024,1024]{1,0:T(8,128)} %ref.1) | copy-start | bytes 12582916
  21.7 18.6 %collective-permute-start.3 = (f32[4,32,512]{2,1,0:T(8,128)S(1)}, f32[4,32,512]{2,1,0:T(8,128)S(1)}, u32[]{:S(2)}, u32[]{:S(2)}) collective-permute-start(f32[4,32,512]{2,1,0:T(8,128)S(1)} %get-tuple-element.66), channel_id=1, source_target_pairs={{0,2},{2,0},{1,3},{3,1},{4,6},{6,4},{5,7},{7,5},{8,10},{10,8},{9,1... | collective-permute-start | bytes 786440 | tf_op jit(solution)/shard_map/ppermute | solution.py:157
  23.7 16.5 %collective-permute-start.5 = (f32[4,32,512]{2,1,0:T(8,128)S(1)}, f32[4,32,512]{2,1,0:T(8,128)}, u32[]{:S(2)}, u32[]{:S(2)}) collective-permute-start(f32[4,32,512]{2,1,0:T(8,128)S(1)} %get-tuple-element.65), channel_id=1, source_target_pairs={{0,16},{16,0},{1,17},{17,1},{2,18},{18,2},{3,19},{19,3},{4,20},{20... | collective-permute-start | bytes 786440 | tf_op jit(solution)/shard_map/ppermute | solution.py:157
  41.4 19.5 %collective-permute-start.6 = (f32[4,2,32,512]{3,2,1,0:T(8,128)S(1)}, f32[4,2,32,512]{3,2,1,0:T(8,128)S(1)}, u32[]{:S(2)}, u32[]{:S(2)}) collective-permute-start(f32[4,2,32,512]{3,2,1,0:T(8,128)S(1)} %pad_maximum_fusion.3), channel_id=1, source_target_pairs={{0,2},{2,0},{1,3},{3,1},{4,6},{6,4},{5,7},{7,5},{8,10},{10,8},{9,1... | collective-permute-start | bytes 1572872 | tf_op jit(solution)/shard_map/ppermute | solution.py:157
  44.0 16.9 %collective-permute-start.4 = (f32[4,2,32,512]{3,2,0,1:T(8,128)S(1)}, f32[4,2,32,512]{3,2,0,1:T(8,128)S(1)}, u32[]{:S(2)}, u32[]{:S(2)}) collective-permute-start(f32[4,2,32,512]{3,2,0,1:T(8,128)S(1)} %pad_maximum_fusion.2), channel_id=1, source_target_pairs={{0,16},{16,0},{1,17},{17,1},{2,18},{18,2},{3,19},{19,3},{4,20},{20... | collective-permute-start | bytes 1572872 | tf_op jit(solution)/shard_map/ppermute | solution.py:157
  48.5 12.5 %copy-start.4 = (bf16[1024,1024]{1,0:T(8,128)(2,1)}, bf16[1024,1024]{1,0:T(8,128)(2,1)S(1)}, u32[]{:S(2)}) copy-start(bf16[1024,1024]{1,0:T(8,128)(2,1)S(1)} %get-tuple-element.41.refs_2_) | copy-start | bytes 6291460
  48.5 12.5 %copy-start.6 = (bf16[1024,1024]{1,0:T(8,128)(2,1)}, bf16[1024,1024]{1,0:T(8,128)(2,1)S(1)}, u32[]{:S(2)}) copy-start(bf16[1024,1024]{1,0:T(8,128)(2,1)S(1)} %get-tuple-element.42.refs_3_) | copy-start | bytes 6291460
  61.1 3.8 %copy-start.10 = (f32[256,128]{1,0:T(8,128)S(1)}, f32[256,128]{1,0:T(8,128)}, u32[]{:S(2)}) copy-start(f32[256,128]{1,0:T(8,128)} %param.6) | copy-start | bytes 393220
  64.8 15.3 %collective-permute-start.8 = (f32[4,2,2,32,1024]{4,3,2,1,0:T(8,128)}, f32[4,2,2,32,1024]{4,3,2,1,0:T(8,128)}, u32[]{:S(2)}, u32[]{:S(2)}) collective-permute-start(f32[4,2,2,32,1024]{4,3,2,1,0:T(8,128)} %maximum_maximum_fusion), channel_id=1, source_target_pairs={{0,1},{1,0},{2,3},{3,2},{4,5},{5,4},{6,7},{7,6},{8,9},{9,8},{10,11... | collective-permute-start | bytes 6291464 | tf_op jit(solution)/shard_map/ppermute | solution.py:157
  65.0 3.8 %collective-permute-start.9 = (f32[2,32,256]{2,1,0:T(8,128)S(1)}, f32[2,32,256]{2,1,0:T(8,128)S(1)}, u32[]{:S(2)}, u32[]{:S(2)}) collective-permute-start(f32[2,32,256]{2,1,0:T(8,128)S(1)} %dynamic-slice_bitcast_fusion), channel_id=1, source_target_pairs={{0,1},{1,0},{2,3},{3,2},{4,5},{5,4},{6,7},{7,6},{8,9},{9,8},{10,11... | collective-permute-start | bytes 196616 | tf_op jit(solution)/shard_map/ppermute | solution.py:157
  68.8 1.6 %copy-start.1 = (bf16[1024,1024]{1,0:T(8,128)(2,1)S(1)}, bf16[1024,1024]{1,0:T(8,128)(2,1)}, u32[]{:S(2)}) copy-start(bf16[1024,1024]{1,0:T(8,128)(2,1)} %copy-done) | copy-start | bytes 6291460
  70.4 1.6 %copy-start.3 = (bf16[1024,1024]{1,0:T(8,128)(2,1)S(1)}, bf16[1024,1024]{1,0:T(8,128)(2,1)}, u32[]{:S(2)}) copy-start(bf16[1024,1024]{1,0:T(8,128)(2,1)} %copy-done.2) | copy-start | bytes 6291460
  73.5 1.6 %copy-start.7 = (bf16[1024,1024]{1,0:T(8,128)(2,1)S(1)}, bf16[1024,1024]{1,0:T(8,128)(2,1)}, u32[]{:S(2)}) copy-start(bf16[1024,1024]{1,0:T(8,128)(2,1)} %copy-done.6) | copy-start | bytes 6291460
  75.1 5.0 %copy-start.9 = (f32[4,2,2,32,1024]{4,3,2,1,0:T(8,128)S(1)}, f32[4,2,2,32,1024]{4,3,2,1,0:T(8,128)}, u32[]{:S(2)}) copy-start(f32[4,2,2,32,1024]{4,3,2,1,0:T(8,128)} %maximum_maximum_fusion) | copy-start | bytes 6291460
  78.6 14.3 %collective-permute-start.10 = (f32[128,1024]{1,0:T(8,128)S(1)}, f32[128,1024]{1,0:T(8,128)S(1)}, u32[]{:S(2)}, u32[]{:S(2)}) collective-permute-start(f32[128,1024]{1,0:T(8,128)S(1)} %get-tuple-element.44), channel_id=1, source_target_pairs={{0,2},{2,0},{1,3},{3,1},{4,6},{6,4},{5,7},{7,5},{8,10},{10,8},{9,1... | collective-permute-start | bytes 1572872 | tf_op jit(solution)/shard_map/ppermute | solution.py:157
  98.1 8.3 %collective-permute-start.11 = (f32[128,256]{1,0:T(8,128)S(1)}, f32[128,256]{1,0:T(8,128)S(1)}, u32[]{:S(2)}, u32[]{:S(2)}) collective-permute-start(f32[128,256]{1,0:T(8,128)S(1)} %get-tuple-element.46), channel_id=1, source_target_pairs={{0,12},{4,8},{8,4},{12,0},{1,13},{5,9},{9,5},{13,1},{2,14},{6,10},... | collective-permute-start | bytes 393224 | tf_op jit(solution)/shard_map/ppermute | solution.py:157
  100.4 12.7 %collective-permute-start.12 = (f32[128,256]{1,0:T(8,128)S(1)}, f32[128,256]{1,0:T(8,128)S(1)}, u32[]{:S(2)}, u32[]{:S(2)}) collective-permute-start(f32[128,256]{1,0:T(8,128)S(1)} %get-tuple-element.47), channel_id=1, source_target_pairs={{0,8},{4,12},{8,0},{12,4},{1,9},{5,13},{9,1},{13,5},{2,10},{6,14},... | collective-permute-start | bytes 393224 | tf_op jit(solution)/shard_map/ppermute | solution.py:157
  101.8 11.4 %collective-permute-start.13 = (f32[128,256]{1,0:T(8,128)S(1)}, f32[128,256]{1,0:T(8,128)S(1)}, u32[]{:S(2)}, u32[]{:S(2)}) collective-permute-start(f32[128,256]{1,0:T(8,128)S(1)} %get-tuple-element.48), channel_id=1, source_target_pairs={{0,4},{4,0},{8,12},{12,8},{1,5},{5,1},{9,13},{13,9},{2,6},{6,2},{1... | collective-permute-start | bytes 393224 | tf_op jit(solution)/shard_map/ppermute | solution.py:157
  113.2 1.3 %collective-permute-start.14 = (f32[64,256]{1,0:T(8,128)S(1)}, f32[64,256]{1,0:T(8,128)S(1)}, u32[]{:S(2)}, u32[]{:S(2)}) collective-permute-start(f32[64,256]{1,0:T(8,128)S(1)} %get-tuple-element.50), channel_id=1, source_target_pairs={{0,1},{1,0},{2,3},{3,2},{4,5},{5,4},{6,7},{7,6},{8,9},{9,8},{10,11... | collective-permute-start | bytes 196616 | tf_op jit(solution)/shard_map/ppermute | solution.py:157
  (3 other events, 4.3 us)

commit v3 on v2

v3 whole, which is shorter than its diff:
```python
import functools
import math

import jax
import jax.numpy as jnp
from jax import lax
from jax.experimental import pallas as pl
from jax.experimental.pallas import tpu as pltpu
from jax.sharding import Mesh
from jax.sharding import PartitionSpec as P

HIGHEST = lax.Precision.HIGHEST
SIZE = 128
VMEM = pl.BlockSpec(memory_space=pltpu.VMEM)
SMEM = pl.BlockSpec(memory_space=pltpu.SMEM)
QUERY_CUTS = (32,)


def exact(a, b):
    return jnp.dot(a, b, precision=HIGHEST, preferred_element_type=jnp.float32)


def exact_t(a, b):
    return lax.dot_general(a, b, (((1,), (1,)), ((), ())), precision=HIGHEST, preferred_element_type=jnp.float32)


def call(kernel, outs, scratch=(), flops=10**6, scalars=0, spare=4):
    def run(*args):
        moved = sum(a.size * a.dtype.itemsize for a in args)
        held = sum(math.prod(a.shape) * a.dtype.itemsize for a in (*jax.tree.leaves(outs), *scratch))
        return pl.pallas_call(
            kernel,
            out_shape=outs,
            in_specs=[SMEM] * scalars + [VMEM] * (len(args) - scalars),
            out_specs=jax.tree.map(lambda _: VMEM, outs),
            scratch_shapes=list(scratch),
            cost_estimate=pl.CostEstimate(flops=flops, bytes_accessed=moved, transcendentals=0),
            compiler_params=pltpu.CompilerParams(vmem_limit_bytes=moved + held + spare * 2**20),
        )(*args)

    return run


def shape(*dims, dtype=jnp.float32):
    return jax.ShapeDtypeStruct(dims, dtype)


def share_kernel(where_ref, strip_ref, share_ref):
    row, group, side, core = (where_ref[i] for i in range(4))
    count = share_ref.shape[0]
    start = (group * 4 + side * 2 + core) * count
    share_ref[...] = strip_ref[pl.ds(pl.multiple_of(start, 8), count), :]


def rows_kernel(where_ref, share_ref, *refs):
    *landed_refs, near_ref, far_ref = refs
    half = near_ref.shape[2]
    for step, ref in enumerate((share_ref, *landed_refs)):
        near_ref[where_ref[0] ^ step] = ref[:, pl.ds(0, half)]
        far_ref[where_ref[0] ^ step] = ref[:, pl.ds(half, half)]


def first_kernel(where_ref, near_ref, near_other_ref, far_ref, far_other_ref, near_out, far_out):
    row, group, side, core = (where_ref[i] for i in range(4))
    near_out[side] = near_ref[...]
    near_out[1 - side] = near_other_ref[...]
    far_out[group] = far_ref[...]
    far_out[1 - group] = far_other_ref[...]


def second_kernel(where_ref, near_ref, near_other_ref, far_ref, far_other_ref, out_ref):
    row, group, side, core = (where_ref[i] for i in range(4))
    half = near_ref.shape[3]
    for r in range(4):
        for i in range(2):
            out_ref[r, group, i, :, pl.ds(0, half)] = near_ref[i, r]
            out_ref[r, 1 - group, i, :, pl.ds(0, half)] = near_other_ref[i, r]
            out_ref[r, i, side, :, pl.ds(half, half)] = far_ref[i, r]
            out_ref[r, i, 1 - side, :, pl.ds(half, half)] = far_other_ref[i, r]


def prepare_kernel(where_ref, own_ref, other_ref, ready_ref, factor_ref):
    core = where_ref[3]
    count = own_ref.shape[3]
    for piece in range(16):
        at = (piece // 4, piece // 2 % 2, piece % 2)
        for ref, index in ((own_ref, core), (other_ref, 1 - core)):
            start = pl.multiple_of((2 * piece + index) * count, 8)
            factor_ref[pl.ds(start, count), :] = ref[at]
    rows = lax.broadcasted_iota(jnp.int32, (SIZE, SIZE), 0)
    cols = lax.broadcasted_iota(jnp.int32, (SIZE, SIZE), 1)
    starts = range(0, factor_ref.shape[0], SIZE)
    blocks = [factor_ref[pl.ds(s, SIZE), pl.ds(s, SIZE)] for s in starts]
    inverses = []
    for block in blocks:
        diagonal = jnp.sum(jnp.where(rows == cols, block, 0.0), axis=1, keepdims=True)
        inverses.append(jnp.where(rows == cols, 1.0 / diagonal, 0.0))
    step = 1
    while step < SIZE:
        below = ((rows // step) % 2 == 1) & (cols // step == rows // step - 1)
        coupled = [exact(jnp.where(below, b, 0.0), i) for b, i in zip(blocks, inverses)]
        inverses = [i - exact(i, c) for i, c in zip(inverses, coupled)]
        step *= 2
    for start, inverse in zip(starts, inverses):
        if start:
            ready_ref[pl.ds(start, SIZE), pl.ds(0, start)] = exact(
                inverse, factor_ref[pl.ds(start, SIZE), pl.ds(0, start)]
            )
        ready_ref[pl.ds(start, SIZE), pl.ds(start, SIZE)] = inverse


def right_kernel(where_ref, right_ref, own_ref, other_ref, by_query):
    core = where_ref[3]
    by_query[...] = right_ref[...].T
    width = own_ref.shape[0] // 2
    for side in range(2):
        for ref, index in ((own_ref, core), (other_ref, 1 - core)):
            start = pl.multiple_of((2 * side + index) * width, 8)
            ref[pl.ds(side * width, width), :] = by_query[pl.ds(start, width), :]


def halves(value):
    high = value.astype(jnp.bfloat16)
    return high, (value - high.astype(jnp.float32)).astype(jnp.bfloat16)


def couple_kernel(where_ref, queries_ref, own_ref, other_ref, kept_ref, far_ref, q_high, q_low):
    side, core = where_ref[2], where_ref[3]
    count, window = kept_ref.shape
    columns = own_ref.shape[1]
    for part in range(2):
        rows = pl.ds(pl.multiple_of(((side + part) % 2) * count, 8), count)
        for half in range(2):
            cols = pl.ds(pl.multiple_of(((core + half) % 2) * columns, 128), columns)
            here = (pl.ds(part * count, count), pl.ds(half * columns, columns))
            q_high[here], q_low[here] = halves(queries_ref[rows, cols])

    def product(a, b):
        return lax.dot_general(a, b, (((1,), (1,)), ((), ())), preferred_element_type=jnp.float32)

    for start in range(0, window, 256):
        here = pl.ds(start, 256)
        total = 0.0
        for half, ref in enumerate((own_ref, other_ref)):
            cols = pl.ds(half * columns, columns)
            high, low = halves(ref[here, :])
            total = total + product(q_high[:, cols], high)
            total = total + product(q_low[:, cols], high) + product(q_high[:, cols], low)
        kept_ref[:, here] = total[:count]
        far_ref[:, here] = total[count:]


def deal_kernel(queries_ref, *out_refs):
    columns = out_refs[0].shape[2]
    offset = 0
    for out_ref in out_refs:
        for chip in range(8):
            out_ref[chip] = queries_ref[pl.ds(offset, out_ref.shape[1]), pl.ds(chip * columns, columns)]
        offset += out_ref.shape[1]


def solve_kernel(where_ref, ready_ref, right_own_ref, right_other_ref, kept_ref, arrived_ref, *out_refs):
    *piece_refs, left = out_refs
    count, strip = right_own_ref.shape
    window = kept_ref.shape[1]
    row, core = where_ref[0], where_ref[3]
    left[...] = -(kept_ref[...] + arrived_ref[...])
    cols = pl.ds(pl.multiple_of(row * strip, strip), strip)
    for ref, index in ((right_own_ref, core), (right_other_ref, 1 - core)):
        here = (pl.ds(pl.multiple_of(index * count, 8), count), cols)
        left[here] = left[here] + ref[...]
    for start in range(0, window, SIZE):
        here = pl.ds(start, SIZE)
        left[:, here] = exact_t(left[:, here], ready_ref[here, here])
    for start in range(0, window, 2 * SIZE):
        first, second = pl.ds(start, SIZE), pl.ds(start + SIZE, SIZE)
        left[:, second] = left[:, second] - exact_t(left[:, first], ready_ref[second, first])
        below = pl.ds(start + 2 * SIZE, window - start - 2 * SIZE)
        if below.size:
            both = pl.ds(start, 2 * SIZE)
            left[:, below] = left[:, below] - exact_t(left[:, both], ready_ref[below, both])
    for step, piece_ref in enumerate(piece_refs):
        piece_ref[...] = left[:, pl.ds(pl.multiple_of((row ^ step) * strip, strip), strip)]


def sum_kernel(where_ref, *refs):
    *piece_refs, own_ref, other_ref, total = refs
    value = piece_refs[0][...]
    for ref in piece_refs[1:]:
        value = value + ref[...]
    total[...] = value
    count = own_ref.shape[0]
    own_ref[...] = total[pl.ds(pl.multiple_of(where_ref[3] * count, 8), count), :]
    other_ref[...] = total[pl.ds(pl.multiple_of((1 - where_ref[3]) * count, 8), count), :]


def finish_kernel(cuts, where_ref, *refs):
    *part_refs, out_ref, total = refs
    offset = 0
    width = sum(cuts)
    for cut, own_ref, other_ref in zip(cuts, part_refs[::2], part_refs[1::2]):
        for ref, core in ((own_ref, where_ref[3]), (other_ref, 1 - where_ref[3])):
            for side in range(2):
                place = pl.multiple_of(side * 2 * width + core * width + offset, 8)
                total[pl.ds(place, cut), :] = ref[pl.ds(side * cut, cut), :]
        offset += cut
    out_ref[...] = total[...].T


def swap(value, axis, step):
    return lax.ppermute(value, axis, [(i, i ^ step) for i in range(lax.axis_size(axis))])


def shards(prev_solution, factor_panel, right_side, window_factor):
    row, group, side, core = (lax.axis_index(a) for a in ("row", "groups", "side", "core"))
    where = jnp.stack([row, group, side, core])
    strip_rows, strip_cols = right_side.shape
    window = window_factor.shape[1]
    width = prev_solution.shape[1]
    share_rows, half_window = strip_rows // 8, window // 2

    share = call(share_kernel, shape(share_rows, window), scalars=1)(where, window_factor)
    landed = [swap(share, "row", step) for step in (1, 2, 3)]
    right_own, right_other = call(
        right_kernel,
        [shape(2 * width, strip_rows)] * 2,
        [pltpu.VMEM((strip_cols, strip_rows), jnp.float32)],
        flops=5 * 10**10,
        scalars=1,
    )(where, right_side)
    panel_other = swap(factor_panel, "core", 1)
    landed, right_own = lax.optimization_barrier((landed, right_own))
    right_other = swap(right_other, "core", 1)
    near, far = call(rows_kernel, [shape(4, share_rows, half_window)] * 2, scalars=1)(where, share, *landed)
    near, far = call(first_kernel, [shape(2, 4, share_rows, half_window)] * 2, scalars=1)(
        where, near, swap(near, "side", 1), far, swap(far, "groups", 1)
    )
    near, panel_other = lax.optimization_barrier((near, panel_other))
    shares = call(second_kernel, shape(4, 2, 2, share_rows, window), scalars=1)(
        where, near, swap(near, "groups", 1), far, swap(far, "side", 1)
    )

    dealt = call(deal_kernel, [shape(8, cut, 2 * factor_panel.shape[1]) for cut in QUERY_CUTS])(prev_solution.T)
    offset = 0
    parts = []
    for number, cut in enumerate(QUERY_CUTS):
        queries = lax.all_to_all(dealt[number], ("row", "side"), split_axis=0, concat_axis=0, tiled=True)
        queries = queries.reshape(8 * cut, -1)
        half = 4 * cut
        if not offset:
            queries, shares, right_other = lax.optimization_barrier((queries, shares, right_other))
            ready = call(
                prepare_kernel, shape(window, window), [pltpu.VMEM((window, window), jnp.float32)], scalars=1
            )(where, shares, swap(shares, "core", 1))
        kept, far = call(
            couple_kernel,
            [shape(half, window)] * 2,
            [pltpu.VMEM(queries.shape, jnp.bfloat16)] * 2,
            scalars=1,
        )(where, queries, factor_panel, panel_other)
        pieces = call(
            solve_kernel, [shape(half, strip_rows)] * 4, [pltpu.VMEM((half, window), jnp.float32)], scalars=1
        )(where, ready, right_own, right_other, kept, swap(far, "side", 1))
        landed = [swap(pieces[step], "row", step) for step in (3, 2, 1)]
        own, other = call(
            sum_kernel, [shape(half // 2, strip_rows)] * 2, [pltpu.VMEM((half, strip_rows), jnp.float32)], scalars=1
        )(where, pieces[0], *landed)
        parts += [own, swap(other, "core", 1)]
        offset += cut
    return call(
        functools.partial(finish_kernel, QUERY_CUTS),
        shape(strip_rows, strip_cols),
        [pltpu.VMEM((strip_cols, strip_rows), jnp.float32)],
        scalars=1,
    )(where, *parts)


def shards_any(prev_solution, factor_panel, right_side, window_factor):
    row = lax.axis_index("row")
    strip_rows, strip_cols = right_side.shape
    by_rows = lax.all_to_all(prev_solution, ("row", "col"), split_axis=0, concat_axis=1, tiled=True)
    factor = lax.all_gather(window_factor, "row", axis=0, tiled=True)
    right = jnp.zeros((factor.shape[0], strip_cols), jnp.float32)
    right = lax.dynamic_update_slice_in_dim(right, right_side, row * strip_rows, 0)
    partial = exact(factor_panel, by_rows)
    coupling = lax.psum_scatter(partial, "col", scatter_dimension=1, tiled=True)
    solved = jax.scipy.linalg.solve_triangular(factor, right - coupling, lower=True)
    return lax.psum_scatter(solved, "row", scatter_dimension=0, tiled=True)


def solution(mesh):
    staged = mesh.shape["groups"] == 2 and mesh.shape["row"] == 4 and mesh.shape["col"] == 4
    if staged:
        mesh = Mesh(mesh.devices.reshape(2, 4, 2, 2), ("groups", "row", "side", "core"))
    col = ("side", "core") if staged else ("col",)
    in_specs = (P(None, ("groups", "row", *col)), P(None, ("row", *col)), P("row", ("groups", *col)), P("row", None))
    out_specs = P("row", ("groups", *col))
    body = shards if staged else shards_any
    return jax.shard_map(body, mesh=mesh, in_specs=in_specs, out_specs=out_specs, check_vma=False)
```

time: 116 us -> 110 us (0.948)
  other arithmetic: 5.74 us -> 0.08 us
  local copies, waits for them, and re-layouts: 15.6 us -> 10.7 us
  waiting for transfers between devices: 46 us -> 49.3 us
  Pallas kernels: 21.6 us -> 24.5 us
    another operation x9 -> x1, other arithmetic: 4.17 us -> 0.08 us  [shards(): where = jnp.stack([row, group, side, core])]
    all_to_all x1 -> x0, local copies, waits for them, and re-layouts: 3.19 us -> none  [shards(): lax.all_to_all(stream, ('row', 'side'), split_axis=0, concat_axis=1, tile...]
    pallas_call x7 -> x11, Pallas kernels: 21.6 us -> 24.5 us  [run(): pl.pallas_call(kernel, out_shape=outs, in_specs=[SMEM] * scalars + [VMEM]...]
    ppermute x15, waiting for transfers between devices: 43.8 us -> 46.2 us  [swap(): lax.ppermute(value, axis, [(i, i ^ step) for i in range(lax.axis_size(axi...]
    concatenate x1 -> x0, other arithmetic: 1.56 us -> none  [gather_window(): return (jnp.concatenate([near, far], axis=-1), first, second)]
    unnamed x23 -> x16, local copies, waits for them, and re-layouts: 11.3 us -> 10.7 us
  transfers between devices with their start and end apart: 16 -> 16, of which waited for: 8 -> 8; matrix products, arithmetic and copies ran while one was open for 8% -> 0% of each run, Pallas kernels for 14% -> 16%
where the time goes in v3:
time: 110 us
  waiting for transfers between devices  49.3 us (45%)
  starting transfers between devices  25.1 us (23%)
  Pallas kernels  24.5 us (22%)
  local copies, waits for them, and re-layouts  10.7 us (10%)
    ppermute x15, waiting for transfers between devices, swap(): lax.ppermute(value, axis, [(i, i ^ step) for i in range(lax.axis_size(axi...  46.2 us
    pallas_call x11, Pallas kernels, run(): pl.pallas_call(kernel, out_shape=outs, in_specs=[SMEM] * scalars + [VMEM]...  24.5 us
    ppermute x15, starting transfers between devices, swap(): lax.ppermute(value, axis, [(i, i ^ step) for i in range(lax.axis_size(axi...  19 us
    unnamed x16, local copies, waits for them, and re-layouts  10.7 us
    all_to_all x1, starting transfers between devices, shards(): lax.all_to_all(dealt[number], ('row', 'side'), split_axis=0, concat_axis=...  6.08 us
    all_to_all x1, waiting for transfers between devices, shards(): lax.all_to_all(dealt[number], ('row', 'side'), split_axis=0, concat_axis=...  3.12 us
  transfers between devices with their start and end apart: 16, of which 8 were waited for; matrix products, arithmetic and copies ran while one was open for 0% of the time, Pallas kernels for 16%

profile of v3, /device:TPU:0, one launch (start us, length us, event | category | flops | bytes accessed | tf_op | source)
XLA Modules:
  0.0 109.8 jit_solution(10788155370532262294)
XLA Ops:
  1.9 5.1 %collective-permute-start.2 = (f32[32,1024]{1,0:T(8,128)S(1)}, f32[32,1024]{1,0:T(8,128)S(1)}, u32[]{:S(2)}, u32[]{:S(2)}) collective-permute-start(f32[32,1024]{1,0:T(8,128)S(1)} %shard_map.47.share_ref), channel_id=1, source_target_pairs={{0,12},{4,8},{8,4},{12,0},{1,13},{5,9},{9,5},{13,1},{2,14},{6,10},... | collective-permute-start | bytes 393224 | tf_op jit(solution)/shard_map/ppermute | solution.py:211
  7.6 1.6 %copy-done.5 = f32[16384,32]{0,1:T(8,128)S(1)} copy-done((f32[16384,32]{0,1:T(8,128)S(1)}, f32[16384,32]{0,1:T(8,128)}, u32[]{:S(2)}) %copy-start.5) | copy-done | bytes 2097176
  9.2 1.5 %shard_map.46 = f32[8,32,2048]{2,1,0:T(8,128)} custom-call(f32[32,16384]{1,0:T(8,128)S(1)} %bitcast.7), custom_call_target="tpu_custom_call" | custom-call | flops 1000000 | bytes 2097152 | tf_op jit(solution)/shard_map/pallas_call | solution.py:31
  10.8 6.1 %all-to-all-start = ((f32[8,32,2048]{2,1,0:T(8,128)}), f32[8,32,2048]{2,1,0:T(8,128)S(1)}, u32[]{:S(2)}, u32[]{:S(2)}) async-start(f32[8,32,2048]{2,1,0:T(8,128)} %shard_map.46), calls=%async_computation | async-start | bytes 4194304 | tf_op jit(solution)/shard_map/all_to_all | solution.py:247
  18.6 1.6 %collective-permute-start.3 = (f32[4,32,512]{2,1,0:T(8,128)S(1)}, f32[4,32,512]{2,1,0:T(8,128)S(1)}, u32[]{:S(2)}, u32[]{:S(2)}) collective-permute-start(f32[4,32,512]{2,1,0:T(8,128)S(1)} %get-tuple-element.32.near_ref), channel_id=1, source_target_pairs={{0,2},{2,0},{1,3},{3,1},{4,6},{6,4},{5,7},{7,5},{8,10},{10,8},{9,1... | collective-permute-start | bytes 786440 | tf_op jit(solution)/shard_map/ppermute | solution.py:211
  20.2 1.5 %collective-permute-start.4 = (f32[4,32,512]{2,1,0:T(8,128)S(1)}, f32[4,32,512]{2,1,0:T(8,128)S(1)}, u32[]{:S(2)}, u32[]{:S(2)}) collective-permute-start(f32[4,32,512]{2,1,0:T(8,128)S(1)} %get-tuple-element.33.far_ref), channel_id=1, source_target_pairs={{0,16},{16,0},{1,17},{17,1},{2,18},{18,2},{3,19},{19,3},{4,20},{20... | collective-permute-start | bytes 786440 | tf_op jit(solution)/shard_map/ppermute | solution.py:211
  21.7 18.6 %collective-permute-done.3.near_other_ref = f32[4,32,512]{2,1,0:T(8,128)S(1)} collective-permute-done((f32[4,32,512]{2,1,0:T(8,128)S(1)}, f32[4,32,512]{2,1,0:T(8,128)S(1)}, u32[]{:S(2)}, u32[]{:S(2)}) %collective-permute-start.3) | collective-permute-done | bytes 262176 | tf_op jit(solution)/shard_map/ppermute | solution.py:211
  40.9 2.5 %collective-permute-start.7 = (f32[2,4,32,512]{3,2,1,0:T(8,128)S(1)}, f32[2,4,32,512]{3,2,1,0:T(8,128)S(1)}, u32[]{:S(2)}, u32[]{:S(2)}) collective-permute-start(f32[2,4,32,512]{3,2,1,0:T(8,128)S(1)} %get-tuple-element.36.far_ref), channel_id=1, source_target_pairs={{0,2},{2,0},{1,3},{3,1},{4,6},{6,4},{5,7},{7,5},{8,10},{10,8},{9,1... | collective-permute-start | bytes 1572872 | tf_op jit(solution)/shard_map/ppermute | solution.py:211
  43.5 2.0 %copy-done.3 = f32[1024,1024]{1,0:T(8,128)} copy-done((f32[1024,1024]{1,0:T(8,128)}, f32[1024,1024]{1,0:T(8,128)S(1)}, u32[]{:S(2)}) %copy-start.3) | copy-done | bytes 4194328
  45.4 1.5 %collective-permute-start.6 = (f32[2,4,32,512]{3,2,1,0:T(8,128)S(1)}, f32[2,4,32,512]{3,2,1,0:T(8,128)S(1)}, u32[]{:S(2)}, u32[]{:S(2)}) collective-permute-start(f32[2,4,32,512]{3,2,1,0:T(8,128)S(1)} %get-tuple-element.35.near_ref), channel_id=1, source_target_pairs={{0,16},{16,0},{1,17},{17,1},{2,18},{18,2},{3,19},{19,3},{4,20},{20... | collective-permute-start | bytes 1572872 | tf_op jit(solution)/shard_map/ppermute | solution.py:211
  46.9 12.1 %collective-permute-done.7.far_other_ref = f32[2,4,32,512]{3,2,1,0:T(8,128)S(1)} collective-permute-done((f32[2,4,32,512]{3,2,1,0:T(8,128)S(1)}, f32[2,4,32,512]{3,2,1,0:T(8,128)S(1)}, u32[]{:S(2)}, u32[]{:S(2)}) %collective-permute-start.7) | collective-permute-done | bytes 524320 | tf_op jit(solution)/shard_map/ppermute | solution.py:211
  59.8 1.4 %copy-done = f32[4,2,2,32,1024]{4,3,2,1,0:T(8,128)} copy-done((f32[4,2,2,32,1024]{4,3,2,1,0:T(8,128)}, f32[4,2,2,32,1024]{4,3,2,1,0:T(8,128)S(1)}, u32[]{:S(2)}) %copy-start) | copy-done | bytes 2097176
  61.1 3.1 %all-to-all-done = f32[8,32,2048]{2,1,0:T(8,128)S(1)} async-done(((f32[8,32,2048]{2,1,0:T(8,128)}), f32[8,32,2048]{2,1,0:T(8,128)S(1)}, u32[]{:S(2)}, u32[]{:S(2)}) %all-to-all-start) | async-done | bytes 2097184 | tf_op jit(solution)/shard_map/all_to_all | solution.py:247
  64.2 2.3 %copy-done.2 = f32[1024,1024]{1,0:T(8,128)S(1)} copy-done((f32[1024,1024]{1,0:T(8,128)S(1)}, f32[1024,1024]{1,0:T(8,128)}, u32[]{:S(2)}) %copy-start.2) | copy-done | bytes 4194328
  66.6 2.2 %copy-done.4 = f32[1024,1024]{1,0:T(8,128)S(1)} copy-done((f32[1024,1024]{1,0:T(8,128)S(1)}, f32[1024,1024]{1,0:T(8,128)}, u32[]{:S(2)}) %copy-start.4) | copy-done | bytes 4194328
  68.8 4.3 %shard_map.53 = (f32[128,1024]{1,0:T(8,128)S(1)}, f32[128,1024]{1,0:T(8,128)S(1)}) custom-call(s32[4]{0:T(128)S(1)} %pad_add_fusion.where_ref, f32[256,2048]{1,0:T(8,128)S(1)} %bitcast.6, f32[1024,1024]{1,0:T(8,128)S(1)} %copy-done.2, f32[1024,1024]{1,0:T(8,128)S(1)} %copy-done.4), custom_call_target="tpu_custom_call" | custom-call | flops 1000000 | bytes 10485776 | tf_op jit(solution)/shard_map/pallas_call | solution.py:31
  73.0 1.6 %collective-permute-start.10 = (f32[128,1024]{1,0:T(8,128)S(1)}, f32[128,1024]{1,0:T(8,128)S(1)}, u32[]{:S(2)}, u32[]{:S(2)}) collective-permute-start(f32[128,1024]{1,0:T(8,128)S(1)} %get-tuple-element.44), channel_id=1, source_target_pairs={{0,2},{2,0},{1,3},{3,1},{4,6},{6,4},{5,7},{7,5},{8,10},{10,8},{9,1... | collective-permute-start | bytes 1572872 | tf_op jit(solution)/shard_map/ppermute | solution.py:211
  74.6 9.2 %shard_map.52.ready_ref = f32[1024,1024]{1,0:T(8,128)S(1)} custom-call(s32[4]{0:T(128)S(1)} %pad_add_fusion.where_ref, f32[4,2,2,32,1024]{4,3,2,1,0:T(8,128)S(1)} %copy-done.1, f32[4,2,2,32,1024]{4,3,2,1,0:T(8,128)S(1)} %collective-permute-done.9.other_ref), custom_call_target="tpu_custom_call" | custom-call | flops 1000000 | bytes 4194320 | tf_op jit(solution)/shard_map/pallas_call | solution.py:31
  83.8 3.5 %collective-permute-done.10.arrived_ref = f32[128,1024]{1,0:T(8,128)S(1)} collective-permute-done((f32[128,1024]{1,0:T(8,128)S(1)}, f32[128,1024]{1,0:T(8,128)S(1)}, u32[]{:S(2)}, u32[]{:S(2)}) %collective-permute-start.10) | collective-permute-done | bytes 524320 | tf_op jit(solution)/shard_map/ppermute | solution.py:211
  87.3 4.6 %shard_map.54 = (f32[128,256]{1,0:T(8,128)S(1)}, f32[128,256]{1,0:T(8,128)S(1)}, f32[128,256]{1,0:T(8,128)S(1)}, f32[128,256]{1,0:T(8,128)S(1)}) custom-call(s32[4]{0:T(128)S(1)} %pad_add_fusion.where_ref, f32[1024,1024]{1,0:T(8,128)S(1)} %shard_map.52.ready_ref, f32[64,256]{1,0:T(8,128)S(1)} %get-tuple-element.39.right_own_ref, ...), custom_call_target="tpu_custom_call" | custom-call | flops 1000000 | bytes 5373968 | tf_op jit(solution)/shard_map/pallas_call | solution.py:31
  91.8 2.1 %collective-permute-start.11 = (f32[128,256]{1,0:T(8,128)S(1)}, f32[128,256]{1,0:T(8,128)S(1)}, u32[]{:S(2)}, u32[]{:S(2)}) collective-permute-start(f32[128,256]{1,0:T(8,128)S(1)} %get-tuple-element.46), channel_id=1, source_target_pairs={{0,12},{4,8},{8,4},{12,0},{1,13},{5,9},{9,5},{13,1},{2,14},{6,10},... | collective-permute-start | bytes 393224 | tf_op jit(solution)/shard_map/ppermute | solution.py:211
  93.9 1.3 %collective-permute-start.12 = (f32[128,256]{1,0:T(8,128)S(1)}, f32[128,256]{1,0:T(8,128)S(1)}, u32[]{:S(2)}, u32[]{:S(2)}) collective-permute-start(f32[128,256]{1,0:T(8,128)S(1)} %get-tuple-element.47), channel_id=1, source_target_pairs={{0,8},{4,12},{8,0},{12,4},{1,9},{5,13},{9,1},{13,5},{2,10},{6,14},... | collective-permute-start | bytes 393224 | tf_op jit(solution)/shard_map/ppermute | solution.py:211
  96.3 3.9 %collective-permute-done.11.refs_1_ = f32[128,256]{1,0:T(8,128)S(1)} collective-permute-done((f32[128,256]{1,0:T(8,128)S(1)}, f32[128,256]{1,0:T(8,128)S(1)}, u32[]{:S(2)}, u32[]{:S(2)}) %collective-permute-start.11) | collective-permute-done | bytes 131104 | tf_op jit(solution)/shard_map/ppermute | solution.py:211
  100.2 6.4 %collective-permute-done.12.refs_2_ = f32[128,256]{1,0:T(8,128)S(1)} collective-permute-done((f32[128,256]{1,0:T(8,128)S(1)}, f32[128,256]{1,0:T(8,128)S(1)}, u32[]{:S(2)}, u32[]{:S(2)}) %collective-permute-start.12) | collective-permute-done | bytes 131104 | tf_op jit(solution)/shard_map/ppermute | solution.py:211
  (36 shorter events, 9.9 us)
Async XLA Ops:
  0.1 1.2 %copy-start.6 = (f32[256,1024]{1,0:T(8,128)S(1)}, f32[256,1024]{1,0:T(8,128)}, u32[]{:S(2)}) copy-start(f32[256,1024]{1,0:T(8,128)} %strip_ref.1) | copy-start | bytes 3145732
  1.9 15.6 %collective-permute-start.2 = (f32[32,1024]{1,0:T(8,128)S(1)}, f32[32,1024]{1,0:T(8,128)S(1)}, u32[]{:S(2)}, u32[]{:S(2)}) collective-permute-start(f32[32,1024]{1,0:T(8,128)S(1)} %shard_map.47.share_ref), channel_id=1, source_target_pairs={{0,12},{4,8},{8,4},{12,0},{1,13},{5,9},{9,5},{13,1},{2,14},{6,10},... | collective-permute-start | bytes 393224 | tf_op jit(solution)/shard_map/ppermute | solution.py:211
  7.0 11.1 %collective-permute-start.1 = (f32[32,1024]{1,0:T(8,128)S(1)}, f32[32,1024]{1,0:T(8,128)S(1)}, u32[]{:S(2)}, u32[]{:S(2)}) collective-permute-start(f32[32,1024]{1,0:T(8,128)S(1)} %shard_map.47.share_ref), channel_id=1, source_target_pairs={{0,8},{4,12},{8,0},{12,4},{1,9},{5,13},{9,1},{13,5},{2,10},{6,14},... | collective-permute-start | bytes 393224 | tf_op jit(solution)/shard_map/ppermute | solution.py:211
  7.0 11.1 %collective-permute-start = (f32[32,1024]{1,0:T(8,128)S(1)}, f32[32,1024]{1,0:T(8,128)S(1)}, u32[]{:S(2)}, u32[]{:S(2)}) collective-permute-start(f32[32,1024]{1,0:T(8,128)S(1)} %shard_map.47.share_ref), channel_id=1, source_target_pairs={{0,4},{4,0},{8,12},{12,8},{1,5},{5,1},{9,13},{13,9},{2,6},{6,2},{1... | collective-permute-start | bytes 393224 | tf_op jit(solution)/shard_map/ppermute | solution.py:211
  7.6 1.6 %copy-start.5 = (f32[16384,32]{0,1:T(8,128)S(1)}, f32[16384,32]{0,1:T(8,128)}, u32[]{:S(2)}) copy-start(f32[16384,32]{0,1:T(8,128)} %param.4) | copy-start | bytes 6291460
  10.7 6.1 %copy-start.7 = (f32[256,128]{1,0:T(8,128)S(1)}, f32[256,128]{1,0:T(8,128)}, u32[]{:S(2)}) copy-start(f32[256,128]{1,0:T(8,128)} %right_ref.1) | copy-start | bytes 393220
  10.8 53.5 %all-to-all-start = ((f32[8,32,2048]{2,1,0:T(8,128)}), f32[8,32,2048]{2,1,0:T(8,128)S(1)}, u32[]{:S(2)}, u32[]{:S(2)}) async-start(f32[8,32,2048]{2,1,0:T(8,128)} %shard_map.46), calls=%async_computation | async-start | bytes 4194304 | tf_op jit(solution)/shard_map/all_to_all | solution.py:247
  16.8 26.6 %collective-permute-start.5 = (f32[1024,1024]{1,0:T(8,128)}, f32[1024,1024]{1,0:T(8,128)S(1)}, u32[]{:S(2)}, u32[]{:S(2)}) collective-permute-start(f32[1024,1024]{1,0:T(8,128)} %own_ref.1), channel_id=1, source_target_pairs={{0,1},{1,0},{2,3},{3,2},{4,5},{5,4},{6,7},{7,6},{8,9},{9,8},{10,11... | collective-permute-start | bytes 12582920 | tf_op jit(solution)/shard_map/ppermute | solution.py:211
  18.6 21.6 %collective-permute-start.3 = (f32[4,32,512]{2,1,0:T(8,128)S(1)}, f32[4,32,512]{2,1,0:T(8,128)S(1)}, u32[]{:S(2)}, u32[]{:S(2)}) collective-permute-start(f32[4,32,512]{2,1,0:T(8,128)S(1)} %get-tuple-element.32.near_ref), channel_id=1, source_target_pairs={{0,2},{2,0},{1,3},{3,1},{4,6},{6,4},{5,7},{7,5},{8,10},{10,8},{9,1... | collective-permute-start | bytes 786440 | tf_op jit(solution)/shard_map/ppermute | solution.py:211
  20.2 20.1 %collective-permute-start.4 = (f32[4,32,512]{2,1,0:T(8,128)S(1)}, f32[4,32,512]{2,1,0:T(8,128)S(1)}, u32[]{:S(2)}, u32[]{:S(2)}) collective-permute-start(f32[4,32,512]{2,1,0:T(8,128)S(1)} %get-tuple-element.33.far_ref), channel_id=1, source_target_pairs={{0,16},{16,0},{1,17},{17,1},{2,18},{18,2},{3,19},{19,3},{4,20},{20... | collective-permute-start | bytes 786440 | tf_op jit(solution)/shard_map/ppermute | solution.py:211
  40.9 18.2 %collective-permute-start.7 = (f32[2,4,32,512]{3,2,1,0:T(8,128)S(1)}, f32[2,4,32,512]{3,2,1,0:T(8,128)S(1)}, u32[]{:S(2)}, u32[]{:S(2)}) collective-permute-start(f32[2,4,32,512]{3,2,1,0:T(8,128)S(1)} %get-tuple-element.36.far_ref), channel_id=1, source_target_pairs={{0,2},{2,0},{1,3},{3,1},{4,6},{6,4},{5,7},{7,5},{8,10},{10,8},{9,1... | collective-permute-start | bytes 1572872 | tf_op jit(solution)/shard_map/ppermute | solution.py:211
  43.5 2.0 %copy-start.3 = (f32[1024,1024]{1,0:T(8,128)}, f32[1024,1024]{1,0:T(8,128)S(1)}, u32[]{:S(2)}) copy-start(f32[1024,1024]{1,0:T(8,128)S(1)} %collective-permute-done.5.other_ref) | copy-start | bytes 12582916
  45.4 13.7 %collective-permute-start.6 = (f32[2,4,32,512]{3,2,1,0:T(8,128)S(1)}, f32[2,4,32,512]{3,2,1,0:T(8,128)S(1)}, u32[]{:S(2)}, u32[]{:S(2)}) collective-permute-start(f32[2,4,32,512]{3,2,1,0:T(8,128)S(1)} %get-tuple-element.35.near_ref), channel_id=1, source_target_pairs={{0,16},{16,0},{1,17},{17,1},{2,18},{18,2},{3,19},{19,3},{4,20},{20... | collective-permute-start | bytes 1572872 | tf_op jit(solution)/shard_map/ppermute | solution.py:211
  46.9 14.2 %collective-permute-start.8 = (f32[64,256]{1,0:T(8,128)S(1)}, f32[64,256]{1,0:T(8,128)S(1)}, u32[]{:S(2)}, u32[]{:S(2)}) collective-permute-start(f32[64,256]{1,0:T(8,128)S(1)} %get-tuple-element.37), channel_id=1, source_target_pairs={{0,1},{1,0},{2,3},{3,2},{4,5},{5,4},{6,7},{7,6},{8,9},{9,8},{10,11... | collective-permute-start | bytes 196616 | tf_op jit(solution)/shard_map/ppermute | solution.py:211
  59.7 1.4 %copy-start = (f32[4,2,2,32,1024]{4,3,2,1,0:T(8,128)}, f32[4,2,2,32,1024]{4,3,2,1,0:T(8,128)S(1)}, u32[]{:S(2)}) copy-start(f32[4,2,2,32,1024]{4,3,2,1,0:T(8,128)S(1)} %shard_map.51.own_ref) | copy-start | bytes 6291460
  64.2 10.4 %copy-start.1 = (f32[4,2,2,32,1024]{4,3,2,1,0:T(8,128)S(1)}, f32[4,2,2,32,1024]{4,3,2,1,0:T(8,128)}, u32[]{:S(2)}) copy-start(f32[4,2,2,32,1024]{4,3,2,1,0:T(8,128)} %copy-done) | copy-start | bytes 6291460
  64.2 10.4 %collective-permute-start.9 = (f32[4,2,2,32,1024]{4,3,2,1,0:T(8,128)}, f32[4,2,2,32,1024]{4,3,2,1,0:T(8,128)S(1)}, u32[]{:S(2)}, u32[]{:S(2)}) collective-permute-start(f32[4,2,2,32,1024]{4,3,2,1,0:T(8,128)} %copy-done), channel_id=1, source_target_pairs={{0,1},{1,0},{2,3},{3,2},{4,5},{5,4},{6,7},{7,6},{8,9},{9,8},{10,11... | collective-permute-start | bytes 6291464 | tf_op jit(solution)/shard_map/ppermute | solution.py:211
  64.2 2.3 %copy-start.2 = (f32[1024,1024]{1,0:T(8,128)S(1)}, f32[1024,1024]{1,0:T(8,128)}, u32[]{:S(2)}) copy-start(f32[1024,1024]{1,0:T(8,128)} %own_ref.1) | copy-start | bytes 12582916
  66.6 2.2 %copy-start.4 = (f32[1024,1024]{1,0:T(8,128)S(1)}, f32[1024,1024]{1,0:T(8,128)}, u32[]{:S(2)}) copy-start(f32[1024,1024]{1,0:T(8,128)} %copy-done.3) | copy-start | bytes 12582916
  73.0 14.3 %collective-permute-start.10 = (f32[128,1024]{1,0:T(8,128)S(1)}, f32[128,1024]{1,0:T(8,128)S(1)}, u32[]{:S(2)}, u32[]{:S(2)}) collective-permute-start(f32[128,1024]{1,0:T(8,128)S(1)} %get-tuple-element.44), channel_id=1, source_target_pairs={{0,2},{2,0},{1,3},{3,1},{4,6},{6,4},{5,7},{7,5},{8,10},{10,8},{9,1... | collective-permute-start | bytes 1572872 | tf_op jit(solution)/shard_map/ppermute | solution.py:211
  91.8 8.3 %collective-permute-start.11 = (f32[128,256]{1,0:T(8,128)S(1)}, f32[128,256]{1,0:T(8,128)S(1)}, u32[]{:S(2)}, u32[]{:S(2)}) collective-permute-start(f32[128,256]{1,0:T(8,128)S(1)} %get-tuple-element.46), channel_id=1, source_target_pairs={{0,12},{4,8},{8,4},{12,0},{1,13},{5,9},{9,5},{13,1},{2,14},{6,10},... | collective-permute-start | bytes 393224 | tf_op jit(solution)/shard_map/ppermute | solution.py:211
  93.9 12.7 %collective-permute-start.12 = (f32[128,256]{1,0:T(8,128)S(1)}, f32[128,256]{1,0:T(8,128)S(1)}, u32[]{:S(2)}, u32[]{:S(2)}) collective-permute-start(f32[128,256]{1,0:T(8,128)S(1)} %get-tuple-element.47), channel_id=1, source_target_pairs={{0,8},{4,12},{8,0},{12,4},{1,9},{5,13},{9,1},{13,5},{2,10},{6,14},... | collective-permute-start | bytes 393224 | tf_op jit(solution)/shard_map/ppermute | solution.py:211
  95.2 11.3 %collective-permute-start.13 = (f32[128,256]{1,0:T(8,128)S(1)}, f32[128,256]{1,0:T(8,128)S(1)}, u32[]{:S(2)}, u32[]{:S(2)}) collective-permute-start(f32[128,256]{1,0:T(8,128)S(1)} %get-tuple-element.48), channel_id=1, source_target_pairs={{0,4},{4,0},{8,12},{12,8},{1,5},{5,1},{9,13},{13,9},{2,6},{6,2},{1... | collective-permute-start | bytes 393224 | tf_op jit(solution)/shard_map/ppermute | solution.py:211
  107.2 1.3 %collective-permute-start.14 = (f32[64,256]{1,0:T(8,128)S(1)}, f32[64,256]{1,0:T(8,128)S(1)}, u32[]{:S(2)}, u32[]{:S(2)}) collective-permute-start(f32[64,256]{1,0:T(8,128)S(1)} %get-tuple-element.50), channel_id=1, source_target_pairs={{0,1},{1,0},{2,3},{3,2},{4,5},{5,4},{6,7},{7,6},{8,9},{9,8},{10,11... | collective-permute-start | bytes 196616 | tf_op jit(solution)/shard_map/ppermute | solution.py:211

commit v4 on v3

--- a/solution.py
+++ b/solution.py
@@ -18,6 +18,14 @@
 
 def exact(a, b):
     return jnp.dot(a, b, precision=HIGHEST, preferred_element_type=jnp.float32)
+
+
+def near(a, b):
+    a_high, a_low = halves(a)
+    b_high, b_low = halves(b)
+    total = jnp.dot(a_high, b_low, preferred_element_type=jnp.float32)
+    total = total + jnp.dot(a_low, b_high, preferred_element_type=jnp.float32)
+    return total + jnp.dot(a_high, b_high, preferred_element_type=jnp.float32)
 
 
 def exact_t(a, b):
@@ -45,13 +53,6 @@
     return jax.ShapeDtypeStruct(dims, dtype)
 
 
-def share_kernel(where_ref, strip_ref, share_ref):
-    row, group, side, core = (where_ref[i] for i in range(4))
-    count = share_ref.shape[0]
-    start = (group * 4 + side * 2 + core) * count
-    share_ref[...] = strip_ref[pl.ds(pl.multiple_of(start, 8), count), :]
-
-
 def rows_kernel(where_ref, share_ref, *refs):
     *landed_refs, near_ref, far_ref = refs
     half = near_ref.shape[2]
@@ -92,15 +93,20 @@
     starts = range(0, factor_ref.shape[0], SIZE)
     blocks = [factor_ref[pl.ds(s, SIZE), pl.ds(s, SIZE)] for s in starts]
     inverses = []
+    below = (rows % 2 == 1) & (cols == rows - 1)
     for block in blocks:
-        diagonal = jnp.sum(jnp.where(rows == cols, block, 0.0), axis=1, keepdims=True)
-        inverses.append(jnp.where(rows == cols, 1.0 / diagonal, 0.0))
-    step = 1
+        lane = 1.0 / jnp.sum(jnp.where(rows == cols, block, 0.0), axis=0, keepdims=True)
+        sublane = 1.0 / jnp.sum(jnp.where(rows == cols, block, 0.0), axis=1, keepdims=True)
+        inverses.append(jnp.where(rows == cols, sublane, 0.0) - jnp.where(below, sublane * block * lane, 0.0))
+    step = 2
     while step < SIZE:
         below = ((rows // step) % 2 == 1) & (cols // step == rows // step - 1)
-        coupled = [exact(jnp.where(below, b, 0.0), i) for b, i in zip(blocks, inverses)]
-        inverses = [i - exact(i, c) for i, c in zip(inverses, coupled)]
+        coupled = [near(jnp.where(below, b, 0.0), i) for b, i in zip(blocks, inverses)]
+        inverses = [i - near(i, c) for i, c in zip(inverses, coupled)]
         step *= 2
+    lower = [jnp.where(rows >= cols, block, 0.0) for block in blocks]
+    errors = [jnp.where(rows == cols, 1.0, 0.0) - exact(b, i) for b, i in zip(lower, inverses)]
+    inverses = [i + near(i, e) for i, e in zip(inverses, errors)]
     for start, inverse in zip(starts, inverses):
         if start:
             ready_ref[pl.ds(start, SIZE), pl.ds(0, start)] = exact(
@@ -124,16 +130,20 @@
     return high, (value - high.astype(jnp.float32)).astype(jnp.bfloat16)
 
 
-def couple_kernel(where_ref, queries_ref, own_ref, other_ref, kept_ref, far_ref, q_high, q_low):
+def split_kernel(where_ref, queries_ref, high_ref, low_ref):
     side, core = where_ref[2], where_ref[3]
-    count, window = kept_ref.shape
-    columns = own_ref.shape[1]
+    count, columns = queries_ref.shape[0] // 2, queries_ref.shape[1] // 2
     for part in range(2):
         rows = pl.ds(pl.multiple_of(((side + part) % 2) * count, 8), count)
         for half in range(2):
             cols = pl.ds(pl.multiple_of(((core + half) % 2) * columns, 128), columns)
             here = (pl.ds(part * count, count), pl.ds(half * columns, columns))
-            q_high[here], q_low[here] = halves(queries_ref[rows, cols])
+            high_ref[here], low_ref[here] = halves(queries_ref[rows, cols])
+
+
+def multiply(high_ref, low_ref, panel_refs, kept_ref, far_ref):
+    count, window = kept_ref.shape
+    columns = panel_refs[0].shape[1]
 
     def product(a, b):
         return lax.dot_general(a, b, (((1,), (1,)), ((), ())), preferred_element_type=jnp.float32)
@@ -141,13 +151,22 @@
     for start in range(0, window, 256):
         here = pl.ds(start, 256)
         total = 0.0
-        for half, ref in enumerate((own_ref, other_ref)):
+        for half, ref in enumerate(panel_refs):
             cols = pl.ds(half * columns, columns)
             high, low = halves(ref[here, :])
-            total = total + product(q_high[:, cols], high)
-            total = total + product(q_low[:, cols], high) + product(q_high[:, cols], low)
+            total = total + product(high_ref[:, cols], high)
+            total = total + product(low_ref[:, cols], high) + product(high_ref[:, cols], low)
         kept_ref[:, here] = total[:count]
         far_ref[:, here] = total[count:]
+
+
+def couple_kernel(where_ref, queries_ref, own_ref, other_ref, kept_ref, far_ref, high_ref, low_ref):
+    split_kernel(where_ref, queries_ref, high_ref, low_ref)
+    multiply(high_ref, low_ref, (own_ref, other_ref), kept_ref, far_ref)
+
+
+def couple_more_kernel(high_ref, low_ref, own_ref, other_ref, kept_ref, far_ref):
+    multiply(high_ref, low_ref, (own_ref, other_ref), kept_ref, far_ref)
 
 
 def deal_kernel(queries_ref, *out_refs):
@@ -159,28 +178,49 @@
         offset += out_ref.shape[1]
 
 
-def solve_kernel(where_ref, ready_ref, right_own_ref, right_other_ref, kept_ref, arrived_ref, *out_refs):
-    *piece_refs, left = out_refs
-    count, strip = right_own_ref.shape
-    window = kept_ref.shape[1]
+def solve_part(base, where_ref, ready_ref, right_refs, kept_ref, arrived_ref, left):
+    count, strip = right_refs[0].shape
+    rows = kept_ref.shape[1]
     row, core = where_ref[0], where_ref[3]
-    left[...] = -(kept_ref[...] + arrived_ref[...])
-    cols = pl.ds(pl.multiple_of(row * strip, strip), strip)
-    for ref, index in ((right_own_ref, core), (right_other_ref, 1 - core)):
-        here = (pl.ds(pl.multiple_of(index * count, 8), count), cols)
-        left[here] = left[here] + ref[...]
-    for start in range(0, window, SIZE):
+    part = pl.ds(base, rows)
+    left[:, part] = -(kept_ref[...] + arrived_ref[...])
+
+    @pl.when(row // (rows // strip) == base // rows)
+    def _():
+        cols = pl.ds(pl.multiple_of(row * strip, strip), strip)
+        for ref, index in zip(right_refs, (core, 1 - core)):
+            here = (pl.ds(pl.multiple_of(index * count, 8), count), cols)
+            left[here] = left[here] + ref[...]
+
+    for start in range(base, base + rows, SIZE):
         here = pl.ds(start, SIZE)
         left[:, here] = exact_t(left[:, here], ready_ref[here, here])
-    for start in range(0, window, 2 * SIZE):
+    if base:
+        solved = pl.ds(0, base)
+        left[:, part] = left[:, part] - exact_t(left[:, solved], ready_ref[part, solved])
+    for start in range(base, base + rows, 2 * SIZE):
         first, second = pl.ds(start, SIZE), pl.ds(start + SIZE, SIZE)
         left[:, second] = left[:, second] - exact_t(left[:, first], ready_ref[second, first])
-        below = pl.ds(start + 2 * SIZE, window - start - 2 * SIZE)
+        below = pl.ds(start + 2 * SIZE, base + rows - start - 2 * SIZE)
         if below.size:
             both = pl.ds(start, 2 * SIZE)
             left[:, below] = left[:, below] - exact_t(left[:, both], ready_ref[below, both])
+
+
+def solve_first_kernel(where_ref, ready_ref, right_own_ref, right_other_ref, kept_ref, arrived_ref, solved_ref):
+    solve_part(0, where_ref, ready_ref, (right_own_ref, right_other_ref), kept_ref, arrived_ref, solved_ref)
+
+
+def solve_second_kernel(
+    where_ref, ready_ref, right_own_ref, right_other_ref, solved_ref, kept_ref, arrived_ref, *out_refs
+):
+    *piece_refs, left = out_refs
+    strip = right_own_ref.shape[1]
+    base = solved_ref.shape[1]
+    left[:, pl.ds(0, base)] = solved_ref[...]
+    solve_part(base, where_ref, ready_ref, (right_own_ref, right_other_ref), kept_ref, arrived_ref, left)
     for step, piece_ref in enumerate(piece_refs):
-        piece_ref[...] = left[:, pl.ds(pl.multiple_of((row ^ step) * strip, strip), strip)]
+        piece_ref[...] = left[:, pl.ds(pl.multiple_of((where_ref[0] ^ step) * strip, strip), strip)]
 
 
 def sum_kernel(where_ref, *refs):
@@ -219,7 +259,7 @@
     width = prev_solution.shape[1]
     share_rows, half_window = strip_rows // 8, window // 2
 
-    share = call(share_kernel, shape(share_rows, window), scalars=1)(where, window_factor)
+    share = lax.dynamic_slice_in_dim(window_factor, (group * 4 + side * 2 + core) * share_rows, share_rows, 0)
     landed = [swap(share, "row", step) for step in (1, 2, 3)]
     right_own, right_other = call(
         right_kernel,
@@ -228,14 +268,15 @@
         flops=5 * 10**10,
         scalars=1,
     )(where, right_side)
-    panel_other = swap(factor_panel, "core", 1)
+    panels = [factor_panel[:half_window], factor_panel[half_window:]]
+    others = [swap(panel, "core", 1) for panel in panels]
     landed, right_own = lax.optimization_barrier((landed, right_own))
     right_other = swap(right_other, "core", 1)
     near, far = call(rows_kernel, [shape(4, share_rows, half_window)] * 2, scalars=1)(where, share, *landed)
     near, far = call(first_kernel, [shape(2, 4, share_rows, half_window)] * 2, scalars=1)(
         where, near, swap(near, "side", 1), far, swap(far, "groups", 1)
     )
-    near, panel_other = lax.optimization_barrier((near, panel_other))
+    near, others, right_other = lax.optimization_barrier((near, others, right_other))
     shares = call(second_kernel, shape(4, 2, 2, share_rows, window), scalars=1)(
         where, near, swap(near, "groups", 1), far, swap(far, "side", 1)
     )
@@ -248,19 +289,25 @@
         queries = queries.reshape(8 * cut, -1)
         half = 4 * cut
         if not offset:
-            queries, shares, right_other = lax.optimization_barrier((queries, shares, right_other))
+            queries, shares = lax.optimization_barrier((queries, shares))
+        kept, far, high, low = call(
+            couple_kernel,
+            [shape(half, half_window)] * 2 + [shape(*queries.shape, dtype=jnp.bfloat16)] * 2,
+            scalars=1,
+        )(where, queries, panels[0], others[0])
+        if not offset:
+            far, shares = lax.optimization_barrier((far, shares))
             ready = call(
                 prepare_kernel, shape(window, window), [pltpu.VMEM((window, window), jnp.float32)], scalars=1
             )(where, shares, swap(shares, "core", 1))
-        kept, far = call(
-            couple_kernel,
-            [shape(half, window)] * 2,
-            [pltpu.VMEM(queries.shape, jnp.bfloat16)] * 2,
-            scalars=1,
-        )(where, queries, factor_panel, panel_other)
+        kept_more, far_more = call(couple_more_kernel, [shape(half, half_window)] * 2)(high, low, panels[1], others[1])
+        rights = (right_own, right_other)
+        solved = call(solve_first_kernel, shape(half, half_window), scalars=1)(
+            where, ready, *rights, kept, swap(far, "side", 1)
+        )
         pieces = call(
-            solve_kernel, [shape(half, strip_rows)] * 4, [pltpu.VMEM((half, window), jnp.float32)], scalars=1
-        )(where, ready, right_own, right_other, kept, swap(far, "side", 1))
+            solve_second_kernel, [shape(half, strip_rows)] * 4, [pltpu.VMEM((half, window), jnp.float32)], scalars=1
+        )(where, ready, *rights, solved, kept_more, swap(far_more, "side", 1))
         landed = [swap(pieces[step], "row", step) for step in (3, 2, 1)]
         own, other = call(
             sum_kernel, [shape(half // 2, strip_rows)] * 2, [pltpu.VMEM((half, strip_rows), jnp.float32)], scalars=1

time: 110 us -> 107 us (0.973)
  waiting for transfers between devices: 49.3 us -> 38.8 us
  starting transfers between devices: 25.1 us -> 31.5 us
    ppermute x15 -> x17, waiting for transfers between devices: 46.2 us -> 35.6 us  [swap(): lax.ppermute(value, axis, [(i, i ^ step) for i in range(lax.axis_size(axi...]
    ppermute x15 -> x17, starting transfers between devices: 19 us -> 25.5 us  [swap(): lax.ppermute(value, axis, [(i, i ^ step) for i in range(lax.axis_size(axi...]
    slice x0 -> x1, local copies, waits for them, and re-layouts: none -> 4.82 us  [shards(): panels = [factor_panel[:half_window], factor_panel[half_window:]]]
    unnamed x16 -> x12, local copies, waits for them, and re-layouts: 10.7 us -> 6.44 us
    pallas_call x11 -> x12, Pallas kernels: 24.5 us -> 24.6 us  [run(): pl.pallas_call(kernel, out_shape=outs, in_specs=[SMEM] * scalars + [VMEM]...]
  transfers between devices with their start and end apart: 16 -> 18, of which waited for: 8 -> 7; matrix products, arithmetic and copies ran while one was open for 0% -> 5% of each run, Pallas kernels for 16% -> 14%
where the time goes in v4:
time: 107 us; the launch traced here: 106 us
  waiting for transfers between devices  38.8 us (36%)
  starting transfers between devices  31.5 us (29%)
  Pallas kernels  24.6 us (23%)
  local copies, waits for them, and re-layouts  11.3 us (11%)
    ppermute x17, waiting for transfers between devices, swap(): lax.ppermute(value, axis, [(i, i ^ step) for i in range(lax.axis_size(axi...  35.6 us
    ppermute x17, starting transfers between devices, swap(): lax.ppermute(value, axis, [(i, i ^ step) for i in range(lax.axis_size(axi...  25.5 us
    pallas_call x12, Pallas kernels, run(): pl.pallas_call(kernel, out_shape=outs, in_specs=[SMEM] * scalars + [VMEM]...  24.6 us
    unnamed x12, local copies, waits for them, and re-layouts  6.44 us
    all_to_all x1, starting transfers between devices, shards(): lax.all_to_all(dealt[number], ('row', 'side'), split_axis=0, concat_axis=...  5.95 us
    slice x1, local copies, waits for them, and re-layouts, shards(): panels = [factor_panel[:half_window], factor_panel[half_window:]]  4.82 us
    all_to_all x1, waiting for transfers between devices, shards(): lax.all_to_all(dealt[number], ('row', 'side'), split_axis=0, concat_axis=...  3.11 us
  transfers between devices with their start and end apart: 18, of which 7 were waited for; matrix products, arithmetic and copies ran while one was open for 5% of the time, Pallas kernels for 14%

profile of v4, /device:TPU:0, one launch (start us, length us, event | category | flops | bytes accessed | tf_op | source)
XLA Modules:
  0.0 106.4 jit_solution(9847031952255652666)
XLA Ops:
  1.2 5.1 %collective-permute-start.2 = (f32[32,1024]{1,0:T(8,128)S(1)}, f32[32,1024]{1,0:T(8,128)S(1)}, u32[]{:S(2)}, u32[]{:S(2)}) collective-permute-start(f32[32,1024]{1,0:T(8,128)S(1)} %constant_dynamic-slice_fusion.share_ref), channel_id=1, source_target_pairs={{0,12},{4,8},{8,4},{12,0},{1,13},{5,9},{9,5},{13,1},{2,14},{6,10},... | collective-permute-start | bytes 393224 | tf_op jit(solution)/shard_map/ppermute | solution.py:251
  7.0 1.6 %copy-done.4 = f32[16384,32]{0,1:T(8,128)S(1)} copy-done((f32[16384,32]{0,1:T(8,128)S(1)}, f32[16384,32]{0,1:T(8,128)}, u32[]{:S(2)}) %copy-start.4) | copy-done | bytes 2097176
  8.7 1.4 %copy-done.1 = f32[8,32,2048]{2,1,0:T(8,128)} copy-done((f32[8,32,2048]{2,1,0:T(8,128)}, f32[8,32,2048]{2,1,0:T(8,128)S(1)}, u32[]{:S(2)}) %copy-start.1) | copy-done | bytes 2097176
  10.1 5.9 %all-to-all-start = ((f32[8,32,2048]{2,1,0:T(8,128)}), f32[8,32,2048]{2,1,0:T(8,128)S(1)}, u32[]{:S(2)}, u32[]{:S(2)}) async-start(f32[8,32,2048]{2,1,0:T(8,128)} %copy-done.1), calls=%async_computation | async-start | bytes 4194304 | tf_op jit(solution)/shard_map/all_to_all | solution.py:288
  16.0 4.8 %fusion = (f32[512,1024]{1,0:T(8,128)}, f32[512,1024]{1,0:T(8,128)}) fusion(f32[1024,1024]{1,0:T(8,128)} %param.5), kind=kLoop, calls=%fused_computation.2 | loop fusion | bytes 8388608 | tf_op jit(solution)/shard_map/slice | solution.py:271
  24.1 2.1 %collective-permute-start.3 = (f32[4,32,512]{2,1,0:T(8,128)S(1)}, f32[4,32,512]{2,1,0:T(8,128)S(1)}, u32[]{:S(2)}, u32[]{:S(2)}) collective-permute-start(f32[4,32,512]{2,1,0:T(8,128)S(1)} %get-tuple-element.39.near_ref), channel_id=1, source_target_pairs={{0,2},{2,0},{1,3},{3,1},{4,6},{6,4},{5,7},{7,5},{8,10},{10,8},{9,1... | collective-permute-start | bytes 786440 | tf_op jit(solution)/shard_map/ppermute | solution.py:251
  26.2 1.5 %collective-permute-start.4 = (f32[4,32,512]{2,1,0:T(8,128)S(1)}, f32[4,32,512]{2,1,0:T(8,128)S(1)}, u32[]{:S(2)}, u32[]{:S(2)}) collective-permute-start(f32[4,32,512]{2,1,0:T(8,128)S(1)} %get-tuple-element.40.far_ref), channel_id=1, source_target_pairs={{0,16},{16,0},{1,17},{17,1},{2,18},{18,2},{3,19},{19,3},{4,20},{20... | collective-permute-start | bytes 786440 | tf_op jit(solution)/shard_map/ppermute | solution.py:251
  27.7 11.8 %collective-permute-done.3.near_other_ref = f32[4,32,512]{2,1,0:T(8,128)S(1)} collective-permute-done((f32[4,32,512]{2,1,0:T(8,128)S(1)}, f32[4,32,512]{2,1,0:T(8,128)S(1)}, u32[]{:S(2)}, u32[]{:S(2)}) %collective-permute-start.3) | collective-permute-done | bytes 262176 | tf_op jit(solution)/shard_map/ppermute | solution.py:251
  40.1 2.5 %collective-permute-start.9 = (f32[2,4,32,512]{3,2,1,0:T(8,128)S(1)}, f32[2,4,32,512]{3,2,1,0:T(8,128)S(1)}, u32[]{:S(2)}, u32[]{:S(2)}) collective-permute-start(f32[2,4,32,512]{3,2,1,0:T(8,128)S(1)} %get-tuple-element.44.far_ref), channel_id=1, source_target_pairs={{0,2},{2,0},{1,3},{3,1},{4,6},{6,4},{5,7},{7,5},{8,10},{10,8},{9,1... | collective-permute-start | bytes 1572872 | tf_op jit(solution)/shard_map/ppermute | solution.py:251
  42.7 1.6 %collective-permute-start.8 = (f32[2,4,32,512]{3,2,1,0:T(8,128)S(1)}, f32[2,4,32,512]{3,2,1,0:T(8,128)S(1)}, u32[]{:S(2)}, u32[]{:S(2)}) collective-permute-start(f32[2,4,32,512]{3,2,1,0:T(8,128)S(1)} %get-tuple-element.43.near_ref), channel_id=1, source_target_pairs={{0,16},{16,0},{1,17},{17,1},{2,18},{18,2},{3,19},{19,3},{4,20},{20... | collective-permute-start | bytes 1572872 | tf_op jit(solution)/shard_map/ppermute | solution.py:251
  44.3 14.0 %collective-permute-done.9.far_other_ref = f32[2,4,32,512]{3,2,1,0:T(8,128)S(1)} collective-permute-done((f32[2,4,32,512]{3,2,1,0:T(8,128)S(1)}, f32[2,4,32,512]{3,2,1,0:T(8,128)S(1)}, u32[]{:S(2)}, u32[]{:S(2)}) %collective-permute-start.9) | collective-permute-done | bytes 524320 | tf_op jit(solution)/shard_map/ppermute | solution.py:251
  59.0 1.4 %copy-done.2 = f32[4,2,2,32,1024]{4,3,2,1,0:T(8,128)} copy-done((f32[4,2,2,32,1024]{4,3,2,1,0:T(8,128)}, f32[4,2,2,32,1024]{4,3,2,1,0:T(8,128)S(1)}, u32[]{:S(2)}) %copy-start.2) | copy-done | bytes 2097176
  60.3 3.1 %all-to-all-done = f32[8,32,2048]{2,1,0:T(8,128)S(1)} async-done(((f32[8,32,2048]{2,1,0:T(8,128)}), f32[8,32,2048]{2,1,0:T(8,128)S(1)}, u32[]{:S(2)}, u32[]{:S(2)}) %all-to-all-start) | async-done | bytes 2097184 | tf_op jit(solution)/shard_map/all_to_all | solution.py:288
  63.4 4.3 %shard_map.51 = (f32[128,512]{1,0:T(8,128)S(1)}, f32[128,512]{1,0:T(8,128)S(1)}, bf16[256,2048]{1,0:T(8,128)(2,1)S(1)}, bf16[256,2048]{1,0:T(8,128)(2,1)S(1)}) custom-call(s32[4]{0:T(128)S(1)} %pad_add_fusion.where_ref, f32[256,2048]{1,0:T(8,128)S(1)} %bitcast.6, f32[512,1024]{1,0:T(8,128)} %get-tuple-element.66.own_ref, ...), custom_call_target="tpu_custom_call" | custom-call | flops 1000000 | bytes 6291472 | tf_op jit(solution)/shard_map/pallas_call | solution.py:39
  67.8 1.6 %collective-permute-start.11 = (f32[128,512]{1,0:T(8,128)S(1)}, f32[128,512]{1,0:T(8,128)S(1)}, u32[]{:S(2)}, u32[]{:S(2)}) collective-permute-start(f32[128,512]{1,0:T(8,128)S(1)} %get-tuple-element.53), channel_id=1, source_target_pairs={{0,2},{2,0},{1,3},{3,1},{4,6},{6,4},{5,7},{7,5},{8,10},{10,8},{9,1... | collective-permute-start | bytes 786440 | tf_op jit(solution)/shard_map/ppermute | solution.py:251
  69.4 4.1 %shard_map.54 = (f32[128,512]{1,0:T(8,128)S(1)}, f32[128,512]{1,0:T(8,128)S(1)}) custom-call(bf16[256,2048]{1,0:T(8,128)(2,1)S(1)} %get-tuple-element.54.high_ref, bf16[256,2048]{1,0:T(8,128)(2,1)S(1)} %get-tuple-element.55.low_ref, f32[512,1024]{1,0:T(8,128)} %get-tuple-element.65.own_ref, f32[512,1024]{1,0:T(8,128)} %collective-permute-done.6.other_ref), custom_call_target="tpu_custom_call" | custom-call | flops 1000000 | bytes 6291456 | tf_op jit(solution)/shard_map/pallas_call | solution.py:39
  74.0 5.8 %shard_map.52.ready_ref = f32[1024,1024]{1,0:T(8,128)S(1)} custom-call(s32[4]{0:T(128)S(1)} %pad_add_fusion.where_ref, f32[4,2,2,32,1024]{4,3,2,1,0:T(8,128)S(1)} %copy-done.3, f32[4,2,2,32,1024]{4,3,2,1,0:T(8,128)S(1)} %collective-permute-done.10.other_ref), custom_call_target="tpu_custom_call" | custom-call | flops 1000000 | bytes 4194320 | tf_op jit(solution)/shard_map/pallas_call | solution.py:39
  79.9 2.1 %shard_map.53.solved_ref = f32[128,512]{1,0:T(8,128)S(1)} custom-call(s32[4]{0:T(128)S(1)} %pad_add_fusion.where_ref, f32[1024,1024]{1,0:T(8,128)S(1)} %shard_map.52.ready_ref, f32[64,256]{1,0:T(8,128)S(1)} %get-tuple-element.50.right_own_ref, f32[64,256]{1,0:T(8,128)S(1)} %collective-permute-done.7.right_other_ref, ...), custom_call_target="tpu_custom_call" | custom-call | flops 1000000 | bytes 4849680 | tf_op jit(solution)/shard_map/pallas_call | solution.py:39
  82.2 3.4 %shard_map.55 = (f32[128,256]{1,0:T(8,128)S(1)}, f32[128,256]{1,0:T(8,128)S(1)}, f32[128,256]{1,0:T(8,128)S(1)}, f32[128,256]{1,0:T(8,128)S(1)}) custom-call(s32[4]{0:T(128)S(1)} %pad_add_fusion.where_ref, f32[1024,1024]{1,0:T(8,128)S(1)} %shard_map.52.ready_ref, f32[64,256]{1,0:T(8,128)S(1)} %get-tuple-element.50.right_own_ref, ...), custom_call_target="tpu_custom_call" | custom-call | flops 1000000 | bytes 5111824 | tf_op jit(solution)/shard_map/pallas_call | solution.py:39
  85.6 8.5 %collective-permute-start.13 = (f32[128,256]{1,0:T(8,128)S(1)}, f32[128,256]{1,0:T(8,128)S(1)}, u32[]{:S(2)}, u32[]{:S(2)}) collective-permute-start(f32[128,256]{1,0:T(8,128)S(1)} %get-tuple-element.60), channel_id=1, source_target_pairs={{0,12},{4,8},{8,4},{12,0},{1,13},{5,9},{9,5},{13,1},{2,14},{6,10},... | collective-permute-start | bytes 393224 | tf_op jit(solution)/shard_map/ppermute | solution.py:251
  94.7 3.8 %collective-permute-done.13.refs_1_ = f32[128,256]{1,0:T(8,128)S(1)} collective-permute-done((f32[128,256]{1,0:T(8,128)S(1)}, f32[128,256]{1,0:T(8,128)S(1)}, u32[]{:S(2)}, u32[]{:S(2)}) %collective-permute-start.13) | collective-permute-done | bytes 131104 | tf_op jit(solution)/shard_map/ppermute | solution.py:251
  98.5 4.6 %collective-permute-done.14.refs_2_ = f32[128,256]{1,0:T(8,128)S(1)} collective-permute-done((f32[128,256]{1,0:T(8,128)S(1)}, f32[128,256]{1,0:T(8,128)S(1)}, u32[]{:S(2)}, u32[]{:S(2)}) %collective-permute-start.14) | collective-permute-done | bytes 131104 | tf_op jit(solution)/shard_map/ppermute | solution.py:251
  103.8 1.2 %collective-permute-done.16.refs_1_ = f32[64,256]{1,0:T(8,128)S(1)} collective-permute-done((f32[64,256]{1,0:T(8,128)S(1)}, f32[64,256]{1,0:T(8,128)S(1)}, u32[]{:S(2)}, u32[]{:S(2)}) %collective-permute-start.16) | collective-permute-done | bytes 65568 | tf_op jit(solution)/shard_map/ppermute | solution.py:251
  105.1 1.3 %shard_map.57 = f32[256,128]{1,0:T(8,128)} custom-call(s32[4]{0:T(128)S(1)} %pad_add_fusion.where_ref, f32[64,256]{1,0:T(8,128)S(1)} %get-tuple-element.63.refs_0_, f32[64,256]{1,0:T(8,128)S(1)} %collective-permute-done.16.refs_1_), custom_call_target="tpu_custom_call" | custom-call | flops 1000000 | bytes 131088 | tf_op jit(solution)/shard_map/pallas_call | solution.py:39
  (39 shorter events, 8.6 us)
Async XLA Ops:
  0.0 1.2 %copy-start = (f32[256,1024]{1,0:T(8,128)S(1)}, f32[256,1024]{1,0:T(8,128)}, u32[]{:S(2)}) copy-start(f32[256,1024]{1,0:T(8,128)} %param.7) | copy-start | bytes 3145732
  1.2 21.8 %collective-permute-start.2 = (f32[32,1024]{1,0:T(8,128)S(1)}, f32[32,1024]{1,0:T(8,128)S(1)}, u32[]{:S(2)}, u32[]{:S(2)}) collective-permute-start(f32[32,1024]{1,0:T(8,128)S(1)} %constant_dynamic-slice_fusion.share_ref), channel_id=1, source_target_pairs={{0,12},{4,8},{8,4},{12,0},{1,13},{5,9},{9,5},{13,1},{2,14},{6,10},... | collective-permute-start | bytes 393224 | tf_op jit(solution)/shard_map/ppermute | solution.py:251
  6.4 16.7 %collective-permute-start.1 = (f32[32,1024]{1,0:T(8,128)S(1)}, f32[32,1024]{1,0:T(8,128)}, u32[]{:S(2)}, u32[]{:S(2)}) collective-permute-start(f32[32,1024]{1,0:T(8,128)S(1)} %constant_dynamic-slice_fusion.share_ref), channel_id=1, source_target_pairs={{0,8},{4,12},{8,0},{12,4},{1,9},{5,13},{9,1},{13,5},{2,10},{6,14},... | collective-permute-start | bytes 393224 | tf_op jit(solution)/shard_map/ppermute | solution.py:251
  6.4 16.7 %collective-permute-start = (f32[32,1024]{1,0:T(8,128)S(1)}, f32[32,1024]{1,0:T(8,128)}, u32[]{:S(2)}, u32[]{:S(2)}) collective-permute-start(f32[32,1024]{1,0:T(8,128)S(1)} %constant_dynamic-slice_fusion.share_ref), channel_id=1, source_target_pairs={{0,4},{4,0},{8,12},{12,8},{1,5},{5,1},{9,13},{13,9},{2,6},{6,2},{1... | collective-permute-start | bytes 393224 | tf_op jit(solution)/shard_map/ppermute | solution.py:251
  7.0 1.6 %copy-start.4 = (f32[16384,32]{0,1:T(8,128)S(1)}, f32[16384,32]{0,1:T(8,128)}, u32[]{:S(2)}) copy-start(f32[16384,32]{0,1:T(8,128)} %param.4) | copy-start | bytes 6291460
  8.7 1.4 %copy-start.1 = (f32[8,32,2048]{2,1,0:T(8,128)}, f32[8,32,2048]{2,1,0:T(8,128)S(1)}, u32[]{:S(2)}) copy-start(f32[8,32,2048]{2,1,0:T(8,128)S(1)} %shard_map.46) | copy-start | bytes 6291460
  10.1 53.3 %all-to-all-start = ((f32[8,32,2048]{2,1,0:T(8,128)}), f32[8,32,2048]{2,1,0:T(8,128)S(1)}, u32[]{:S(2)}, u32[]{:S(2)}) async-start(f32[8,32,2048]{2,1,0:T(8,128)} %copy-done.1), calls=%async_computation | async-start | bytes 4194304 | tf_op jit(solution)/shard_map/all_to_all | solution.py:288
  20.9 21.8 %collective-permute-start.6 = (f32[512,1024]{1,0:T(8,128)}, f32[512,1024]{1,0:T(8,128)}, u32[]{:S(2)}, u32[]{:S(2)}) collective-permute-start(f32[512,1024]{1,0:T(8,128)} %get-tuple-element.65.own_ref), channel_id=1, source_target_pairs={{0,1},{1,0},{2,3},{3,2},{4,5},{5,4},{6,7},{7,6},{8,9},{9,8},{10,11... | collective-permute-start | bytes 6291464 | tf_op jit(solution)/shard_map/ppermute | solution.py:251
  20.9 21.8 %collective-permute-start.5 = (f32[512,1024]{1,0:T(8,128)}, f32[512,1024]{1,0:T(8,128)}, u32[]{:S(2)}, u32[]{:S(2)}) collective-permute-start(f32[512,1024]{1,0:T(8,128)} %get-tuple-element.66.own_ref), channel_id=1, source_target_pairs={{0,1},{1,0},{2,3},{3,2},{4,5},{5,4},{6,7},{7,6},{8,9},{9,8},{10,11... | collective-permute-start | bytes 6291464 | tf_op jit(solution)/shard_map/ppermute | solution.py:251
  21.5 0.9 copy-start.5
  24.1 15.4 %collective-permute-start.3 = (f32[4,32,512]{2,1,0:T(8,128)S(1)}, f32[4,32,512]{2,1,0:T(8,128)S(1)}, u32[]{:S(2)}, u32[]{:S(2)}) collective-permute-start(f32[4,32,512]{2,1,0:T(8,128)S(1)} %get-tuple-element.39.near_ref), channel_id=1, source_target_pairs={{0,2},{2,0},{1,3},{3,1},{4,6},{6,4},{5,7},{7,5},{8,10},{10,8},{9,1... | collective-permute-start | bytes 786440 | tf_op jit(solution)/shard_map/ppermute | solution.py:251
  26.2 13.3 %collective-permute-start.4 = (f32[4,32,512]{2,1,0:T(8,128)S(1)}, f32[4,32,512]{2,1,0:T(8,128)S(1)}, u32[]{:S(2)}, u32[]{:S(2)}) collective-permute-start(f32[4,32,512]{2,1,0:T(8,128)S(1)} %get-tuple-element.40.far_ref), channel_id=1, source_target_pairs={{0,16},{16,0},{1,17},{17,1},{2,18},{18,2},{3,19},{19,3},{4,20},{20... | collective-permute-start | bytes 786440 | tf_op jit(solution)/shard_map/ppermute | solution.py:251
  27.7 15.0 %collective-permute-start.7 = (f32[64,256]{1,0:T(8,128)S(1)}, f32[64,256]{1,0:T(8,128)S(1)}, u32[]{:S(2)}, u32[]{:S(2)}) collective-permute-start(f32[64,256]{1,0:T(8,128)S(1)} %get-tuple-element.42), channel_id=1, source_target_pairs={{0,1},{1,0},{2,3},{3,2},{4,5},{5,4},{6,7},{7,6},{8,9},{9,8},{10,11... | collective-permute-start | bytes 196616 | tf_op jit(solution)/shard_map/ppermute | solution.py:251
  40.1 18.2 %collective-permute-start.9 = (f32[2,4,32,512]{3,2,1,0:T(8,128)S(1)}, f32[2,4,32,512]{3,2,1,0:T(8,128)S(1)}, u32[]{:S(2)}, u32[]{:S(2)}) collective-permute-start(f32[2,4,32,512]{3,2,1,0:T(8,128)S(1)} %get-tuple-element.44.far_ref), channel_id=1, source_target_pairs={{0,2},{2,0},{1,3},{3,1},{4,6},{6,4},{5,7},{7,5},{8,10},{10,8},{9,1... | collective-permute-start | bytes 1572872 | tf_op jit(solution)/shard_map/ppermute | solution.py:251
  42.7 15.6 %collective-permute-start.8 = (f32[2,4,32,512]{3,2,1,0:T(8,128)S(1)}, f32[2,4,32,512]{3,2,1,0:T(8,128)S(1)}, u32[]{:S(2)}, u32[]{:S(2)}) collective-permute-start(f32[2,4,32,512]{3,2,1,0:T(8,128)S(1)} %get-tuple-element.43.near_ref), channel_id=1, source_target_pairs={{0,16},{16,0},{1,17},{17,1},{2,18},{18,2},{3,19},{19,3},{4,20},{20... | collective-permute-start | bytes 1572872 | tf_op jit(solution)/shard_map/ppermute | solution.py:251
  59.0 1.4 %copy-start.2 = (f32[4,2,2,32,1024]{4,3,2,1,0:T(8,128)}, f32[4,2,2,32,1024]{4,3,2,1,0:T(8,128)S(1)}, u32[]{:S(2)}) copy-start(f32[4,2,2,32,1024]{4,3,2,1,0:T(8,128)S(1)} %shard_map.50.own_ref) | copy-start | bytes 6291460
  63.4 4.3 %copy-start.3 = (f32[4,2,2,32,1024]{4,3,2,1,0:T(8,128)S(1)}, f32[4,2,2,32,1024]{4,3,2,1,0:T(8,128)}, u32[]{:S(2)}) copy-start(f32[4,2,2,32,1024]{4,3,2,1,0:T(8,128)} %copy-done.2) | copy-start | bytes 6291460
  67.7 6.3 %collective-permute-start.10 = (f32[4,2,2,32,1024]{4,3,2,1,0:T(8,128)S(1)}, f32[4,2,2,32,1024]{4,3,2,1,0:T(8,128)S(1)}, u32[]{:S(2)}, u32[]{:S(2)}) collective-permute-start(f32[4,2,2,32,1024]{4,3,2,1,0:T(8,128)S(1)} %copy-done.3), channel_id=1, source_target_pairs={{0,1},{1,0},{2,3},{3,2},{4,5},{5,4},{6,7},{7,6},{8,9},{9,8},{10,11... | collective-permute-start | bytes 6291464 | tf_op jit(solution)/shard_map/ppermute | solution.py:251
  67.8 12.0 %collective-permute-start.11 = (f32[128,512]{1,0:T(8,128)S(1)}, f32[128,512]{1,0:T(8,128)S(1)}, u32[]{:S(2)}, u32[]{:S(2)}) collective-permute-start(f32[128,512]{1,0:T(8,128)S(1)} %get-tuple-element.53), channel_id=1, source_target_pairs={{0,2},{2,0},{1,3},{3,1},{4,6},{6,4},{5,7},{7,5},{8,10},{10,8},{9,1... | collective-permute-start | bytes 786440 | tf_op jit(solution)/shard_map/ppermute | solution.py:251
  73.5 8.7 %collective-permute-start.12 = (f32[128,512]{1,0:T(8,128)S(1)}, f32[128,512]{1,0:T(8,128)S(1)}, u32[]{:S(2)}, u32[]{:S(2)}) collective-permute-start(f32[128,512]{1,0:T(8,128)S(1)} %get-tuple-element.58), channel_id=1, source_target_pairs={{0,2},{2,0},{1,3},{3,1},{4,6},{6,4},{5,7},{7,5},{8,10},{10,8},{9,1... | collective-permute-start | bytes 786440 | tf_op jit(solution)/shard_map/ppermute | solution.py:251
  85.6 13.0 %collective-permute-start.13 = (f32[128,256]{1,0:T(8,128)S(1)}, f32[128,256]{1,0:T(8,128)S(1)}, u32[]{:S(2)}, u32[]{:S(2)}) collective-permute-start(f32[128,256]{1,0:T(8,128)S(1)} %get-tuple-element.60), channel_id=1, source_target_pairs={{0,12},{4,8},{8,4},{12,0},{1,13},{5,9},{9,5},{13,1},{2,14},{6,10},... | collective-permute-start | bytes 393224 | tf_op jit(solution)/shard_map/ppermute | solution.py:251
  94.1 9.0 %collective-permute-start.14 = (f32[128,256]{1,0:T(8,128)S(1)}, f32[128,256]{1,0:T(8,128)S(1)}, u32[]{:S(2)}, u32[]{:S(2)}) collective-permute-start(f32[128,256]{1,0:T(8,128)S(1)} %get-tuple-element.61), channel_id=1, source_target_pairs={{0,8},{4,12},{8,0},{12,4},{1,9},{5,13},{9,1},{13,5},{2,10},{6,14},... | collective-permute-start | bytes 393224 | tf_op jit(solution)/shard_map/ppermute | solution.py:251
  94.1 9.0 %collective-permute-start.15 = (f32[128,256]{1,0:T(8,128)S(1)}, f32[128,256]{1,0:T(8,128)S(1)}, u32[]{:S(2)}, u32[]{:S(2)}) collective-permute-start(f32[128,256]{1,0:T(8,128)S(1)} %get-tuple-element.62), channel_id=1, source_target_pairs={{0,4},{4,0},{8,12},{12,8},{1,5},{5,1},{9,13},{13,9},{2,6},{6,2},{1... | collective-permute-start | bytes 393224 | tf_op jit(solution)/shard_map/ppermute | solution.py:251
  103.7 1.3 %collective-permute-start.16 = (f32[64,256]{1,0:T(8,128)S(1)}, f32[64,256]{1,0:T(8,128)S(1)}, u32[]{:S(2)}, u32[]{:S(2)}) collective-permute-start(f32[64,256]{1,0:T(8,128)S(1)} %get-tuple-element.64), channel_id=1, source_target_pairs={{0,1},{1,0},{2,3},{3,2},{4,5},{5,4},{6,7},{7,6},{8,9},{9,8},{10,11... | collective-permute-start | bytes 196616 | tf_op jit(solution)/shard_map/ppermute | solution.py:251

commit v5 on v4

--- a/solution.py
+++ b/solution.py
@@ -57,8 +57,12 @@
     *landed_refs, near_ref, far_ref = refs
     half = near_ref.shape[2]
     for step, ref in enumerate((share_ref, *landed_refs)):
-        near_ref[where_ref[0] ^ step] = ref[:, pl.ds(0, half)]
-        far_ref[where_ref[0] ^ step] = ref[:, pl.ds(half, half)]
+        source = where_ref[0] ^ step
+        near_ref[source] = ref[:, pl.ds(0, half)]
+
+        @pl.when(source >= 2)
+        def _(source=source, ref=ref):
+            far_ref[source - 2] = ref[:, pl.ds(half, half)]
 
 
 def first_kernel(where_ref, near_ref, near_other_ref, far_ref, far_other_ref, near_out, far_out):
@@ -76,8 +80,11 @@
         for i in range(2):
             out_ref[r, group, i, :, pl.ds(0, half)] = near_ref[i, r]
             out_ref[r, 1 - group, i, :, pl.ds(0, half)] = near_other_ref[i, r]
-            out_ref[r, i, side, :, pl.ds(half, half)] = far_ref[i, r]
-            out_ref[r, i, 1 - side, :, pl.ds(half, half)] = far_other_ref[i, r]
+            if r < 2:
+                out_ref[r, i, :, :, pl.ds(half, half)] = jnp.zeros((2, *near_ref.shape[2:]), jnp.float32)
+            else:
+                out_ref[r, i, side, :, pl.ds(half, half)] = far_ref[i, r - 2]
+                out_ref[r, i, 1 - side, :, pl.ds(half, half)] = far_other_ref[i, r - 2]
 
 
 def prepare_kernel(where_ref, own_ref, other_ref, ready_ref, factor_ref):
@@ -272,8 +279,9 @@
     others = [swap(panel, "core", 1) for panel in panels]
     landed, right_own = lax.optimization_barrier((landed, right_own))
     right_other = swap(right_other, "core", 1)
-    near, far = call(rows_kernel, [shape(4, share_rows, half_window)] * 2, scalars=1)(where, share, *landed)
-    near, far = call(first_kernel, [shape(2, 4, share_rows, half_window)] * 2, scalars=1)(
+    sizes = [shape(4, share_rows, half_window), shape(2, share_rows, half_window)]
+    near, far = call(rows_kernel, sizes, scalars=1)(where, share, *landed)
+    near, far = call(first_kernel, [shape(2, *size.shape) for size in sizes], scalars=1)(
         where, near, swap(near, "side", 1), far, swap(far, "groups", 1)
     )
     near, others, right_other = lax.optimization_barrier((near, others, right_other))

time: 107 us -> 102 us (0.953)
  starting transfers between devices: 31.5 us -> 27.2 us
    all_to_all x1, waiting for transfers between devices: 3.11 us -> 8.11 us  [shards(): lax.all_to_all(dealt[number], ('row', 'side'), split_axis=0, concat_axis=...]
    ppermute x17, waiting for transfers between devices: 35.6 us -> 30.7 us  [swap(): lax.ppermute(value, axis, [(i, i ^ step) for i in range(lax.axis_size(axi...]
    ppermute x17, starting transfers between devices: 25.5 us -> 21.3 us  [swap(): lax.ppermute(value, axis, [(i, i ^ step) for i in range(lax.axis_size(axi...]
  transfers between devices with their start and end apart: 18 -> 18, of which waited for: 7 -> 8; matrix products, arithmetic and copies ran while one was open for 5% -> 5% of each run, Pallas kernels for 14% -> 15%
where the time goes in v5:
time: 102 us
  waiting for transfers between devices  38.8 us (38%)
  starting transfers between devices  27.2 us (27%)
  Pallas kernels  24.6 us (24%)
  local copies, waits for them, and re-layouts  11.3 us (11%)
    ppermute x17, waiting for transfers between devices, swap(): lax.ppermute(value, axis, [(i, i ^ step) for i in range(lax.axis_size(axi...  30.7 us
    pallas_call x12, Pallas kernels, run(): pl.pallas_call(kernel, out_shape=outs, in_specs=[SMEM] * scalars + [VMEM]...  24.6 us
    ppermute x17, starting transfers between devices, swap(): lax.ppermute(value, axis, [(i, i ^ step) for i in range(lax.axis_size(axi...  21.3 us
    all_to_all x1, waiting for transfers between devices, shards(): lax.all_to_all(dealt[number], ('row', 'side'), split_axis=0, concat_axis=...  8.11 us
    unnamed x12, local copies, waits for them, and re-layouts  6.44 us
    all_to_all x1, starting transfers between devices, shards(): lax.all_to_all(dealt[number], ('row', 'side'), split_axis=0, concat_axis=...  5.95 us
    slice x1, local copies, waits for them, and re-layouts, shards(): panels = [factor_panel[:half_window], factor_panel[half_window:]]  4.82 us
  transfers between devices with their start and end apart: 18, of which 8 were waited for; matrix products, arithmetic and copies ran while one was open for 5% of the time, Pallas kernels for 15%

profile of v5, /device:TPU:0, one launch (start us, length us, event | category | flops | bytes accessed | tf_op | source)
XLA Modules:
  0.0 102.2 jit_solution(13741556428909745078)
XLA Ops:
  1.2 5.1 %collective-permute-start.2 = (f32[32,1024]{1,0:T(8,128)S(1)}, f32[32,1024]{1,0:T(8,128)S(1)}, u32[]{:S(2)}, u32[]{:S(2)}) collective-permute-start(f32[32,1024]{1,0:T(8,128)S(1)} %constant_dynamic-slice_fusion.share_ref), channel_id=1, source_target_pairs={{0,12},{4,8},{8,4},{12,0},{1,13},{5,9},{9,5},{13,1},{2,14},{6,10},... | collective-permute-start | bytes 393224 | tf_op jit(solution)/shard_map/ppermute | solution.py:258
  7.0 1.6 %copy-done.4 = f32[16384,32]{0,1:T(8,128)S(1)} copy-done((f32[16384,32]{0,1:T(8,128)S(1)}, f32[16384,32]{0,1:T(8,128)}, u32[]{:S(2)}) %copy-start.4) | copy-done | bytes 2097176
  8.7 1.4 %copy-done.1 = f32[8,32,2048]{2,1,0:T(8,128)} copy-done((f32[8,32,2048]{2,1,0:T(8,128)}, f32[8,32,2048]{2,1,0:T(8,128)S(1)}, u32[]{:S(2)}) %copy-start.1) | copy-done | bytes 2097176
  10.1 5.9 %all-to-all-start = ((f32[8,32,2048]{2,1,0:T(8,128)}), f32[8,32,2048]{2,1,0:T(8,128)S(1)}, u32[]{:S(2)}, u32[]{:S(2)}) async-start(f32[8,32,2048]{2,1,0:T(8,128)} %copy-done.1), calls=%async_computation | async-start | bytes 4194304 | tf_op jit(solution)/shard_map/all_to_all | solution.py:296
  16.0 4.8 %fusion = (f32[512,1024]{1,0:T(8,128)}, f32[512,1024]{1,0:T(8,128)}) fusion(f32[1024,1024]{1,0:T(8,128)} %param.5), kind=kLoop, calls=%fused_computation.2 | loop fusion | bytes 8388608 | tf_op jit(solution)/shard_map/slice | solution.py:278
  24.1 2.1 %collective-permute-start.3 = (f32[4,32,512]{2,1,0:T(8,128)S(1)}, f32[4,32,512]{2,1,0:T(8,128)S(1)}, u32[]{:S(2)}, u32[]{:S(2)}) collective-permute-start(f32[4,32,512]{2,1,0:T(8,128)S(1)} %get-tuple-element.39.near_ref), channel_id=1, source_target_pairs={{0,2},{2,0},{1,3},{3,1},{4,6},{6,4},{5,7},{7,5},{8,10},{10,8},{9,1... | collective-permute-start | bytes 786440 | tf_op jit(solution)/shard_map/ppermute | solution.py:258
  26.2 1.5 %collective-permute-start.4 = (f32[2,32,512]{2,1,0:T(8,128)S(1)}, f32[2,32,512]{2,1,0:T(8,128)S(1)}, u32[]{:S(2)}, u32[]{:S(2)}) collective-permute-start(f32[2,32,512]{2,1,0:T(8,128)S(1)} %get-tuple-element.40.far_ref), channel_id=1, source_target_pairs={{0,16},{16,0},{1,17},{17,1},{2,18},{18,2},{3,19},{19,3},{4,20},{20... | collective-permute-start | bytes 393224 | tf_op jit(solution)/shard_map/ppermute | solution.py:258
  27.7 3.6 %collective-permute-done.4.far_other_ref = f32[2,32,512]{2,1,0:T(8,128)S(1)} collective-permute-done((f32[2,32,512]{2,1,0:T(8,128)S(1)}, f32[2,32,512]{2,1,0:T(8,128)S(1)}, u32[]{:S(2)}, u32[]{:S(2)}) %collective-permute-start.4) | collective-permute-done | bytes 131104 | tf_op jit(solution)/shard_map/ppermute | solution.py:258
  31.3 8.2 %collective-permute-done.3.near_other_ref = f32[4,32,512]{2,1,0:T(8,128)S(1)} collective-permute-done((f32[4,32,512]{2,1,0:T(8,128)S(1)}, f32[4,32,512]{2,1,0:T(8,128)S(1)}, u32[]{:S(2)}, u32[]{:S(2)}) %collective-permute-start.3) | collective-permute-done | bytes 262176 | tf_op jit(solution)/shard_map/ppermute | solution.py:258
  40.1 1.6 %collective-permute-start.8 = (f32[2,4,32,512]{3,2,1,0:T(8,128)S(1)}, f32[2,4,32,512]{3,2,1,0:T(8,128)S(1)}, u32[]{:S(2)}, u32[]{:S(2)}) collective-permute-start(f32[2,4,32,512]{3,2,1,0:T(8,128)S(1)} %get-tuple-element.43.near_ref), channel_id=1, source_target_pairs={{0,16},{16,0},{1,17},{17,1},{2,18},{18,2},{3,19},{19,3},{4,20},{20... | collective-permute-start | bytes 1572872 | tf_op jit(solution)/shard_map/ppermute | solution.py:258
  41.7 2.5 %collective-permute-start.9 = (f32[2,2,32,512]{3,2,1,0:T(8,128)S(1)}, f32[2,2,32,512]{3,2,1,0:T(8,128)S(1)}, u32[]{:S(2)}, u32[]{:S(2)}) collective-permute-start(f32[2,2,32,512]{3,2,1,0:T(8,128)S(1)} %get-tuple-element.44.far_ref), channel_id=1, source_target_pairs={{0,2},{2,0},{1,3},{3,1},{4,6},{6,4},{5,7},{7,5},{8,10},{10,8},{9,1... | collective-permute-start | bytes 786440 | tf_op jit(solution)/shard_map/ppermute | solution.py:258
  44.2 9.1 %collective-permute-done.9.far_other_ref = f32[2,2,32,512]{3,2,1,0:T(8,128)S(1)} collective-permute-done((f32[2,2,32,512]{3,2,1,0:T(8,128)S(1)}, f32[2,2,32,512]{3,2,1,0:T(8,128)S(1)}, u32[]{:S(2)}, u32[]{:S(2)}) %collective-permute-start.9) | collective-permute-done | bytes 262176 | tf_op jit(solution)/shard_map/ppermute | solution.py:258
  54.0 1.4 %copy-done.2 = f32[4,2,2,32,1024]{4,3,2,1,0:T(8,128)} copy-done((f32[4,2,2,32,1024]{4,3,2,1,0:T(8,128)}, f32[4,2,2,32,1024]{4,3,2,1,0:T(8,128)S(1)}, u32[]{:S(2)}) %copy-start.2) | copy-done | bytes 2097176
  55.3 8.1 %all-to-all-done = f32[8,32,2048]{2,1,0:T(8,128)S(1)} async-done(((f32[8,32,2048]{2,1,0:T(8,128)}), f32[8,32,2048]{2,1,0:T(8,128)S(1)}, u32[]{:S(2)}, u32[]{:S(2)}) %all-to-all-start) | async-done | bytes 2097184 | tf_op jit(solution)/shard_map/all_to_all | solution.py:296
  63.4 4.3 %shard_map.51 = (f32[128,512]{1,0:T(8,128)S(1)}, f32[128,512]{1,0:T(8,128)S(1)}, bf16[256,2048]{1,0:T(8,128)(2,1)S(1)}, bf16[256,2048]{1,0:T(8,128)(2,1)S(1)}) custom-call(s32[4]{0:T(128)S(1)} %pad_add_fusion.where_ref, f32[256,2048]{1,0:T(8,128)S(1)} %bitcast.6, f32[512,1024]{1,0:T(8,128)} %get-tuple-element.66.own_ref, ...), custom_call_target="tpu_custom_call" | custom-call | flops 1000000 | bytes 6291472 | tf_op jit(solution)/shard_map/pallas_call | solution.py:39
  67.8 1.5 %collective-permute-start.11 = (f32[128,512]{1,0:T(8,128)S(1)}, f32[128,512]{1,0:T(8,128)S(1)}, u32[]{:S(2)}, u32[]{:S(2)}) collective-permute-start(f32[128,512]{1,0:T(8,128)S(1)} %get-tuple-element.53), channel_id=1, source_target_pairs={{0,2},{2,0},{1,3},{3,1},{4,6},{6,4},{5,7},{7,5},{8,10},{10,8},{9,1... | collective-permute-start | bytes 786440 | tf_op jit(solution)/shard_map/ppermute | solution.py:258
  69.3 4.1 %shard_map.54 = (f32[128,512]{1,0:T(8,128)S(1)}, f32[128,512]{1,0:T(8,128)S(1)}) custom-call(bf16[256,2048]{1,0:T(8,128)(2,1)S(1)} %get-tuple-element.54.high_ref, bf16[256,2048]{1,0:T(8,128)(2,1)S(1)} %get-tuple-element.55.low_ref, f32[512,1024]{1,0:T(8,128)} %get-tuple-element.65.own_ref, f32[512,1024]{1,0:T(8,128)} %collective-permute-done.6.other_ref), custom_call_target="tpu_custom_call" | custom-call | flops 1000000 | bytes 6291456 | tf_op jit(solution)/shard_map/pallas_call | solution.py:39
  74.0 5.8 %shard_map.52.ready_ref = f32[1024,1024]{1,0:T(8,128)S(1)} custom-call(s32[4]{0:T(128)S(1)} %pad_add_fusion.where_ref, f32[4,2,2,32,1024]{4,3,2,1,0:T(8,128)S(1)} %copy-done.3, f32[4,2,2,32,1024]{4,3,2,1,0:T(8,128)S(1)} %collective-permute-done.10.other_ref), custom_call_target="tpu_custom_call" | custom-call | flops 1000000 | bytes 4194320 | tf_op jit(solution)/shard_map/pallas_call | solution.py:39
  79.9 2.1 %shard_map.53.solved_ref = f32[128,512]{1,0:T(8,128)S(1)} custom-call(s32[4]{0:T(128)S(1)} %pad_add_fusion.where_ref, f32[1024,1024]{1,0:T(8,128)S(1)} %shard_map.52.ready_ref, f32[64,256]{1,0:T(8,128)S(1)} %get-tuple-element.50.right_own_ref, f32[64,256]{1,0:T(8,128)S(1)} %collective-permute-done.7.right_other_ref, ...), custom_call_target="tpu_custom_call" | custom-call | flops 1000000 | bytes 4849680 | tf_op jit(solution)/shard_map/pallas_call | solution.py:39
  82.2 3.4 %shard_map.55 = (f32[128,256]{1,0:T(8,128)S(1)}, f32[128,256]{1,0:T(8,128)S(1)}, f32[128,256]{1,0:T(8,128)S(1)}, f32[128,256]{1,0:T(8,128)S(1)}) custom-call(s32[4]{0:T(128)S(1)} %pad_add_fusion.where_ref, f32[1024,1024]{1,0:T(8,128)S(1)} %shard_map.52.ready_ref, f32[64,256]{1,0:T(8,128)S(1)} %get-tuple-element.50.right_own_ref, ...), custom_call_target="tpu_custom_call" | custom-call | flops 1000000 | bytes 5111824 | tf_op jit(solution)/shard_map/pallas_call | solution.py:39
  85.6 4.4 %collective-permute-start.13 = (f32[128,256]{1,0:T(8,128)S(1)}, f32[128,256]{1,0:T(8,128)S(1)}, u32[]{:S(2)}, u32[]{:S(2)}) collective-permute-start(f32[128,256]{1,0:T(8,128)S(1)} %get-tuple-element.60), channel_id=1, source_target_pairs={{0,12},{4,8},{8,4},{12,0},{1,13},{5,9},{9,5},{13,1},{2,14},{6,10},... | collective-permute-start | bytes 393224 | tf_op jit(solution)/shard_map/ppermute | solution.py:258
  90.6 3.8 %collective-permute-done.13.refs_1_ = f32[128,256]{1,0:T(8,128)S(1)} collective-permute-done((f32[128,256]{1,0:T(8,128)S(1)}, f32[128,256]{1,0:T(8,128)S(1)}, u32[]{:S(2)}, u32[]{:S(2)}) %collective-permute-start.13) | collective-permute-done | bytes 131104 | tf_op jit(solution)/shard_map/ppermute | solution.py:258
  94.4 4.6 %collective-permute-done.14.refs_2_ = f32[128,256]{1,0:T(8,128)S(1)} collective-permute-done((f32[128,256]{1,0:T(8,128)S(1)}, f32[128,256]{1,0:T(8,128)S(1)}, u32[]{:S(2)}, u32[]{:S(2)}) %collective-permute-start.14) | collective-permute-done | bytes 131104 | tf_op jit(solution)/shard_map/ppermute | solution.py:258
  100.9 1.3 %shard_map.57 = f32[256,128]{1,0:T(8,128)} custom-call(s32[4]{0:T(128)S(1)} %pad_add_fusion.where_ref, f32[64,256]{1,0:T(8,128)S(1)} %get-tuple-element.63.refs_0_, f32[64,256]{1,0:T(8,128)S(1)} %collective-permute-done.16.refs_1_), custom_call_target="tpu_custom_call" | custom-call | flops 1000000 | bytes 131088 | tf_op jit(solution)/shard_map/pallas_call | solution.py:39
  (39 shorter events, 9.9 us)
Async XLA Ops:
  0.0 1.2 %copy-start = (f32[256,1024]{1,0:T(8,128)S(1)}, f32[256,1024]{1,0:T(8,128)}, u32[]{:S(2)}) copy-start(f32[256,1024]{1,0:T(8,128)} %param.7) | copy-start | bytes 3145732
  1.2 21.8 %collective-permute-start.2 = (f32[32,1024]{1,0:T(8,128)S(1)}, f32[32,1024]{1,0:T(8,128)S(1)}, u32[]{:S(2)}, u32[]{:S(2)}) collective-permute-start(f32[32,1024]{1,0:T(8,128)S(1)} %constant_dynamic-slice_fusion.share_ref), channel_id=1, source_target_pairs={{0,12},{4,8},{8,4},{12,0},{1,13},{5,9},{9,5},{13,1},{2,14},{6,10},... | collective-permute-start | bytes 393224 | tf_op jit(solution)/shard_map/ppermute | solution.py:258
  6.4 16.7 %collective-permute-start.1 = (f32[32,1024]{1,0:T(8,128)S(1)}, f32[32,1024]{1,0:T(8,128)}, u32[]{:S(2)}, u32[]{:S(2)}) collective-permute-start(f32[32,1024]{1,0:T(8,128)S(1)} %constant_dynamic-slice_fusion.share_ref), channel_id=1, source_target_pairs={{0,8},{4,12},{8,0},{12,4},{1,9},{5,13},{9,1},{13,5},{2,10},{6,14},... | collective-permute-start | bytes 393224 | tf_op jit(solution)/shard_map/ppermute | solution.py:258
  6.4 16.7 %collective-permute-start = (f32[32,1024]{1,0:T(8,128)S(1)}, f32[32,1024]{1,0:T(8,128)}, u32[]{:S(2)}, u32[]{:S(2)}) collective-permute-start(f32[32,1024]{1,0:T(8,128)S(1)} %constant_dynamic-slice_fusion.share_ref), channel_id=1, source_target_pairs={{0,4},{4,0},{8,12},{12,8},{1,5},{5,1},{9,13},{13,9},{2,6},{6,2},{1... | collective-permute-start | bytes 393224 | tf_op jit(solution)/shard_map/ppermute | solution.py:258
  7.0 1.6 %copy-start.4 = (f32[16384,32]{0,1:T(8,128)S(1)}, f32[16384,32]{0,1:T(8,128)}, u32[]{:S(2)}) copy-start(f32[16384,32]{0,1:T(8,128)} %param.4) | copy-start | bytes 6291460
  8.7 1.4 %copy-start.1 = (f32[8,32,2048]{2,1,0:T(8,128)}, f32[8,32,2048]{2,1,0:T(8,128)S(1)}, u32[]{:S(2)}) copy-start(f32[8,32,2048]{2,1,0:T(8,128)S(1)} %shard_map.46) | copy-start | bytes 6291460
  10.1 53.3 %all-to-all-start = ((f32[8,32,2048]{2,1,0:T(8,128)}), f32[8,32,2048]{2,1,0:T(8,128)S(1)}, u32[]{:S(2)}, u32[]{:S(2)}) async-start(f32[8,32,2048]{2,1,0:T(8,128)} %copy-done.1), calls=%async_computation | async-start | bytes 4194304 | tf_op jit(solution)/shard_map/all_to_all | solution.py:296
  20.9 19.2 %collective-permute-start.6 = (f32[512,1024]{1,0:T(8,128)}, f32[512,1024]{1,0:T(8,128)}, u32[]{:S(2)}, u32[]{:S(2)}) collective-permute-start(f32[512,1024]{1,0:T(8,128)} %get-tuple-element.65.own_ref), channel_id=1, source_target_pairs={{0,1},{1,0},{2,3},{3,2},{4,5},{5,4},{6,7},{7,6},{8,9},{9,8},{10,11... | collective-permute-start | bytes 6291464 | tf_op jit(solution)/shard_map/ppermute | solution.py:258
  20.9 19.3 %collective-permute-start.5 = (f32[512,1024]{1,0:T(8,128)}, f32[512,1024]{1,0:T(8,128)}, u32[]{:S(2)}, u32[]{:S(2)}) collective-permute-start(f32[512,1024]{1,0:T(8,128)} %get-tuple-element.66.own_ref), channel_id=1, source_target_pairs={{0,1},{1,0},{2,3},{3,2},{4,5},{5,4},{6,7},{7,6},{8,9},{9,8},{10,11... | collective-permute-start | bytes 6291464 | tf_op jit(solution)/shard_map/ppermute | solution.py:258
  21.5 0.9 copy-start.5
  24.1 15.4 %collective-permute-start.3 = (f32[4,32,512]{2,1,0:T(8,128)S(1)}, f32[4,32,512]{2,1,0:T(8,128)S(1)}, u32[]{:S(2)}, u32[]{:S(2)}) collective-permute-start(f32[4,32,512]{2,1,0:T(8,128)S(1)} %get-tuple-element.39.near_ref), channel_id=1, source_target_pairs={{0,2},{2,0},{1,3},{3,1},{4,6},{6,4},{5,7},{7,5},{8,10},{10,8},{9,1... | collective-permute-start | bytes 786440 | tf_op jit(solution)/shard_map/ppermute | solution.py:258
  26.2 5.1 %collective-permute-start.4 = (f32[2,32,512]{2,1,0:T(8,128)S(1)}, f32[2,32,512]{2,1,0:T(8,128)S(1)}, u32[]{:S(2)}, u32[]{:S(2)}) collective-permute-start(f32[2,32,512]{2,1,0:T(8,128)S(1)} %get-tuple-element.40.far_ref), channel_id=1, source_target_pairs={{0,16},{16,0},{1,17},{17,1},{2,18},{18,2},{3,19},{19,3},{4,20},{20... | collective-permute-start | bytes 393224 | tf_op jit(solution)/shard_map/ppermute | solution.py:258
  27.7 12.4 %collective-permute-start.7 = (f32[64,256]{1,0:T(8,128)S(1)}, f32[64,256]{1,0:T(8,128)S(1)}, u32[]{:S(2)}, u32[]{:S(2)}) collective-permute-start(f32[64,256]{1,0:T(8,128)S(1)} %get-tuple-element.42), channel_id=1, source_target_pairs={{0,1},{1,0},{2,3},{3,2},{4,5},{5,4},{6,7},{7,6},{8,9},{9,8},{10,11... | collective-permute-start | bytes 196616 | tf_op jit(solution)/shard_map/ppermute | solution.py:258
  40.1 13.2 %collective-permute-start.8 = (f32[2,4,32,512]{3,2,1,0:T(8,128)S(1)}, f32[2,4,32,512]{3,2,1,0:T(8,128)S(1)}, u32[]{:S(2)}, u32[]{:S(2)}) collective-permute-start(f32[2,4,32,512]{3,2,1,0:T(8,128)S(1)} %get-tuple-element.43.near_ref), channel_id=1, source_target_pairs={{0,16},{16,0},{1,17},{17,1},{2,18},{18,2},{3,19},{19,3},{4,20},{20... | collective-permute-start | bytes 1572872 | tf_op jit(solution)/shard_map/ppermute | solution.py:258
  41.7 11.6 %collective-permute-start.9 = (f32[2,2,32,512]{3,2,1,0:T(8,128)S(1)}, f32[2,2,32,512]{3,2,1,0:T(8,128)S(1)}, u32[]{:S(2)}, u32[]{:S(2)}) collective-permute-start(f32[2,2,32,512]{3,2,1,0:T(8,128)S(1)} %get-tuple-element.44.far_ref), channel_id=1, source_target_pairs={{0,2},{2,0},{1,3},{3,1},{4,6},{6,4},{5,7},{7,5},{8,10},{10,8},{9,1... | collective-permute-start | bytes 786440 | tf_op jit(solution)/shard_map/ppermute | solution.py:258
  54.0 1.4 %copy-start.2 = (f32[4,2,2,32,1024]{4,3,2,1,0:T(8,128)}, f32[4,2,2,32,1024]{4,3,2,1,0:T(8,128)S(1)}, u32[]{:S(2)}) copy-start(f32[4,2,2,32,1024]{4,3,2,1,0:T(8,128)S(1)} %shard_map.50.own_ref) | copy-start | bytes 6291460
  63.4 4.3 %copy-start.3 = (f32[4,2,2,32,1024]{4,3,2,1,0:T(8,128)S(1)}, f32[4,2,2,32,1024]{4,3,2,1,0:T(8,128)}, u32[]{:S(2)}) copy-start(f32[4,2,2,32,1024]{4,3,2,1,0:T(8,128)} %copy-done.2) | copy-start | bytes 6291460
  67.7 6.3 %collective-permute-start.10 = (f32[4,2,2,32,1024]{4,3,2,1,0:T(8,128)S(1)}, f32[4,2,2,32,1024]{4,3,2,1,0:T(8,128)S(1)}, u32[]{:S(2)}, u32[]{:S(2)}) collective-permute-start(f32[4,2,2,32,1024]{4,3,2,1,0:T(8,128)S(1)} %copy-done.3), channel_id=1, source_target_pairs={{0,1},{1,0},{2,3},{3,2},{4,5},{5,4},{6,7},{7,6},{8,9},{9,8},{10,11... | collective-permute-start | bytes 6291464 | tf_op jit(solution)/shard_map/ppermute | solution.py:258
  67.8 12.0 %collective-permute-start.11 = (f32[128,512]{1,0:T(8,128)S(1)}, f32[128,512]{1,0:T(8,128)S(1)}, u32[]{:S(2)}, u32[]{:S(2)}) collective-permute-start(f32[128,512]{1,0:T(8,128)S(1)} %get-tuple-element.53), channel_id=1, source_target_pairs={{0,2},{2,0},{1,3},{3,1},{4,6},{6,4},{5,7},{7,5},{8,10},{10,8},{9,1... | collective-permute-start | bytes 786440 | tf_op jit(solution)/shard_map/ppermute | solution.py:258
  73.4 8.7 %collective-permute-start.12 = (f32[128,512]{1,0:T(8,128)S(1)}, f32[128,512]{1,0:T(8,128)S(1)}, u32[]{:S(2)}, u32[]{:S(2)}) collective-permute-start(f32[128,512]{1,0:T(8,128)S(1)} %get-tuple-element.58), channel_id=1, source_target_pairs={{0,2},{2,0},{1,3},{3,1},{4,6},{6,4},{5,7},{7,5},{8,10},{10,8},{9,1... | collective-permute-start | bytes 786440 | tf_op jit(solution)/shard_map/ppermute | solution.py:258
  85.6 8.8 %collective-permute-start.13 = (f32[128,256]{1,0:T(8,128)S(1)}, f32[128,256]{1,0:T(8,128)S(1)}, u32[]{:S(2)}, u32[]{:S(2)}) collective-permute-start(f32[128,256]{1,0:T(8,128)S(1)} %get-tuple-element.60), channel_id=1, source_target_pairs={{0,12},{4,8},{8,4},{12,0},{1,13},{5,9},{9,5},{13,1},{2,14},{6,10},... | collective-permute-start | bytes 393224 | tf_op jit(solution)/shard_map/ppermute | solution.py:258
  90.0 9.0 %collective-permute-start.14 = (f32[128,256]{1,0:T(8,128)S(1)}, f32[128,256]{1,0:T(8,128)S(1)}, u32[]{:S(2)}, u32[]{:S(2)}) collective-permute-start(f32[128,256]{1,0:T(8,128)S(1)} %get-tuple-element.61), channel_id=1, source_target_pairs={{0,8},{4,12},{8,0},{12,4},{1,9},{5,13},{9,1},{13,5},{2,10},{6,14},... | collective-permute-start | bytes 393224 | tf_op jit(solution)/shard_map/ppermute | solution.py:258
  90.0 9.0 %collective-permute-start.15 = (f32[128,256]{1,0:T(8,128)S(1)}, f32[128,256]{1,0:T(8,128)S(1)}, u32[]{:S(2)}, u32[]{:S(2)}) collective-permute-start(f32[128,256]{1,0:T(8,128)S(1)} %get-tuple-element.62), channel_id=1, source_target_pairs={{0,4},{4,0},{8,12},{12,8},{1,5},{5,1},{9,13},{13,9},{2,6},{6,2},{1... | collective-permute-start | bytes 393224 | tf_op jit(solution)/shard_map/ppermute | solution.py:258
  99.6 1.3 %collective-permute-start.16 = (f32[64,256]{1,0:T(8,128)S(1)}, f32[64,256]{1,0:T(8,128)S(1)}, u32[]{:S(2)}, u32[]{:S(2)}) collective-permute-start(f32[64,256]{1,0:T(8,128)S(1)} %get-tuple-element.64), channel_id=1, source_target_pairs={{0,1},{1,0},{2,3},{3,2},{4,5},{5,4},{6,7},{7,6},{8,9},{9,8},{10,11... | collective-permute-start | bytes 196616 | tf_op jit(solution)/shard_map/ppermute | solution.py:258

commit v6 on v4

--- a/solution.py
+++ b/solution.py
@@ -55,10 +55,15 @@
 
 def rows_kernel(where_ref, share_ref, *refs):
     *landed_refs, near_ref, far_ref = refs
-    half = near_ref.shape[2]
+    width = near_ref.shape[2]
     for step, ref in enumerate((share_ref, *landed_refs)):
-        near_ref[where_ref[0] ^ step] = ref[:, pl.ds(0, half)]
-        far_ref[where_ref[0] ^ step] = ref[:, pl.ds(half, half)]
+        source = where_ref[0] ^ step
+        near_ref[source] = ref[:, pl.ds(0, width)]
+        for quarter, out_ref, first in ((1, near_ref, 3), (2, far_ref, -2), (3, far_ref, -1)):
+
+            @pl.when(source >= quarter)
+            def _(source=source, ref=ref, quarter=quarter, out_ref=out_ref, first=first):
+                out_ref[source + first] = ref[:, pl.ds(quarter * width, width)]
 
 
 def first_kernel(where_ref, near_ref, near_other_ref, far_ref, far_other_ref, near_out, far_out):
@@ -71,13 +76,20 @@
 
 def second_kernel(where_ref, near_ref, near_other_ref, far_ref, far_other_ref, out_ref):
     row, group, side, core = (where_ref[i] for i in range(4))
-    half = near_ref.shape[3]
+    width = near_ref.shape[3]
+    zero = jnp.zeros(near_ref.shape[2:], jnp.float32)
     for r in range(4):
         for i in range(2):
-            out_ref[r, group, i, :, pl.ds(0, half)] = near_ref[i, r]
-            out_ref[r, 1 - group, i, :, pl.ds(0, half)] = near_other_ref[i, r]
-            out_ref[r, i, side, :, pl.ds(half, half)] = far_ref[i, r]
-            out_ref[r, i, 1 - side, :, pl.ds(half, half)] = far_other_ref[i, r]
+            for quarter, first in enumerate((0, 3, -2, -1)):
+                cols = pl.ds(quarter * width, width)
+                if quarter < 2:
+                    here, other = out_ref.at[r, group, i, :, cols], out_ref.at[r, 1 - group, i, :, cols]
+                    refs = near_ref, near_other_ref
+                else:
+                    here, other = out_ref.at[r, i, side, :, cols], out_ref.at[r, i, 1 - side, :, cols]
+                    refs = far_ref, far_other_ref
+                here[...] = refs[0][i, r + first] if r >= quarter else zero
+                other[...] = refs[1][i, r + first] if r >= quarter else zero
 
 
 def prepare_kernel(where_ref, own_ref, other_ref, ready_ref, factor_ref):
@@ -272,8 +284,9 @@
     others = [swap(panel, "core", 1) for panel in panels]
     landed, right_own = lax.optimization_barrier((landed, right_own))
     right_other = swap(right_other, "core", 1)
-    near, far = call(rows_kernel, [shape(4, share_rows, half_window)] * 2, scalars=1)(where, share, *landed)
-    near, far = call(first_kernel, [shape(2, 4, share_rows, half_window)] * 2, scalars=1)(
+    sizes = [shape(7, share_rows, strip_rows), shape(3, share_rows, strip_rows)]
+    near, far = call(rows_kernel, sizes, scalars=1)(where, share, *landed)
+    near, far = call(first_kernel, [shape(2, *size.shape) for size in sizes], scalars=1)(
         where, near, swap(near, "side", 1), far, swap(far, "groups", 1)
     )
     near, others, right_other = lax.optimization_barrier((near, others, right_other))

time: 107 us -> 102 us (0.953)
  starting transfers between devices: 31.5 us -> 26.6 us
    ppermute x17, waiting for transfers between devices: 35.6 us -> 28.7 us  [swap(): lax.ppermute(value, axis, [(i, i ^ step) for i in range(lax.axis_size(axi...]
    all_to_all x1, waiting for transfers between devices: 3.11 us -> 9.92 us  [shards(): lax.all_to_all(dealt[number], ('row', 'side'), split_axis=0, concat_axis=...]
    ppermute x17, starting transfers between devices: 25.5 us -> 20.7 us  [swap(): lax.ppermute(value, axis, [(i, i ^ step) for i in range(lax.axis_size(axi...]
  transfers between devices with their start and end apart: 18 -> 18, of which waited for: 7 -> 8; matrix products, arithmetic and copies ran while one was open for 5% -> 5% of each run, Pallas kernels for 14% -> 15%
where the time goes in v6:
time: 102 us; the launch traced here: 101 us
  waiting for transfers between devices  38.6 us (38%)
  starting transfers between devices  26.6 us (26%)
  Pallas kernels  24.6 us (24%)
  local copies, waits for them, and re-layouts  11.3 us (11%)
    ppermute x17, waiting for transfers between devices, swap(): lax.ppermute(value, axis, [(i, i ^ step) for i in range(lax.axis_size(axi...  28.7 us
    pallas_call x12, Pallas kernels, run(): pl.pallas_call(kernel, out_shape=outs, in_specs=[SMEM] * scalars + [VMEM]...  24.6 us
    ppermute x17, starting transfers between devices, swap(): lax.ppermute(value, axis, [(i, i ^ step) for i in range(lax.axis_size(axi...  20.7 us
    all_to_all x1, waiting for transfers between devices, shards(): lax.all_to_all(dealt[number], ('row', 'side'), split_axis=0, concat_axis=...  9.92 us
    unnamed x12, local copies, waits for them, and re-layouts  6.44 us
    all_to_all x1, starting transfers between devices, shards(): lax.all_to_all(dealt[number], ('row', 'side'), split_axis=0, concat_axis=...  5.95 us
    slice x1, local copies, waits for them, and re-layouts, shards(): panels = [factor_panel[:half_window], factor_panel[half_window:]]  4.82 us
  transfers between devices with their start and end apart: 18, of which 8 were waited for; matrix products, arithmetic and copies ran while one was open for 5% of the time, Pallas kernels for 15%

profile of v6, /device:TPU:0, one launch (start us, length us, event | category | flops | bytes accessed | tf_op | source)
XLA Modules:
  0.0 101.4 jit_solution(5552809513188918076)
XLA Ops:
  1.2 5.1 %collective-permute-start.2 = (f32[32,1024]{1,0:T(8,128)S(1)}, f32[32,1024]{1,0:T(8,128)S(1)}, u32[]{:S(2)}, u32[]{:S(2)}) collective-permute-start(f32[32,1024]{1,0:T(8,128)S(1)} %constant_dynamic-slice_fusion.share_ref), channel_id=1, source_target_pairs={{0,12},{4,8},{8,4},{12,0},{1,13},{5,9},{9,5},{13,1},{2,14},{6,10},... | collective-permute-start | bytes 393224 | tf_op jit(solution)/shard_map/ppermute | solution.py:263
  7.0 1.6 %copy-done.4 = f32[16384,32]{0,1:T(8,128)S(1)} copy-done((f32[16384,32]{0,1:T(8,128)S(1)}, f32[16384,32]{0,1:T(8,128)}, u32[]{:S(2)}) %copy-start.4) | copy-done | bytes 2097176
  8.7 1.4 %copy-done.1 = f32[8,32,2048]{2,1,0:T(8,128)} copy-done((f32[8,32,2048]{2,1,0:T(8,128)}, f32[8,32,2048]{2,1,0:T(8,128)S(1)}, u32[]{:S(2)}) %copy-start.1) | copy-done | bytes 2097176
  10.1 5.9 %all-to-all-start = ((f32[8,32,2048]{2,1,0:T(8,128)}), f32[8,32,2048]{2,1,0:T(8,128)S(1)}, u32[]{:S(2)}, u32[]{:S(2)}) async-start(f32[8,32,2048]{2,1,0:T(8,128)} %copy-done.1), calls=%async_computation | async-start | bytes 4194304 | tf_op jit(solution)/shard_map/all_to_all | solution.py:301
  16.0 4.8 %fusion = (f32[512,1024]{1,0:T(8,128)}, f32[512,1024]{1,0:T(8,128)}) fusion(f32[1024,1024]{1,0:T(8,128)} %param.5), kind=kLoop, calls=%fused_computation.2 | loop fusion | bytes 8388608 | tf_op jit(solution)/shard_map/slice | solution.py:283
  24.1 2.1 %collective-permute-start.3 = (f32[7,32,256]{2,1,0:T(8,128)S(1)}, f32[7,32,256]{2,1,0:T(8,128)S(1)}, u32[]{:S(2)}, u32[]{:S(2)}) collective-permute-start(f32[7,32,256]{2,1,0:T(8,128)S(1)} %get-tuple-element.39.near_ref), channel_id=1, source_target_pairs={{0,2},{2,0},{1,3},{3,1},{4,6},{6,4},{5,7},{7,5},{8,10},{10,8},{9,1... | collective-permute-start | bytes 688136 | tf_op jit(solution)/shard_map/ppermute | solution.py:263
  26.2 1.5 %collective-permute-start.4 = (f32[3,32,256]{2,1,0:T(8,128)S(1)}, f32[3,32,256]{2,1,0:T(8,128)S(1)}, u32[]{:S(2)}, u32[]{:S(2)}) collective-permute-start(f32[3,32,256]{2,1,0:T(8,128)S(1)} %get-tuple-element.40.far_ref), channel_id=1, source_target_pairs={{0,16},{16,0},{1,17},{17,1},{2,18},{18,2},{3,19},{19,3},{4,20},{20... | collective-permute-start | bytes 294920 | tf_op jit(solution)/shard_map/ppermute | solution.py:263
  27.7 3.1 %collective-permute-done.4.far_other_ref = f32[3,32,256]{2,1,0:T(8,128)S(1)} collective-permute-done((f32[3,32,256]{2,1,0:T(8,128)S(1)}, f32[3,32,256]{2,1,0:T(8,128)S(1)}, u32[]{:S(2)}, u32[]{:S(2)}) %collective-permute-start.4) | collective-permute-done | bytes 98336 | tf_op jit(solution)/shard_map/ppermute | solution.py:263
  30.8 8.0 %collective-permute-done.3.near_other_ref = f32[7,32,256]{2,1,0:T(8,128)S(1)} collective-permute-done((f32[7,32,256]{2,1,0:T(8,128)S(1)}, f32[7,32,256]{2,1,0:T(8,128)S(1)}, u32[]{:S(2)}, u32[]{:S(2)}) %collective-permute-start.3) | collective-permute-done | bytes 229408 | tf_op jit(solution)/shard_map/ppermute | solution.py:263
  39.4 1.6 %collective-permute-start.8 = (f32[2,7,32,256]{3,2,1,0:T(8,128)S(1)}, f32[2,7,32,256]{3,2,1,0:T(8,128)S(1)}, u32[]{:S(2)}, u32[]{:S(2)}) collective-permute-start(f32[2,7,32,256]{3,2,1,0:T(8,128)S(1)} %get-tuple-element.43.near_ref), channel_id=1, source_target_pairs={{0,16},{16,0},{1,17},{17,1},{2,18},{18,2},{3,19},{19,3},{4,20},{20... | collective-permute-start | bytes 1376264 | tf_op jit(solution)/shard_map/ppermute | solution.py:263
  41.0 2.5 %collective-permute-start.9 = (f32[2,3,32,256]{3,2,1,0:T(8,128)S(1)}, f32[2,3,32,256]{3,2,1,0:T(8,128)S(1)}, u32[]{:S(2)}, u32[]{:S(2)}) collective-permute-start(f32[2,3,32,256]{3,2,1,0:T(8,128)S(1)} %get-tuple-element.44.far_ref), channel_id=1, source_target_pairs={{0,2},{2,0},{1,3},{3,1},{4,6},{6,4},{5,7},{7,5},{8,10},{10,8},{9,1... | collective-permute-start | bytes 589832 | tf_op jit(solution)/shard_map/ppermute | solution.py:263
  43.5 8.0 %collective-permute-done.9.far_other_ref = f32[2,3,32,256]{3,2,1,0:T(8,128)S(1)} collective-permute-done((f32[2,3,32,256]{3,2,1,0:T(8,128)S(1)}, f32[2,3,32,256]{3,2,1,0:T(8,128)S(1)}, u32[]{:S(2)}, u32[]{:S(2)}) %collective-permute-start.9) | collective-permute-done | bytes 196640 | tf_op jit(solution)/shard_map/ppermute | solution.py:263
  52.2 1.4 %copy-done.2 = f32[4,2,2,32,1024]{4,3,2,1,0:T(8,128)} copy-done((f32[4,2,2,32,1024]{4,3,2,1,0:T(8,128)}, f32[4,2,2,32,1024]{4,3,2,1,0:T(8,128)S(1)}, u32[]{:S(2)}) %copy-start.2) | copy-done | bytes 2097176
  53.5 9.9 %all-to-all-done = f32[8,32,2048]{2,1,0:T(8,128)S(1)} async-done(((f32[8,32,2048]{2,1,0:T(8,128)}), f32[8,32,2048]{2,1,0:T(8,128)S(1)}, u32[]{:S(2)}, u32[]{:S(2)}) %all-to-all-start) | async-done | bytes 2097184 | tf_op jit(solution)/shard_map/all_to_all | solution.py:301
  63.4 4.3 %shard_map.51 = (f32[128,512]{1,0:T(8,128)S(1)}, f32[128,512]{1,0:T(8,128)S(1)}, bf16[256,2048]{1,0:T(8,128)(2,1)S(1)}, bf16[256,2048]{1,0:T(8,128)(2,1)S(1)}) custom-call(s32[4]{0:T(128)S(1)} %pad_add_fusion.where_ref, f32[256,2048]{1,0:T(8,128)S(1)} %bitcast.6, f32[512,1024]{1,0:T(8,128)} %get-tuple-element.66.own_ref, ...), custom_call_target="tpu_custom_call" | custom-call | flops 1000000 | bytes 6291472 | tf_op jit(solution)/shard_map/pallas_call | solution.py:39
  67.8 1.5 %collective-permute-start.11 = (f32[128,512]{1,0:T(8,128)S(1)}, f32[128,512]{1,0:T(8,128)S(1)}, u32[]{:S(2)}, u32[]{:S(2)}) collective-permute-start(f32[128,512]{1,0:T(8,128)S(1)} %get-tuple-element.53), channel_id=1, source_target_pairs={{0,2},{2,0},{1,3},{3,1},{4,6},{6,4},{5,7},{7,5},{8,10},{10,8},{9,1... | collective-permute-start | bytes 786440 | tf_op jit(solution)/shard_map/ppermute | solution.py:263
  69.3 4.1 %shard_map.54 = (f32[128,512]{1,0:T(8,128)S(1)}, f32[128,512]{1,0:T(8,128)S(1)}) custom-call(bf16[256,2048]{1,0:T(8,128)(2,1)S(1)} %get-tuple-element.54.high_ref, bf16[256,2048]{1,0:T(8,128)(2,1)S(1)} %get-tuple-element.55.low_ref, f32[512,1024]{1,0:T(8,128)} %get-tuple-element.65.own_ref, f32[512,1024]{1,0:T(8,128)} %collective-permute-done.6.other_ref), custom_call_target="tpu_custom_call" | custom-call | flops 1000000 | bytes 6291456 | tf_op jit(solution)/shard_map/pallas_call | solution.py:39
  74.0 5.8 %shard_map.52.ready_ref = f32[1024,1024]{1,0:T(8,128)S(1)} custom-call(s32[4]{0:T(128)S(1)} %pad_add_fusion.where_ref, f32[4,2,2,32,1024]{4,3,2,1,0:T(8,128)S(1)} %copy-done.3, f32[4,2,2,32,1024]{4,3,2,1,0:T(8,128)S(1)} %collective-permute-done.10.other_ref), custom_call_target="tpu_custom_call" | custom-call | flops 1000000 | bytes 4194320 | tf_op jit(solution)/shard_map/pallas_call | solution.py:39
  79.9 2.1 %shard_map.53.solved_ref = f32[128,512]{1,0:T(8,128)S(1)} custom-call(s32[4]{0:T(128)S(1)} %pad_add_fusion.where_ref, f32[1024,1024]{1,0:T(8,128)S(1)} %shard_map.52.ready_ref, f32[64,256]{1,0:T(8,128)S(1)} %get-tuple-element.50.right_own_ref, f32[64,256]{1,0:T(8,128)S(1)} %collective-permute-done.7.right_other_ref, ...), custom_call_target="tpu_custom_call" | custom-call | flops 1000000 | bytes 4849680 | tf_op jit(solution)/shard_map/pallas_call | solution.py:39
  82.2 3.4 %shard_map.55 = (f32[128,256]{1,0:T(8,128)S(1)}, f32[128,256]{1,0:T(8,128)S(1)}, f32[128,256]{1,0:T(8,128)S(1)}, f32[128,256]{1,0:T(8,128)S(1)}) custom-call(s32[4]{0:T(128)S(1)} %pad_add_fusion.where_ref, f32[1024,1024]{1,0:T(8,128)S(1)} %shard_map.52.ready_ref, f32[64,256]{1,0:T(8,128)S(1)} %get-tuple-element.50.right_own_ref, ...), custom_call_target="tpu_custom_call" | custom-call | flops 1000000 | bytes 5111824 | tf_op jit(solution)/shard_map/pallas_call | solution.py:39
  85.6 2.3 %collective-permute-start.13 = (f32[128,256]{1,0:T(8,128)S(1)}, f32[128,256]{1,0:T(8,128)S(1)}, u32[]{:S(2)}, u32[]{:S(2)}) collective-permute-start(f32[128,256]{1,0:T(8,128)S(1)} %get-tuple-element.60), channel_id=1, source_target_pairs={{0,12},{4,8},{8,4},{12,0},{1,13},{5,9},{9,5},{13,1},{2,14},{6,10},... | collective-permute-start | bytes 393224 | tf_op jit(solution)/shard_map/ppermute | solution.py:263
  87.9 2.2 %collective-permute-start.15 = (f32[128,256]{1,0:T(8,128)S(1)}, f32[128,256]{1,0:T(8,128)S(1)}, u32[]{:S(2)}, u32[]{:S(2)}) collective-permute-start(f32[128,256]{1,0:T(8,128)S(1)} %get-tuple-element.62), channel_id=1, source_target_pairs={{0,4},{4,0},{8,12},{12,8},{1,5},{5,1},{9,13},{13,9},{2,6},{6,2},{1... | collective-permute-start | bytes 393224 | tf_op jit(solution)/shard_map/ppermute | solution.py:263
  90.0 3.9 %collective-permute-done.13.refs_1_ = f32[128,256]{1,0:T(8,128)S(1)} collective-permute-done((f32[128,256]{1,0:T(8,128)S(1)}, f32[128,256]{1,0:T(8,128)S(1)}, u32[]{:S(2)}, u32[]{:S(2)}) %collective-permute-start.13) | collective-permute-done | bytes 131104 | tf_op jit(solution)/shard_map/ppermute | solution.py:263
  93.9 4.3 %collective-permute-done.14.refs_2_ = f32[128,256]{1,0:T(8,128)S(1)} collective-permute-done((f32[128,256]{1,0:T(8,128)S(1)}, f32[128,256]{1,0:T(8,128)S(1)}, u32[]{:S(2)}, u32[]{:S(2)}) %collective-permute-start.14) | collective-permute-done | bytes 131104 | tf_op jit(solution)/shard_map/ppermute | solution.py:263
  (39 shorter events, 10.6 us)
Async XLA Ops:
  0.0 1.2 %copy-start = (f32[256,1024]{1,0:T(8,128)S(1)}, f32[256,1024]{1,0:T(8,128)}, u32[]{:S(2)}) copy-start(f32[256,1024]{1,0:T(8,128)} %param.7) | copy-start | bytes 3145732
  1.2 21.8 %collective-permute-start.2 = (f32[32,1024]{1,0:T(8,128)S(1)}, f32[32,1024]{1,0:T(8,128)S(1)}, u32[]{:S(2)}, u32[]{:S(2)}) collective-permute-start(f32[32,1024]{1,0:T(8,128)S(1)} %constant_dynamic-slice_fusion.share_ref), channel_id=1, source_target_pairs={{0,12},{4,8},{8,4},{12,0},{1,13},{5,9},{9,5},{13,1},{2,14},{6,10},... | collective-permute-start | bytes 393224 | tf_op jit(solution)/shard_map/ppermute | solution.py:263
  6.4 16.7 %collective-permute-start.1 = (f32[32,1024]{1,0:T(8,128)S(1)}, f32[32,1024]{1,0:T(8,128)}, u32[]{:S(2)}, u32[]{:S(2)}) collective-permute-start(f32[32,1024]{1,0:T(8,128)S(1)} %constant_dynamic-slice_fusion.share_ref), channel_id=1, source_target_pairs={{0,8},{4,12},{8,0},{12,4},{1,9},{5,13},{9,1},{13,5},{2,10},{6,14},... | collective-permute-start | bytes 393224 | tf_op jit(solution)/shard_map/ppermute | solution.py:263
  6.4 16.7 %collective-permute-start = (f32[32,1024]{1,0:T(8,128)S(1)}, f32[32,1024]{1,0:T(8,128)}, u32[]{:S(2)}, u32[]{:S(2)}) collective-permute-start(f32[32,1024]{1,0:T(8,128)S(1)} %constant_dynamic-slice_fusion.share_ref), channel_id=1, source_target_pairs={{0,4},{4,0},{8,12},{12,8},{1,5},{5,1},{9,13},{13,9},{2,6},{6,2},{1... | collective-permute-start | bytes 393224 | tf_op jit(solution)/shard_map/ppermute | solution.py:263
  7.0 1.6 %copy-start.4 = (f32[16384,32]{0,1:T(8,128)S(1)}, f32[16384,32]{0,1:T(8,128)}, u32[]{:S(2)}) copy-start(f32[16384,32]{0,1:T(8,128)} %param.4) | copy-start | bytes 6291460
  8.7 1.4 %copy-start.1 = (f32[8,32,2048]{2,1,0:T(8,128)}, f32[8,32,2048]{2,1,0:T(8,128)S(1)}, u32[]{:S(2)}) copy-start(f32[8,32,2048]{2,1,0:T(8,128)S(1)} %shard_map.46) | copy-start | bytes 6291460
  10.1 53.3 %all-to-all-start = ((f32[8,32,2048]{2,1,0:T(8,128)}), f32[8,32,2048]{2,1,0:T(8,128)S(1)}, u32[]{:S(2)}, u32[]{:S(2)}) async-start(f32[8,32,2048]{2,1,0:T(8,128)} %copy-done.1), calls=%async_computation | async-start | bytes 4194304 | tf_op jit(solution)/shard_map/all_to_all | solution.py:301
  20.9 18.5 %collective-permute-start.6 = (f32[512,1024]{1,0:T(8,128)}, f32[512,1024]{1,0:T(8,128)}, u32[]{:S(2)}, u32[]{:S(2)}) collective-permute-start(f32[512,1024]{1,0:T(8,128)} %get-tuple-element.65.own_ref), channel_id=1, source_target_pairs={{0,1},{1,0},{2,3},{3,2},{4,5},{5,4},{6,7},{7,6},{8,9},{9,8},{10,11... | collective-permute-start | bytes 6291464 | tf_op jit(solution)/shard_map/ppermute | solution.py:263
  20.9 18.5 %collective-permute-start.5 = (f32[512,1024]{1,0:T(8,128)}, f32[512,1024]{1,0:T(8,128)}, u32[]{:S(2)}, u32[]{:S(2)}) collective-permute-start(f32[512,1024]{1,0:T(8,128)} %get-tuple-element.66.own_ref), channel_id=1, source_target_pairs={{0,1},{1,0},{2,3},{3,2},{4,5},{5,4},{6,7},{7,6},{8,9},{9,8},{10,11... | collective-permute-start | bytes 6291464 | tf_op jit(solution)/shard_map/ppermute | solution.py:263
  21.5 0.9 copy-start.5
  24.1 14.7 %collective-permute-start.3 = (f32[7,32,256]{2,1,0:T(8,128)S(1)}, f32[7,32,256]{2,1,0:T(8,128)S(1)}, u32[]{:S(2)}, u32[]{:S(2)}) collective-permute-start(f32[7,32,256]{2,1,0:T(8,128)S(1)} %get-tuple-element.39.near_ref), channel_id=1, source_target_pairs={{0,2},{2,0},{1,3},{3,1},{4,6},{6,4},{5,7},{7,5},{8,10},{10,8},{9,1... | collective-permute-start | bytes 688136 | tf_op jit(solution)/shard_map/ppermute | solution.py:263
  26.2 4.6 %collective-permute-start.4 = (f32[3,32,256]{2,1,0:T(8,128)S(1)}, f32[3,32,256]{2,1,0:T(8,128)S(1)}, u32[]{:S(2)}, u32[]{:S(2)}) collective-permute-start(f32[3,32,256]{2,1,0:T(8,128)S(1)} %get-tuple-element.40.far_ref), channel_id=1, source_target_pairs={{0,16},{16,0},{1,17},{17,1},{2,18},{18,2},{3,19},{19,3},{4,20},{20... | collective-permute-start | bytes 294920 | tf_op jit(solution)/shard_map/ppermute | solution.py:263
  27.7 11.7 %collective-permute-start.7 = (f32[64,256]{1,0:T(8,128)S(1)}, f32[64,256]{1,0:T(8,128)S(1)}, u32[]{:S(2)}, u32[]{:S(2)}) collective-permute-start(f32[64,256]{1,0:T(8,128)S(1)} %get-tuple-element.42), channel_id=1, source_target_pairs={{0,1},{1,0},{2,3},{3,2},{4,5},{5,4},{6,7},{7,6},{8,9},{9,8},{10,11... | collective-permute-start | bytes 196616 | tf_op jit(solution)/shard_map/ppermute | solution.py:263
  39.4 12.0 %collective-permute-start.8 = (f32[2,7,32,256]{3,2,1,0:T(8,128)S(1)}, f32[2,7,32,256]{3,2,1,0:T(8,128)S(1)}, u32[]{:S(2)}, u32[]{:S(2)}) collective-permute-start(f32[2,7,32,256]{3,2,1,0:T(8,128)S(1)} %get-tuple-element.43.near_ref), channel_id=1, source_target_pairs={{0,16},{16,0},{1,17},{17,1},{2,18},{18,2},{3,19},{19,3},{4,20},{20... | collective-permute-start | bytes 1376264 | tf_op jit(solution)/shard_map/ppermute | solution.py:263
  41.0 10.5 %collective-permute-start.9 = (f32[2,3,32,256]{3,2,1,0:T(8,128)S(1)}, f32[2,3,32,256]{3,2,1,0:T(8,128)S(1)}, u32[]{:S(2)}, u32[]{:S(2)}) collective-permute-start(f32[2,3,32,256]{3,2,1,0:T(8,128)S(1)} %get-tuple-element.44.far_ref), channel_id=1, source_target_pairs={{0,2},{2,0},{1,3},{3,1},{4,6},{6,4},{5,7},{7,5},{8,10},{10,8},{9,1... | collective-permute-start | bytes 589832 | tf_op jit(solution)/shard_map/ppermute | solution.py:263
  52.2 1.4 %copy-start.2 = (f32[4,2,2,32,1024]{4,3,2,1,0:T(8,128)}, f32[4,2,2,32,1024]{4,3,2,1,0:T(8,128)S(1)}, u32[]{:S(2)}) copy-start(f32[4,2,2,32,1024]{4,3,2,1,0:T(8,128)S(1)} %shard_map.50.own_ref) | copy-start | bytes 6291460
  63.4 4.3 %copy-start.3 = (f32[4,2,2,32,1024]{4,3,2,1,0:T(8,128)S(1)}, f32[4,2,2,32,1024]{4,3,2,1,0:T(8,128)}, u32[]{:S(2)}) copy-start(f32[4,2,2,32,1024]{4,3,2,1,0:T(8,128)} %copy-done.2) | copy-start | bytes 6291460
  67.7 6.3 %collective-permute-start.10 = (f32[4,2,2,32,1024]{4,3,2,1,0:T(8,128)S(1)}, f32[4,2,2,32,1024]{4,3,2,1,0:T(8,128)S(1)}, u32[]{:S(2)}, u32[]{:S(2)}) collective-permute-start(f32[4,2,2,32,1024]{4,3,2,1,0:T(8,128)S(1)} %copy-done.3), channel_id=1, source_target_pairs={{0,1},{1,0},{2,3},{3,2},{4,5},{5,4},{6,7},{7,6},{8,9},{9,8},{10,11... | collective-permute-start | bytes 6291464 | tf_op jit(solution)/shard_map/ppermute | solution.py:263
  67.8 12.0 %collective-permute-start.11 = (f32[128,512]{1,0:T(8,128)S(1)}, f32[128,512]{1,0:T(8,128)S(1)}, u32[]{:S(2)}, u32[]{:S(2)}) collective-permute-start(f32[128,512]{1,0:T(8,128)S(1)} %get-tuple-element.53), channel_id=1, source_target_pairs={{0,2},{2,0},{1,3},{3,1},{4,6},{6,4},{5,7},{7,5},{8,10},{10,8},{9,1... | collective-permute-start | bytes 786440 | tf_op jit(solution)/shard_map/ppermute | solution.py:263
  73.4 8.7 %collective-permute-start.12 = (f32[128,512]{1,0:T(8,128)S(1)}, f32[128,512]{1,0:T(8,128)S(1)}, u32[]{:S(2)}, u32[]{:S(2)}) collective-permute-start(f32[128,512]{1,0:T(8,128)S(1)} %get-tuple-element.58), channel_id=1, source_target_pairs={{0,2},{2,0},{1,3},{3,1},{4,6},{6,4},{5,7},{7,5},{8,10},{10,8},{9,1... | collective-permute-start | bytes 786440 | tf_op jit(solution)/shard_map/ppermute | solution.py:263
  85.6 8.4 %collective-permute-start.13 = (f32[128,256]{1,0:T(8,128)S(1)}, f32[128,256]{1,0:T(8,128)S(1)}, u32[]{:S(2)}, u32[]{:S(2)}) collective-permute-start(f32[128,256]{1,0:T(8,128)S(1)} %get-tuple-element.60), channel_id=1, source_target_pairs={{0,12},{4,8},{8,4},{12,0},{1,13},{5,9},{9,5},{13,1},{2,14},{6,10},... | collective-permute-start | bytes 393224 | tf_op jit(solution)/shard_map/ppermute | solution.py:263
  87.9 10.3 %collective-permute-start.14 = (f32[128,256]{1,0:T(8,128)S(1)}, f32[128,256]{1,0:T(8,128)S(1)}, u32[]{:S(2)}, u32[]{:S(2)}) collective-permute-start(f32[128,256]{1,0:T(8,128)S(1)} %get-tuple-element.61), channel_id=1, source_target_pairs={{0,8},{4,12},{8,0},{12,4},{1,9},{5,13},{9,1},{13,5},{2,10},{6,14},... | collective-permute-start | bytes 393224 | tf_op jit(solution)/shard_map/ppermute | solution.py:263
  87.9 10.3 %collective-permute-start.15 = (f32[128,256]{1,0:T(8,128)S(1)}, f32[128,256]{1,0:T(8,128)S(1)}, u32[]{:S(2)}, u32[]{:S(2)}) collective-permute-start(f32[128,256]{1,0:T(8,128)S(1)} %get-tuple-element.62), channel_id=1, source_target_pairs={{0,4},{4,0},{8,12},{12,8},{1,5},{5,1},{9,13},{13,9},{2,6},{6,2},{1... | collective-permute-start | bytes 393224 | tf_op jit(solution)/shard_map/ppermute | solution.py:263
  98.8 1.3 %collective-permute-start.16 = (f32[64,256]{1,0:T(8,128)S(1)}, f32[64,256]{1,0:T(8,128)S(1)}, u32[]{:S(2)}, u32[]{:S(2)}) collective-permute-start(f32[64,256]{1,0:T(8,128)S(1)} %get-tuple-element.64), channel_id=1, source_target_pairs={{0,1},{1,0},{2,3},{3,2},{4,5},{5,4},{6,7},{7,6},{8,9},{9,8},{10,11... | collective-permute-start | bytes 196616 | tf_op jit(solution)/shard_map/ppermute | solution.py:263

commit v7 on v6

--- a/solution.py
+++ b/solution.py
@@ -13,6 +13,7 @@
 SIZE = 128
 VMEM = pl.BlockSpec(memory_space=pltpu.VMEM)
 SMEM = pl.BlockSpec(memory_space=pltpu.SMEM)
+TILE = 256
 QUERY_CUTS = (32,)
 
 
@@ -173,12 +174,30 @@
 
 
 def couple_kernel(where_ref, queries_ref, own_ref, other_ref, kept_ref, far_ref, high_ref, low_ref):
-    split_kernel(where_ref, queries_ref, high_ref, low_ref)
+    @pl.when(pl.program_id(0) == 0)
+    def _():
+        split_kernel(where_ref, queries_ref, high_ref, low_ref)
+
     multiply(high_ref, low_ref, (own_ref, other_ref), kept_ref, far_ref)
 
 
 def couple_more_kernel(high_ref, low_ref, own_ref, other_ref, kept_ref, far_ref):
     multiply(high_ref, low_ref, (own_ref, other_ref), kept_ref, far_ref)
+
+
+def by_tiles(kernel, queries, panels, count, scalars=(), split=()):
+    window, columns = panels[0].shape
+    panel = pl.BlockSpec((TILE, columns), lambda i: (i, 0))
+    out = pl.BlockSpec((count, TILE), lambda i: (0, i))
+    return pl.pallas_call(
+        kernel,
+        grid=(window // TILE,),
+        out_shape=[shape(count, window)] * 2 + list(split),
+        in_specs=[SMEM] * len(scalars) + [VMEM] * len(queries) + [panel] * 2,
+        out_specs=[out] * 2 + [pl.BlockSpec(s.shape, lambda i: (0, 0)) for s in split],
+        cost_estimate=pl.CostEstimate(flops=10**6, bytes_accessed=10**7, transcendentals=0),
+        compiler_params=pltpu.CompilerParams(vmem_limit_bytes=20 * 2**20),
+    )(*scalars, *queries, *panels)
 
 
 def deal_kernel(queries_ref, *out_refs):
@@ -303,17 +322,20 @@
         half = 4 * cut
         if not offset:
             queries, shares = lax.optimization_barrier((queries, shares))
-        kept, far, high, low = call(
+        kept, far, high, low = by_tiles(
             couple_kernel,
-            [shape(half, half_window)] * 2 + [shape(*queries.shape, dtype=jnp.bfloat16)] * 2,
-            scalars=1,
-        )(where, queries, panels[0], others[0])
+            (queries,),
+            (panels[0], others[0]),
+            half,
+            scalars=(where,),
+            split=[shape(*queries.shape, dtype=jnp.bfloat16)] * 2,
+        )
         if not offset:
             far, shares = lax.optimization_barrier((far, shares))
             ready = call(
                 prepare_kernel, shape(window, window), [pltpu.VMEM((window, window), jnp.float32)], scalars=1
             )(where, shares, swap(shares, "core", 1))
-        kept_more, far_more = call(couple_more_kernel, [shape(half, half_window)] * 2)(high, low, panels[1], others[1])
+        kept_more, far_more = by_tiles(couple_more_kernel, (high, low), (panels[1], others[1]), half)
         rights = (right_own, right_other)
         solved = call(solve_first_kernel, shape(half, half_window), scalars=1)(
             where, ready, *rights, kept, swap(far, "side", 1)

time: 102 us -> 102 us (level)
    pallas_call x12 -> x10, Pallas kernels: 24.6 us -> 16.3 us  [run(): pl.pallas_call(kernel, out_shape=outs, in_specs=[SMEM] * scalars + [VMEM]...]
    pallas_call x0 -> x2, Pallas kernels: none -> 7.82 us  [by_tiles(): pl.pallas_call(kernel, grid=(window // TILE,), out_shape=[shape(count, wi...]
  transfers between devices with their start and end apart: 18 -> 18, of which waited for: 8 -> 8; matrix products, arithmetic and copies ran while one was open for 5% -> 5% of each run, Pallas kernels for 15% -> 14%
where the time goes in v7:
time: 102 us; the launch traced here: 101 us
  waiting for transfers between devices  38.9 us (38%)
  starting transfers between devices  26.7 us (26%)
  Pallas kernels  24.1 us (24%)
  local copies, waits for them, and re-layouts  11.3 us (11%)
    ppermute x17, waiting for transfers between devices, swap(): lax.ppermute(value, axis, [(i, i ^ step) for i in range(lax.axis_size(axi...  29 us
    ppermute x17, starting transfers between devices, swap(): lax.ppermute(value, axis, [(i, i ^ step) for i in range(lax.axis_size(axi...  20.7 us
    pallas_call x10, Pallas kernels, run(): pl.pallas_call(kernel, out_shape=outs, in_specs=[SMEM] * scalars + [VMEM]...  16.3 us
    all_to_all x1, waiting for transfers between devices, shards(): lax.all_to_all(dealt[number], ('row', 'side'), split_axis=0, concat_axis=...  9.92 us
    pallas_call x2, Pallas kernels, by_tiles(): pl.pallas_call(kernel, grid=(window // TILE,), out_shape=[shape(count, wi...  7.82 us
    unnamed x12, local copies, waits for them, and re-layouts  6.44 us
    all_to_all x1, starting transfers between devices, shards(): lax.all_to_all(dealt[number], ('row', 'side'), split_axis=0, concat_axis=...  5.95 us
    slice x1, local copies, waits for them, and re-layouts, shards(): panels = [factor_panel[:half_window], factor_panel[half_window:]]  4.82 us
  transfers between devices with their start and end apart: 18, of which 8 were waited for; matrix products, arithmetic and copies ran while one was open for 5% of the time, Pallas kernels for 14%

profile of v7, /device:TPU:0, one launch (start us, length us, event | category | flops | bytes accessed | tf_op | source)
XLA Modules:
  0.0 101.2 jit_solution(17222341396502465038)
XLA Ops:
  1.2 5.1 %collective-permute-start.2 = (f32[32,1024]{1,0:T(8,128)S(1)}, f32[32,1024]{1,0:T(8,128)S(1)}, u32[]{:S(2)}, u32[]{:S(2)}) collective-permute-start(f32[32,1024]{1,0:T(8,128)S(1)} %constant_dynamic-slice_fusion.share_ref), channel_id=1, source_target_pairs={{0,12},{4,8},{8,4},{12,0},{1,13},{5,9},{9,5},{13,1},{2,14},{6,10},... | collective-permute-start | bytes 393224 | tf_op jit(solution)/shard_map/ppermute | solution.py:282
  7.0 1.6 %copy-done.4 = f32[16384,32]{0,1:T(8,128)S(1)} copy-done((f32[16384,32]{0,1:T(8,128)S(1)}, f32[16384,32]{0,1:T(8,128)}, u32[]{:S(2)}) %copy-start.4) | copy-done | bytes 2097176
  8.7 1.4 %copy-done.1 = f32[8,32,2048]{2,1,0:T(8,128)} copy-done((f32[8,32,2048]{2,1,0:T(8,128)}, f32[8,32,2048]{2,1,0:T(8,128)S(1)}, u32[]{:S(2)}) %copy-start.1) | copy-done | bytes 2097176
  10.1 5.9 %all-to-all-start = ((f32[8,32,2048]{2,1,0:T(8,128)}), f32[8,32,2048]{2,1,0:T(8,128)S(1)}, u32[]{:S(2)}, u32[]{:S(2)}) async-start(f32[8,32,2048]{2,1,0:T(8,128)} %copy-done.1), calls=%async_computation | async-start | bytes 4194304 | tf_op jit(solution)/shard_map/all_to_all | solution.py:320
  16.0 4.8 %fusion = (f32[512,1024]{1,0:T(8,128)}, f32[512,1024]{1,0:T(8,128)}) fusion(f32[1024,1024]{1,0:T(8,128)} %param.5), kind=kLoop, calls=%fused_computation.2 | loop fusion | bytes 8388608 | tf_op jit(solution)/shard_map/slice | solution.py:302
  24.1 2.1 %collective-permute-start.3 = (f32[7,32,256]{2,1,0:T(8,128)S(1)}, f32[7,32,256]{2,1,0:T(8,128)S(1)}, u32[]{:S(2)}, u32[]{:S(2)}) collective-permute-start(f32[7,32,256]{2,1,0:T(8,128)S(1)} %get-tuple-element.39.near_ref), channel_id=1, source_target_pairs={{0,2},{2,0},{1,3},{3,1},{4,6},{6,4},{5,7},{7,5},{8,10},{10,8},{9,1... | collective-permute-start | bytes 688136 | tf_op jit(solution)/shard_map/ppermute | solution.py:282
  26.2 1.5 %collective-permute-start.4 = (f32[3,32,256]{2,1,0:T(8,128)S(1)}, f32[3,32,256]{2,1,0:T(8,128)S(1)}, u32[]{:S(2)}, u32[]{:S(2)}) collective-permute-start(f32[3,32,256]{2,1,0:T(8,128)S(1)} %get-tuple-element.40.far_ref), channel_id=1, source_target_pairs={{0,16},{16,0},{1,17},{17,1},{2,18},{18,2},{3,19},{19,3},{4,20},{20... | collective-permute-start | bytes 294920 | tf_op jit(solution)/shard_map/ppermute | solution.py:282
  27.7 3.1 %collective-permute-done.4.far_other_ref = f32[3,32,256]{2,1,0:T(8,128)S(1)} collective-permute-done((f32[3,32,256]{2,1,0:T(8,128)S(1)}, f32[3,32,256]{2,1,0:T(8,128)S(1)}, u32[]{:S(2)}, u32[]{:S(2)}) %collective-permute-start.4) | collective-permute-done | bytes 98336 | tf_op jit(solution)/shard_map/ppermute | solution.py:282
  30.8 8.0 %collective-permute-done.3.near_other_ref = f32[7,32,256]{2,1,0:T(8,128)S(1)} collective-permute-done((f32[7,32,256]{2,1,0:T(8,128)S(1)}, f32[7,32,256]{2,1,0:T(8,128)S(1)}, u32[]{:S(2)}, u32[]{:S(2)}) %collective-permute-start.3) | collective-permute-done | bytes 229408 | tf_op jit(solution)/shard_map/ppermute | solution.py:282
  39.4 1.6 %collective-permute-start.8 = (f32[2,7,32,256]{3,2,1,0:T(8,128)S(1)}, f32[2,7,32,256]{3,2,1,0:T(8,128)S(1)}, u32[]{:S(2)}, u32[]{:S(2)}) collective-permute-start(f32[2,7,32,256]{3,2,1,0:T(8,128)S(1)} %get-tuple-element.43.near_ref), channel_id=1, source_target_pairs={{0,16},{16,0},{1,17},{17,1},{2,18},{18,2},{3,19},{19,3},{4,20},{20... | collective-permute-start | bytes 1376264 | tf_op jit(solution)/shard_map/ppermute | solution.py:282
  41.0 2.5 %collective-permute-start.9 = (f32[2,3,32,256]{3,2,1,0:T(8,128)S(1)}, f32[2,3,32,256]{3,2,1,0:T(8,128)S(1)}, u32[]{:S(2)}, u32[]{:S(2)}) collective-permute-start(f32[2,3,32,256]{3,2,1,0:T(8,128)S(1)} %get-tuple-element.44.far_ref), channel_id=1, source_target_pairs={{0,2},{2,0},{1,3},{3,1},{4,6},{6,4},{5,7},{7,5},{8,10},{10,8},{9,1... | collective-permute-start | bytes 589832 | tf_op jit(solution)/shard_map/ppermute | solution.py:282
  43.5 8.0 %collective-permute-done.9.far_other_ref = f32[2,3,32,256]{3,2,1,0:T(8,128)S(1)} collective-permute-done((f32[2,3,32,256]{3,2,1,0:T(8,128)S(1)}, f32[2,3,32,256]{3,2,1,0:T(8,128)S(1)}, u32[]{:S(2)}, u32[]{:S(2)}) %collective-permute-start.9) | collective-permute-done | bytes 196640 | tf_op jit(solution)/shard_map/ppermute | solution.py:282
  52.2 1.4 %copy-done.2 = f32[4,2,2,32,1024]{4,3,2,1,0:T(8,128)} copy-done((f32[4,2,2,32,1024]{4,3,2,1,0:T(8,128)}, f32[4,2,2,32,1024]{4,3,2,1,0:T(8,128)S(1)}, u32[]{:S(2)}) %copy-start.2) | copy-done | bytes 2097176
  53.5 9.9 %all-to-all-done = f32[8,32,2048]{2,1,0:T(8,128)S(1)} async-done(((f32[8,32,2048]{2,1,0:T(8,128)}), f32[8,32,2048]{2,1,0:T(8,128)S(1)}, u32[]{:S(2)}, u32[]{:S(2)}) %all-to-all-start) | async-done | bytes 2097184 | tf_op jit(solution)/shard_map/all_to_all | solution.py:320
  63.4 4.2 %shard_map.51 = (f32[128,512]{1,0:T(8,128)S(1)}, f32[128,512]{1,0:T(8,128)S(1)}, bf16[256,2048]{1,0:T(8,128)(2,1)S(1)}, bf16[256,2048]{1,0:T(8,128)(2,1)S(1)}) custom-call(s32[4]{0:T(128)S(1)} %pad_add_fusion.where_ref, f32[256,2048]{1,0:T(8,128)S(1)} %bitcast.6, f32[512,1024]{1,0:T(8,128)} %get-tuple-element.66.own_ref, ...), custom_call_target="tpu_custom_call" | custom-call | flops 1000000 | bytes 10000000 | tf_op jit(solution)/shard_map/pallas_call | solution.py:192
  67.7 1.5 %collective-permute-start.11 = (f32[128,512]{1,0:T(8,128)S(1)}, f32[128,512]{1,0:T(8,128)S(1)}, u32[]{:S(2)}, u32[]{:S(2)}) collective-permute-start(f32[128,512]{1,0:T(8,128)S(1)} %get-tuple-element.53), channel_id=1, source_target_pairs={{0,2},{2,0},{1,3},{3,1},{4,6},{6,4},{5,7},{7,5},{8,10},{10,8},{9,1... | collective-permute-start | bytes 786440 | tf_op jit(solution)/shard_map/ppermute | solution.py:282
  69.3 3.6 %shard_map.54 = (f32[128,512]{1,0:T(8,128)S(1)}, f32[128,512]{1,0:T(8,128)S(1)}) custom-call(bf16[256,2048]{1,0:T(8,128)(2,1)S(1)} %get-tuple-element.54.high_ref, bf16[256,2048]{1,0:T(8,128)(2,1)S(1)} %get-tuple-element.55.low_ref, f32[512,1024]{1,0:T(8,128)} %get-tuple-element.65.own_ref, f32[512,1024]{1,0:T(8,128)} %collective-permute-done.6.other_ref), custom_call_target="tpu_custom_call" | custom-call | flops 1000000 | bytes 10000000 | tf_op jit(solution)/shard_map/pallas_call | solution.py:192
  73.5 5.8 %shard_map.52.ready_ref = f32[1024,1024]{1,0:T(8,128)S(1)} custom-call(s32[4]{0:T(128)S(1)} %pad_add_fusion.where_ref, f32[4,2,2,32,1024]{4,3,2,1,0:T(8,128)S(1)} %copy-done.3, f32[4,2,2,32,1024]{4,3,2,1,0:T(8,128)S(1)} %collective-permute-done.10.other_ref), custom_call_target="tpu_custom_call" | custom-call | flops 1000000 | bytes 4194320 | tf_op jit(solution)/shard_map/pallas_call | solution.py:40
  79.3 2.1 %shard_map.53.solved_ref = f32[128,512]{1,0:T(8,128)S(1)} custom-call(s32[4]{0:T(128)S(1)} %pad_add_fusion.where_ref, f32[1024,1024]{1,0:T(8,128)S(1)} %shard_map.52.ready_ref, f32[64,256]{1,0:T(8,128)S(1)} %get-tuple-element.50.right_own_ref, f32[64,256]{1,0:T(8,128)S(1)} %collective-permute-done.7.right_other_ref, ...), custom_call_target="tpu_custom_call" | custom-call | flops 1000000 | bytes 4849680 | tf_op jit(solution)/shard_map/pallas_call | solution.py:40
  82.1 3.4 %shard_map.55 = (f32[128,256]{1,0:T(8,128)S(1)}, f32[128,256]{1,0:T(8,128)S(1)}, f32[128,256]{1,0:T(8,128)S(1)}, f32[128,256]{1,0:T(8,128)S(1)}) custom-call(s32[4]{0:T(128)S(1)} %pad_add_fusion.where_ref, f32[1024,1024]{1,0:T(8,128)S(1)} %shard_map.52.ready_ref, f32[64,256]{1,0:T(8,128)S(1)} %get-tuple-element.50.right_own_ref, ...), custom_call_target="tpu_custom_call" | custom-call | flops 1000000 | bytes 5111824 | tf_op jit(solution)/shard_map/pallas_call | solution.py:40
  85.5 2.3 %collective-permute-start.13 = (f32[128,256]{1,0:T(8,128)S(1)}, f32[128,256]{1,0:T(8,128)S(1)}, u32[]{:S(2)}, u32[]{:S(2)}) collective-permute-start(f32[128,256]{1,0:T(8,128)S(1)} %get-tuple-element.60), channel_id=1, source_target_pairs={{0,12},{4,8},{8,4},{12,0},{1,13},{5,9},{9,5},{13,1},{2,14},{6,10},... | collective-permute-start | bytes 393224 | tf_op jit(solution)/shard_map/ppermute | solution.py:282
  87.8 2.1 %collective-permute-start.15 = (f32[128,256]{1,0:T(8,128)S(1)}, f32[128,256]{1,0:T(8,128)S(1)}, u32[]{:S(2)}, u32[]{:S(2)}) collective-permute-start(f32[128,256]{1,0:T(8,128)S(1)} %get-tuple-element.62), channel_id=1, source_target_pairs={{0,4},{4,0},{8,12},{12,8},{1,5},{5,1},{9,13},{13,9},{2,6},{6,2},{1... | collective-permute-start | bytes 393224 | tf_op jit(solution)/shard_map/ppermute | solution.py:282
  89.9 3.9 %collective-permute-done.13.refs_1_ = f32[128,256]{1,0:T(8,128)S(1)} collective-permute-done((f32[128,256]{1,0:T(8,128)S(1)}, f32[128,256]{1,0:T(8,128)S(1)}, u32[]{:S(2)}, u32[]{:S(2)}) %collective-permute-start.13) | collective-permute-done | bytes 131104 | tf_op jit(solution)/shard_map/ppermute | solution.py:282
  93.8 4.2 %collective-permute-done.14.refs_2_ = f32[128,256]{1,0:T(8,128)S(1)} collective-permute-done((f32[128,256]{1,0:T(8,128)S(1)}, f32[128,256]{1,0:T(8,128)S(1)}, u32[]{:S(2)}, u32[]{:S(2)}) %collective-permute-start.14) | collective-permute-done | bytes 131104 | tf_op jit(solution)/shard_map/ppermute | solution.py:282
  (39 shorter events, 11.0 us)
Async XLA Ops:
  0.0 1.2 %copy-start = (f32[256,1024]{1,0:T(8,128)S(1)}, f32[256,1024]{1,0:T(8,128)}, u32[]{:S(2)}) copy-start(f32[256,1024]{1,0:T(8,128)} %param.7) | copy-start | bytes 3145732
  1.2 21.8 %collective-permute-start.2 = (f32[32,1024]{1,0:T(8,128)S(1)}, f32[32,1024]{1,0:T(8,128)S(1)}, u32[]{:S(2)}, u32[]{:S(2)}) collective-permute-start(f32[32,1024]{1,0:T(8,128)S(1)} %constant_dynamic-slice_fusion.share_ref), channel_id=1, source_target_pairs={{0,12},{4,8},{8,4},{12,0},{1,13},{5,9},{9,5},{13,1},{2,14},{6,10},... | collective-permute-start | bytes 393224 | tf_op jit(solution)/shard_map/ppermute | solution.py:282
  6.4 16.7 %collective-permute-start.1 = (f32[32,1024]{1,0:T(8,128)S(1)}, f32[32,1024]{1,0:T(8,128)}, u32[]{:S(2)}, u32[]{:S(2)}) collective-permute-start(f32[32,1024]{1,0:T(8,128)S(1)} %constant_dynamic-slice_fusion.share_ref), channel_id=1, source_target_pairs={{0,8},{4,12},{8,0},{12,4},{1,9},{5,13},{9,1},{13,5},{2,10},{6,14},... | collective-permute-start | bytes 393224 | tf_op jit(solution)/shard_map/ppermute | solution.py:282
  6.4 16.7 %collective-permute-start = (f32[32,1024]{1,0:T(8,128)S(1)}, f32[32,1024]{1,0:T(8,128)}, u32[]{:S(2)}, u32[]{:S(2)}) collective-permute-start(f32[32,1024]{1,0:T(8,128)S(1)} %constant_dynamic-slice_fusion.share_ref), channel_id=1, source_target_pairs={{0,4},{4,0},{8,12},{12,8},{1,5},{5,1},{9,13},{13,9},{2,6},{6,2},{1... | collective-permute-start | bytes 393224 | tf_op jit(solution)/shard_map/ppermute | solution.py:282
  7.0 1.6 %copy-start.4 = (f32[16384,32]{0,1:T(8,128)S(1)}, f32[16384,32]{0,1:T(8,128)}, u32[]{:S(2)}) copy-start(f32[16384,32]{0,1:T(8,128)} %param.4) | copy-start | bytes 6291460
  8.7 1.4 %copy-start.1 = (f32[8,32,2048]{2,1,0:T(8,128)}, f32[8,32,2048]{2,1,0:T(8,128)S(1)}, u32[]{:S(2)}) copy-start(f32[8,32,2048]{2,1,0:T(8,128)S(1)} %shard_map.46) | copy-start | bytes 6291460
  10.1 53.3 %all-to-all-start = ((f32[8,32,2048]{2,1,0:T(8,128)}), f32[8,32,2048]{2,1,0:T(8,128)S(1)}, u32[]{:S(2)}, u32[]{:S(2)}) async-start(f32[8,32,2048]{2,1,0:T(8,128)} %copy-done.1), calls=%async_computation | async-start | bytes 4194304 | tf_op jit(solution)/shard_map/all_to_all | solution.py:320
  20.9 18.5 %collective-permute-start.6 = (f32[512,1024]{1,0:T(8,128)}, f32[512,1024]{1,0:T(8,128)}, u32[]{:S(2)}, u32[]{:S(2)}) collective-permute-start(f32[512,1024]{1,0:T(8,128)} %get-tuple-element.65.own_ref), channel_id=1, source_target_pairs={{0,1},{1,0},{2,3},{3,2},{4,5},{5,4},{6,7},{7,6},{8,9},{9,8},{10,11... | collective-permute-start | bytes 6291464 | tf_op jit(solution)/shard_map/ppermute | solution.py:282
  20.9 18.5 %collective-permute-start.5 = (f32[512,1024]{1,0:T(8,128)}, f32[512,1024]{1,0:T(8,128)}, u32[]{:S(2)}, u32[]{:S(2)}) collective-permute-start(f32[512,1024]{1,0:T(8,128)} %get-tuple-element.66.own_ref), channel_id=1, source_target_pairs={{0,1},{1,0},{2,3},{3,2},{4,5},{5,4},{6,7},{7,6},{8,9},{9,8},{10,11... | collective-permute-start | bytes 6291464 | tf_op jit(solution)/shard_map/ppermute | solution.py:282
  21.5 0.9 copy-start.5
  24.1 14.7 %collective-permute-start.3 = (f32[7,32,256]{2,1,0:T(8,128)S(1)}, f32[7,32,256]{2,1,0:T(8,128)S(1)}, u32[]{:S(2)}, u32[]{:S(2)}) collective-permute-start(f32[7,32,256]{2,1,0:T(8,128)S(1)} %get-tuple-element.39.near_ref), channel_id=1, source_target_pairs={{0,2},{2,0},{1,3},{3,1},{4,6},{6,4},{5,7},{7,5},{8,10},{10,8},{9,1... | collective-permute-start | bytes 688136 | tf_op jit(solution)/shard_map/ppermute | solution.py:282
  26.2 4.6 %collective-permute-start.4 = (f32[3,32,256]{2,1,0:T(8,128)S(1)}, f32[3,32,256]{2,1,0:T(8,128)S(1)}, u32[]{:S(2)}, u32[]{:S(2)}) collective-permute-start(f32[3,32,256]{2,1,0:T(8,128)S(1)} %get-tuple-element.40.far_ref), channel_id=1, source_target_pairs={{0,16},{16,0},{1,17},{17,1},{2,18},{18,2},{3,19},{19,3},{4,20},{20... | collective-permute-start | bytes 294920 | tf_op jit(solution)/shard_map/ppermute | solution.py:282
  27.7 11.7 %collective-permute-start.7 = (f32[64,256]{1,0:T(8,128)S(1)}, f32[64,256]{1,0:T(8,128)S(1)}, u32[]{:S(2)}, u32[]{:S(2)}) collective-permute-start(f32[64,256]{1,0:T(8,128)S(1)} %get-tuple-element.42), channel_id=1, source_target_pairs={{0,1},{1,0},{2,3},{3,2},{4,5},{5,4},{6,7},{7,6},{8,9},{9,8},{10,11... | collective-permute-start | bytes 196616 | tf_op jit(solution)/shard_map/ppermute | solution.py:282
  39.4 12.0 %collective-permute-start.8 = (f32[2,7,32,256]{3,2,1,0:T(8,128)S(1)}, f32[2,7,32,256]{3,2,1,0:T(8,128)S(1)}, u32[]{:S(2)}, u32[]{:S(2)}) collective-permute-start(f32[2,7,32,256]{3,2,1,0:T(8,128)S(1)} %get-tuple-element.43.near_ref), channel_id=1, source_target_pairs={{0,16},{16,0},{1,17},{17,1},{2,18},{18,2},{3,19},{19,3},{4,20},{20... | collective-permute-start | bytes 1376264 | tf_op jit(solution)/shard_map/ppermute | solution.py:282
  41.0 10.5 %collective-permute-start.9 = (f32[2,3,32,256]{3,2,1,0:T(8,128)S(1)}, f32[2,3,32,256]{3,2,1,0:T(8,128)S(1)}, u32[]{:S(2)}, u32[]{:S(2)}) collective-permute-start(f32[2,3,32,256]{3,2,1,0:T(8,128)S(1)} %get-tuple-element.44.far_ref), channel_id=1, source_target_pairs={{0,2},{2,0},{1,3},{3,1},{4,6},{6,4},{5,7},{7,5},{8,10},{10,8},{9,1... | collective-permute-start | bytes 589832 | tf_op jit(solution)/shard_map/ppermute | solution.py:282
  52.2 1.4 %copy-start.2 = (f32[4,2,2,32,1024]{4,3,2,1,0:T(8,128)}, f32[4,2,2,32,1024]{4,3,2,1,0:T(8,128)S(1)}, u32[]{:S(2)}) copy-start(f32[4,2,2,32,1024]{4,3,2,1,0:T(8,128)S(1)} %shard_map.50.own_ref) | copy-start | bytes 6291460
  63.4 4.2 %copy-start.3 = (f32[4,2,2,32,1024]{4,3,2,1,0:T(8,128)S(1)}, f32[4,2,2,32,1024]{4,3,2,1,0:T(8,128)}, u32[]{:S(2)}) copy-start(f32[4,2,2,32,1024]{4,3,2,1,0:T(8,128)} %copy-done.2) | copy-start | bytes 6291460
  67.7 5.9 %collective-permute-start.10 = (f32[4,2,2,32,1024]{4,3,2,1,0:T(8,128)S(1)}, f32[4,2,2,32,1024]{4,3,2,1,0:T(8,128)S(1)}, u32[]{:S(2)}, u32[]{:S(2)}) collective-permute-start(f32[4,2,2,32,1024]{4,3,2,1,0:T(8,128)S(1)} %copy-done.3), channel_id=1, source_target_pairs={{0,1},{1,0},{2,3},{3,2},{4,5},{5,4},{6,7},{7,6},{8,9},{9,8},{10,11... | collective-permute-start | bytes 6291464 | tf_op jit(solution)/shard_map/ppermute | solution.py:282
  67.7 11.6 %collective-permute-start.11 = (f32[128,512]{1,0:T(8,128)S(1)}, f32[128,512]{1,0:T(8,128)S(1)}, u32[]{:S(2)}, u32[]{:S(2)}) collective-permute-start(f32[128,512]{1,0:T(8,128)S(1)} %get-tuple-element.53), channel_id=1, source_target_pairs={{0,2},{2,0},{1,3},{3,1},{4,6},{6,4},{5,7},{7,5},{8,10},{10,8},{9,1... | collective-permute-start | bytes 786440 | tf_op jit(solution)/shard_map/ppermute | solution.py:282
  72.9 9.2 %collective-permute-start.12 = (f32[128,512]{1,0:T(8,128)S(1)}, f32[128,512]{1,0:T(8,128)S(1)}, u32[]{:S(2)}, u32[]{:S(2)}) collective-permute-start(f32[128,512]{1,0:T(8,128)S(1)} %get-tuple-element.58), channel_id=1, source_target_pairs={{0,2},{2,0},{1,3},{3,1},{4,6},{6,4},{5,7},{7,5},{8,10},{10,8},{9,1... | collective-permute-start | bytes 786440 | tf_op jit(solution)/shard_map/ppermute | solution.py:282
  85.5 8.4 %collective-permute-start.13 = (f32[128,256]{1,0:T(8,128)S(1)}, f32[128,256]{1,0:T(8,128)S(1)}, u32[]{:S(2)}, u32[]{:S(2)}) collective-permute-start(f32[128,256]{1,0:T(8,128)S(1)} %get-tuple-element.60), channel_id=1, source_target_pairs={{0,12},{4,8},{8,4},{12,0},{1,13},{5,9},{9,5},{13,1},{2,14},{6,10},... | collective-permute-start | bytes 393224 | tf_op jit(solution)/shard_map/ppermute | solution.py:282
  87.8 10.2 %collective-permute-start.14 = (f32[128,256]{1,0:T(8,128)S(1)}, f32[128,256]{1,0:T(8,128)S(1)}, u32[]{:S(2)}, u32[]{:S(2)}) collective-permute-start(f32[128,256]{1,0:T(8,128)S(1)} %get-tuple-element.61), channel_id=1, source_target_pairs={{0,8},{4,12},{8,0},{12,4},{1,9},{5,13},{9,1},{13,5},{2,10},{6,14},... | collective-permute-start | bytes 393224 | tf_op jit(solution)/shard_map/ppermute | solution.py:282
  87.8 10.2 %collective-permute-start.15 = (f32[128,256]{1,0:T(8,128)S(1)}, f32[128,256]{1,0:T(8,128)S(1)}, u32[]{:S(2)}, u32[]{:S(2)}) collective-permute-start(f32[128,256]{1,0:T(8,128)S(1)} %get-tuple-element.62), channel_id=1, source_target_pairs={{0,4},{4,0},{8,12},{12,8},{1,5},{5,1},{9,13},{13,9},{2,6},{6,2},{1... | collective-permute-start | bytes 393224 | tf_op jit(solution)/shard_map/ppermute | solution.py:282
  98.6 1.3 %collective-permute-start.16 = (f32[64,256]{1,0:T(8,128)S(1)}, f32[64,256]{1,0:T(8,128)S(1)}, u32[]{:S(2)}, u32[]{:S(2)}) collective-permute-start(f32[64,256]{1,0:T(8,128)S(1)} %get-tuple-element.64), channel_id=1, source_target_pairs={{0,1},{1,0},{2,3},{3,2},{4,5},{5,4},{6,7},{7,6},{8,9},{9,8},{10,11... | collective-permute-start | bytes 196616 | tf_op jit(solution)/shard_map/ppermute | solution.py:282
